TPU v7x, 32 devices: a whole 2x2x4 slice. The times are simulated.
32 devices in a mesh: ep: 16 (over z, y, x), tp: 2 (over core).
Axes of the slice: x: 2, y: 2, z: 4, core: 2. Of those that a mesh axis runs over, the one named last changes fastest.
Arguments:
- stream: bfloat16 [8192, 1536], P('ep'), may hold values from -6 to 6
- cotangent: bfloat16 [8192, 1536], P('ep'), may hold values from -6 to 6
- attention_gain: bfloat16 [1536], replicated, may hold values from 0.5 to 1.5
- query_weight: bfloat16 [1536, 1536], P(None, 'tp'), may hold values from -0.625 to 0.625
- key_matrix: bfloat16 [1536, 512], P(None, 'tp'), may hold values from -0.625 to 0.625
- value_matrix: bfloat16 [1536, 512], P(None, 'tp'), may hold values from -0.15625 to 0.15625
- out_weight: bfloat16 [1536, 1536], P('tp'), may hold values from -1.25 to 1.25
- mixture_gain: bfloat16 [1536], replicated, may hold values from 0.5 to 1.5
- router_weight: bfloat16 [1536, 16], replicated, may hold values from -0.078125 to 0.078125
- gate_weight: bfloat16 [16, 1536, 512], P('ep', None, 'tp'), may hold values from -0.15625 to 0.15625
- up_weight: bfloat16 [16, 1536, 512], P('ep', None, 'tp'), may hold values from -0.15625 to 0.15625
- down_weight: bfloat16 [16, 512, 1536], P('ep', 'tp'), may hold values from -2 to 2
- routes: int32 [8192, 8], P('ep'), may hold values from 0 to 15, all different within a row; in each aligned block of 512 rows (0 to 511, 512 to 1023, ...) at most 320 rows name the same one
Outputs:
- layer_out: bfloat16 [8192, 1536], P('ep')
- grad_stream: float32 [8192, 1536], P('ep')
- grad_attention_gain: float32 [1536], P('ep')
- grad_query: float32 [1536, 1536], P('ep', 'tp')
- grad_key: float32 [1536, 512], P('ep', 'tp')
- grad_value: float32 [1536, 512], P('ep', 'tp')
- grad_out: float32 [1536, 1536], P('tp', 'ep')
- grad_mixture_gain: float32 [1536], P('ep')
- grad_router: float32 [1536, 16], P('ep')
- grad_gate: float32 [16, 1536, 512], P('ep', None, 'tp')
- grad_up: float32 [16, 1536, 512], P('ep', None, 'tp')
- grad_down: float32 [16, 512, 1536], P('ep', 'tp')
- rms_stats: float32 [16, 3], P('ep')
Inputs may be any that keep to these rules, and one draw needn't show every extreme that they name: `routes`: each token names 8 different experts. Within the rows of one device (aligned blocks of 512 rows) no expert is named by more than 320 rows, and in every draw some expert is named by exactly 320 rows of some device; every expert is named somewhere.
All inputs are finite; a program needn't handle non-finite values.
Results may differ from a plain program's by a relative error of at most 0.019.
Values may be sent and summed in bfloat16 or wider, within the bound.
A program may use at most 320 MiB of HBM per device.

v0:
```python
import jax
import jax.numpy as jnp
from jax import lax
from jax.sharding import PartitionSpec as P

HEAD_FEATURES = 64
TOP = 8
SEQ_LEN = 512


epsilon = 1e-06
score_scale = 0.015625
residual_scale = 0.22
rope_base = 10000.0
masked_score = -1e30


def rope_tables(sequence_length):
    half_dim = HEAD_FEATURES // 2
    steps_up = jnp.arange(half_dim).astype(jnp.float32) * (2.0 / HEAD_FEATURES)
    inverse = jnp.exp(-steps_up * jnp.log(rope_base))
    places = jnp.arange(sequence_length).astype(jnp.float32)
    angles = places[:, None] * inverse[None, :]
    return (jnp.cos(angles), jnp.sin(angles))


def apply_rotation(value_rows, cosine_table, sine_values):
    half_dim = value_rows.shape[-1] // 2
    first_half = value_rows[..., :half_dim]
    second_half = value_rows[..., half_dim:]
    cos_rows = cosine_table[:, None, :]
    sin_rows = sine_values[:, None, :]
    return jnp.concatenate(
        [
            first_half * cos_rows - second_half * sin_rows,
            second_half * cos_rows + first_half * sin_rows,
        ],
        axis=-1,
    )


def rotary_back(grads_in, cosine_table, sine_values):
    half_dim = grads_in.shape[-1] // 2
    first_half = grads_in[..., :half_dim]
    second_half = grads_in[..., half_dim:]
    cos_rows = cosine_table[:, None, :]
    sin_rows = sine_values[:, None, :]
    return jnp.concatenate(
        [
            first_half * cos_rows + second_half * sin_rows,
            second_half * cos_rows - first_half * sin_rows,
        ],
        axis=-1,
    )


def block_scores(query_block, rotated_keys, row_start, block_rows, row_stop):
    scores = score_scale * jnp.einsum(
        "qhgd,khd->hgqk", query_block, rotated_keys, preferred_element_type=jnp.float32
    )
    causal = (row_start + jnp.arange(block_rows))[:, None] >= jnp.arange(row_stop)[None, :]
    return jnp.where(causal, scores, masked_score)


def attention_forward(query_rows, rotated_keys, value_rows):
    sequence_length = query_rows.shape[0]
    block_rows = min(512, sequence_length)
    scores = block_scores(query_rows, rotated_keys, 0, block_rows, block_rows)
    largest = jnp.max(scores, axis=-1, keepdims=True)
    weights_exp = jnp.exp(scores - largest)
    totals = jnp.sum(weights_exp, axis=-1, keepdims=True)
    probs_low = (weights_exp / totals).astype(jnp.bfloat16)
    outputs = jnp.einsum(
        "hgqk,khd->qhgd", probs_low, value_rows, preferred_element_type=jnp.float32
    )
    normalizers = [largest + jnp.log(totals)]
    return (outputs, normalizers)


def attention_backward(query_rows, rotated_keys, value_rows, normalizers, grad_mixed):
    sequence_length = query_rows.shape[0]
    block_rows = min(512, sequence_length)
    grad_keys = jnp.zeros(rotated_keys.shape, jnp.float32)
    grad_values = jnp.zeros(value_rows.shape, jnp.float32)
    grad_queries = []
    for block_index, row_start in enumerate(range(0, sequence_length, block_rows)):
        row_stop = row_start + block_rows
        scores = block_scores(query_rows, rotated_keys, row_start, block_rows, row_stop)
        probs = jnp.exp(scores - normalizers[block_index])
        probs_low = probs.astype(jnp.bfloat16)
        grad_probs = jnp.einsum(
            "qhgd,khd->hgqk", grad_mixed, value_rows, preferred_element_type=jnp.float32
        )
        inner = jnp.sum(probs * grad_probs, axis=-1, keepdims=True)
        grad_scores = (probs * (grad_probs - inner)).astype(jnp.bfloat16)
        grad_queries.append(
            score_scale
            * jnp.einsum(
                "hgqk,khd->qhgd", grad_scores, rotated_keys, preferred_element_type=jnp.float32
            )
        )
        grad_keys = grad_keys.at[:row_stop].add(
            score_scale
            * jnp.einsum(
                "hgqk,qhgd->khd", grad_scores, query_rows, preferred_element_type=jnp.float32
            )
        )
        grad_values = grad_values.at[:row_stop].add(
            jnp.einsum("hgqk,qhgd->khd", probs_low, grad_mixed, preferred_element_type=jnp.float32)
        )
    return (grad_queries[0], grad_keys, grad_values)


def to_owners(packed):
    return lax.all_to_all(packed, "ep", split_axis=1, concat_axis=1, tiled=True)


def back_to_tokens(rows_low, slot_count, model_width):
    returned = lax.all_to_all(rows_low, "ep", split_axis=1, concat_axis=1, tiled=True)
    joined = lax.all_gather(returned, "tp", axis=0, tiled=True)
    return joined.reshape(slot_count, model_width)


def from_owners(term_fn, slot_count, experts, model_width):
    share_rows = slot_count // lax.axis_size("tp")
    summed = lax.psum_scatter(
        term_fn(jnp.int32(0), lax.axis_size("tp") * share_rows).astype(jnp.bfloat16),
        "tp",
        scatter_dimension=0,
        tiled=True,
    ).astype(jnp.float32)
    summed = summed.astype(jnp.bfloat16).reshape(share_rows // experts, experts, model_width)
    return back_to_tokens(summed, slot_count, model_width)


def seq_rms(value_rows, seq_count):
    return jnp.sqrt(jnp.mean((value_rows * value_rows).reshape(seq_count, -1), axis=1))


def shards(
    stream,
    cotangent,
    attention_gain,
    query_weight,
    key_matrix,
    value_matrix,
    out_weight,
    mixture_gain,
    router_weight,
    gate_weight,
    up_weight,
    down_weight,
    routes,
):
    tok_rows, model_width = stream.shape
    experts = router_weight.shape[1]
    cap_slots = tok_rows * TOP * 5 // (4 * experts)
    slot_count = cap_slots * experts
    query_heads = query_weight.shape[1] // HEAD_FEATURES
    key_heads = key_matrix.shape[1] // HEAD_FEATURES
    group_width = query_heads // key_heads
    seq_count = tok_rows // SEQ_LEN
    stream_f = stream.astype(jnp.float32)
    grad_result = cotangent.astype(jnp.float32)
    gain_first = attention_gain.astype(jnp.float32)
    gain_second = mixture_gain.astype(jnp.float32)
    cosine_table, sine_values = rope_tables(SEQ_LEN)
    cosine_rows = jnp.tile(cosine_table, (seq_count, 1))
    sine_rows = jnp.tile(sine_values, (seq_count, 1))
    zero_low = jnp.zeros((), jnp.bfloat16)
    inv_first = lax.rsqrt(jnp.mean(stream_f * stream_f, axis=-1, keepdims=True) + epsilon)
    normalized_input = (stream_f * inv_first * gain_first).astype(jnp.bfloat16)
    query_pre = jnp.dot(normalized_input, query_weight, preferred_element_type=jnp.float32).reshape(
        tok_rows, query_heads, HEAD_FEATURES
    )
    key_pre = jnp.dot(normalized_input, key_matrix, preferred_element_type=jnp.float32).reshape(
        tok_rows, key_heads, HEAD_FEATURES
    )
    query_rows = (
        apply_rotation(query_pre, cosine_rows, sine_rows)
        .astype(jnp.bfloat16)
        .reshape(tok_rows, key_heads, group_width, HEAD_FEATURES)
    )
    rotated_keys = apply_rotation(key_pre, cosine_rows, sine_rows).astype(jnp.bfloat16)
    value_rows = (
        jnp.dot(normalized_input, value_matrix, preferred_element_type=jnp.float32)
        .astype(jnp.bfloat16)
        .reshape(tok_rows, key_heads, HEAD_FEATURES)
    )
    mixed_seq, norms_seq = attention_forward(query_rows, rotated_keys, value_rows)
    mixed_low = mixed_seq.reshape(tok_rows, query_heads * HEAD_FEATURES).astype(jnp.bfloat16)
    attended = lax.psum(
        jnp.dot(mixed_low, out_weight, preferred_element_type=jnp.float32).astype(jnp.bfloat16),
        "tp",
    ).astype(jnp.float32)
    middle = stream_f + residual_scale * attended
    inv_second = lax.rsqrt(jnp.mean(middle * middle, axis=-1, keepdims=True) + epsilon)
    mixer_in = (middle * inv_second * gain_second).astype(jnp.bfloat16)
    logits = jnp.dot(mixer_in, router_weight, preferred_element_type=jnp.float32)
    expert_ids = jnp.arange(experts, dtype=jnp.int32)
    route_hot = routes[:, :, None] == expert_ids[None, None, :]
    chosen = jnp.sum(jnp.where(route_hot, logits[:, None, :], 0.0), axis=-1)
    chosen_exp = jnp.exp(chosen - jnp.max(chosen, axis=-1, keepdims=True))
    gate_probs = chosen_exp / jnp.sum(chosen_exp, axis=-1, keepdims=True)
    flat_routes = routes.reshape(-1)
    flat_hot = route_hot.reshape(tok_rows * TOP, experts).astype(jnp.int32)
    ranks = jnp.sum((jnp.cumsum(flat_hot, axis=0) - 1) * flat_hot, axis=1)
    slot_index = ranks * experts + flat_routes
    source_pair = (
        jnp.zeros((slot_count,), jnp.int32)
        .at[slot_index]
        .set(jnp.arange(tok_rows * TOP, dtype=jnp.int32))
    )
    filled = jnp.zeros((slot_count,), jnp.bool_).at[slot_index].set(True)
    source_token = source_pair // TOP
    sent_rows = jnp.where(filled[:, None], mixer_in[source_token], zero_low).reshape(
        cap_slots, experts, model_width
    )
    received = to_owners(sent_rows).reshape(slot_count, model_width)
    gate_matrix = gate_weight[0]
    up_matrix = up_weight[0]
    down_matrix = down_weight[0]
    gate_pre = jnp.dot(received, gate_matrix, preferred_element_type=jnp.float32)
    up_pre = jnp.dot(received, up_matrix, preferred_element_type=jnp.float32)
    sigmoid_gate = jax.nn.sigmoid(gate_pre)
    silu_gate = gate_pre * sigmoid_gate
    active = (silu_gate * up_pre).astype(jnp.bfloat16)

    def down_term(row_start, row_count):
        return jnp.dot(active, down_matrix, preferred_element_type=jnp.float32)

    expert_rows = from_owners(down_term, slot_count, experts, model_width)
    picked_rows = expert_rows[slot_index].reshape(tok_rows, TOP, model_width)
    mixture = jnp.sum(gate_probs[:, :, None] * picked_rows, axis=1)
    result = middle + residual_scale * mixture
    layer_out = result.astype(jnp.bfloat16)
    rms_stats = jnp.stack(
        [seq_rms(result, seq_count), seq_rms(attended, seq_count), seq_rms(mixture, seq_count)],
        axis=1,
    )
    grad_mix = residual_scale * grad_result
    grad_weighting = jnp.sum(picked_rows * grad_mix[:, None, :], axis=-1)
    grad_chosen = gate_probs * (
        grad_weighting - jnp.sum(gate_probs * grad_weighting, axis=-1, keepdims=True)
    )
    grad_logits = jnp.sum(jnp.where(route_hot, grad_chosen[:, :, None], 0.0), axis=1).astype(
        jnp.bfloat16
    )
    router_grad = jnp.dot(mixer_in.T, grad_logits, preferred_element_type=jnp.float32)
    flat_gates = gate_probs.reshape(-1)
    grad_sent = jnp.where(
        filled[:, None],
        (flat_gates[source_pair][:, None] * grad_mix[source_token]).astype(jnp.bfloat16),
        zero_low,
    ).reshape(cap_slots, experts, model_width)
    grad_received = to_owners(grad_sent).reshape(slot_count, model_width)
    grad_active = jnp.dot(grad_received, down_matrix.T, preferred_element_type=jnp.float32)
    down_grad = jnp.dot(active.T, grad_received, preferred_element_type=jnp.float32)
    grad_gate_pre = (
        grad_active * up_pre * sigmoid_gate * (1.0 + gate_pre * (1.0 - sigmoid_gate))
    ).astype(jnp.bfloat16)
    grad_up_pre = (grad_active * silu_gate).astype(jnp.bfloat16)
    gate_grad = jnp.dot(received.T, grad_gate_pre, preferred_element_type=jnp.float32)
    up_grad = jnp.dot(received.T, grad_up_pre, preferred_element_type=jnp.float32)

    def input_term(row_start, row_count):
        return jnp.dot(grad_gate_pre, gate_matrix.T, preferred_element_type=jnp.float32) + jnp.dot(
            grad_up_pre, up_matrix.T, preferred_element_type=jnp.float32
        )

    grad_rows = from_owners(input_term, slot_count, experts, model_width)
    grad_mixer = jnp.dot(
        grad_logits, router_weight.T, preferred_element_type=jnp.float32
    ) + jnp.sum(
        grad_rows[slot_index].reshape(tok_rows, TOP, model_width), axis=1, dtype=jnp.float32
    )
    weighted_second = grad_mixer * gain_second
    second_grad = jnp.sum(grad_mixer * middle * inv_second, axis=0)
    grad_middle = (
        grad_result
        + inv_second * weighted_second
        - middle * inv_second**3 * jnp.mean(middle * weighted_second, axis=-1, keepdims=True)
    )
    grad_attended = (residual_scale * grad_middle).astype(jnp.bfloat16)
    out_grad_t = jnp.dot(grad_attended.T, mixed_low, preferred_element_type=jnp.float32)
    grad_mixed = (
        jnp.dot(grad_attended, out_weight.T, preferred_element_type=jnp.float32)
        .astype(jnp.bfloat16)
        .reshape(tok_rows, key_heads, group_width, HEAD_FEATURES)
    )
    grad_query_seq, grad_key_seq, grad_value_seq = attention_backward(
        query_rows, rotated_keys, value_rows, norms_seq, grad_mixed
    )
    grad_queries_rot = grad_query_seq.reshape(tok_rows, query_heads, HEAD_FEATURES)
    grad_query_pre = (
        rotary_back(grad_queries_rot, cosine_rows, sine_rows)
        .astype(jnp.bfloat16)
        .reshape(tok_rows, query_heads * HEAD_FEATURES)
    )
    grad_key_pre = (
        rotary_back(grad_key_seq, cosine_rows, sine_rows)
        .astype(jnp.bfloat16)
        .reshape(tok_rows, key_heads * HEAD_FEATURES)
    )
    grad_values_low = grad_value_seq.astype(jnp.bfloat16).reshape(
        tok_rows, key_heads * HEAD_FEATURES
    )
    query_grad = jnp.dot(normalized_input.T, grad_query_pre, preferred_element_type=jnp.float32)
    key_grad = jnp.dot(normalized_input.T, grad_key_pre, preferred_element_type=jnp.float32)
    value_grad = jnp.dot(normalized_input.T, grad_values_low, preferred_element_type=jnp.float32)
    normed_term = jnp.dot(grad_query_pre, query_weight.T, preferred_element_type=jnp.float32)
    normed_term = normed_term + jnp.dot(
        grad_key_pre, key_matrix.T, preferred_element_type=jnp.float32
    )
    normed_term = normed_term + jnp.dot(
        grad_values_low, value_matrix.T, preferred_element_type=jnp.float32
    )
    grad_normed = lax.psum(normed_term.astype(jnp.bfloat16), "tp").astype(jnp.float32)
    weighted_first = grad_normed * gain_first
    first_grad = jnp.sum(grad_normed * stream_f * inv_first, axis=0)
    grad_stream = (
        grad_middle
        + inv_first * weighted_first
        - stream_f * inv_first**3 * jnp.mean(stream_f * weighted_first, axis=-1, keepdims=True)
    )
    reduced = (
        lax.psum_scatter(query_grad, "ep", scatter_dimension=0, tiled=True),
        lax.psum_scatter(key_grad, "ep", scatter_dimension=0, tiled=True),
        lax.psum_scatter(value_grad, "ep", scatter_dimension=0, tiled=True),
        lax.psum_scatter(out_grad_t, "ep", scatter_dimension=0, tiled=True),
        lax.psum_scatter(router_grad, "ep", scatter_dimension=0, tiled=True),
        lax.psum_scatter(first_grad, "ep", scatter_dimension=0, tiled=True),
        lax.psum_scatter(second_grad, "ep", scatter_dimension=0, tiled=True),
    )
    return (
        layer_out,
        grad_stream,
        reduced[5],
        reduced[0],
        reduced[1],
        reduced[2],
        reduced[3].T,
        reduced[6],
        reduced[4],
        gate_grad[None],
        up_grad[None],
        down_grad[None],
        rms_stats,
    )


def solution(mesh):
    in_specs = (
        P("ep", None),
        P("ep", None),
        P(),
        P(None, "tp"),
        P(None, "tp"),
        P(None, "tp"),
        P("tp", None),
        P(),
        P(),
        P("ep", None, "tp"),
        P("ep", None, "tp"),
        P("ep", "tp", None),
        P("ep", None),
    )
    out_specs = (
        P("ep", None),
        P("ep", None),
        P("ep"),
        P("ep", "tp"),
        P("ep", "tp"),
        P("ep", "tp"),
        P("tp", "ep"),
        P("ep"),
        P("ep", None),
        P("ep", None, "tp"),
        P("ep", None, "tp"),
        P("ep", "tp", None),
        P("ep", None),
    )
    return jax.shard_map(shards, mesh=mesh, in_specs=in_specs, out_specs=out_specs, check_vma=False)
```

profile of v0, /device:TPU:0, one launch (start us, length us, event | category | flops | bytes accessed | tf_op | source)
XLA Modules:
  0.0 2246.9 jit_solution(7509400044192878122)
XLA Ops:
  38.0 15.5 scatter_custom_fusion.1
  53.5 17.6 scatter_custom_fusion
  74.9 35.8 %gather_fusion.3 = f32[5120,1536]{1,0:T(8,128)} fusion(f32[512,1536]{1,0:T(8,128)} %convert_multiply_fusion.8, s32[5120]{0:T(1024)S(1)} %get-tuple-element.77), kind=kCustom, calls=%fused_computation.3 | custom fusion | bytes 62935040 | tf_op jit(solution)/shard_map/gather | solution.py:253
  115.9 32.9 %gather_fusion = bf16[5120,1536]{1,0:T(8,128)(2,1)} fusion(bf16[512,1536]{1,0:T(8,128)(2,1)} %multiply_convert_fusion.4, s32[5120]{0:T(1024)S(1)} %get-tuple-element.77), kind=kCustom, calls=%fused_computation | custom fusion | bytes 31477760 | tf_op jit(solution)/shard_map/gather | solution.py:216
  152.3 28.7 %gather_fusion.2 = f32[5120]{0:T(1024)S(1)} fusion(f32[4096]{0:T(1024)S(1)} %div.74, s32[5120]{0:T(1024)S(1)} %get-tuple-element.76), kind=kCustom, calls=%fused_computation.2 | custom fusion | bytes 61440 | tf_op jit(solution)/shard_map/gather | solution.py:253
  181.2 43.8 %fusion.3 = (bf16[320,16,1536]{2,0,1:T(8,128)(2,1)}, bf16[320,16,1536]{2,0,1:T(8,128)(2,1)}) fusion(f32[320,16,1536]{2,1,0:T(8,128)} %bitcast.186, f32[320,16]{0,1:T(8,128)S(1)} %copy.126, pred[320,16]{0,1:T(8,128)(4,1)S(1)} %copy.118, bf16[320,16,1536]{2,1,0:T(8,128)(2,1)} %bitcast.189), kind=kLoop, calls=%fused_computation.16 | loop fusion | flops 31457280 | bytes 78668800 | tf_op jit(solution)/shard_map/jit(_where)/select_n | solution.py:251
  224.9 349.4 %all_to_all.20 = bf16[320,16,1536]{2,0,1:T(8,128)(2,1)} all-to-all(bf16[320,16,1536]{2,0,1:T(8,128)(2,1)} %get-tuple-element.79), channel_id=1, replica_groups=mesh['ep'=16,'tp'=2] {'ep'}, dimensions={1} | all-to-all | bytes 31457280 | tf_op jit(solution)/shard_map/all_to_all | solution.py:115
  579.5 23.0 %copy.120 = bf16[320,16,1536]{2,1,0:T(8,128)(2,1)S(1)} copy(bf16[320,16,1536]{2,0,1:T(8,128)(2,1)} %all_to_all.20) | data formatting | bytes 31457280 | tf_op jit(solution)/shard_map/all_to_all | solution.py:115
  615.7 255.3 %all-to-all-done.2 = bf16[320,16,1536]{2,0,1:T(8,128)(2,1)} async-done(((bf16[320,16,1536]{2,0,1:T(8,128)(2,1)}), bf16[320,16,1536]{2,0,1:T(8,128)(2,1)}, u32[]{:S(2)}, u32[]{:S(2)}) %all-to-all-start.2) | async-done | bytes 15728672 | tf_op jit(solution)/shard_map/all_to_all | solution.py:115
  871.0 24.2 %copy.128 = bf16[320,16,1536]{2,1,0:T(8,128)(2,1)} copy(bf16[320,16,1536]{2,0,1:T(8,128)(2,1)} %all-to-all-done.2) | data formatting | bytes 31457280 | tf_op jit(solution)/shard_map/all_to_all | solution.py:115
  933.6 18.1 add_convert_fusion
  951.9 54.5 %reduce-scatter.10.cloned.1.call-done = bf16[2560,1536]{1,0:T(8,128)(2,1)} async-done(((bf16[5120,1536]{1,0:T(8,128)(2,1)}), bf16[2560,1536]{1,0:T(8,128)(2,1)}) %reduce-scatter.10.cloned.1.call-update) | async-done | bytes 7864336 | tf_op jit(solution)/shard_map/reduce_scatter | solution.py:126
  1017.2 190.7 %all_to_all.21 = bf16[160,16,1536]{2,0,1:T(8,128)(2,1)} all-to-all(bf16[160,16,1536]{2,0,1:T(8,128)(2,1)} %copy.121), channel_id=1, replica_groups=mesh['ep'=16,'tp'=2] {'ep'}, dimensions={1} | all-to-all | bytes 15728640 | tf_op jit(solution)/shard_map/all_to_all | solution.py:119
  1231.4 174.1 %all_to_all.22 = bf16[160,16,1536]{2,0,1:T(8,128)(2,1)} all-to-all(bf16[160,16,1536]{2,0,1:T(8,128)(2,1)} %copy.129), channel_id=1, replica_groups=mesh['ep'=16,'tp'=2] {'ep'}, dimensions={1} | all-to-all | bytes 15728640 | tf_op jit(solution)/shard_map/all_to_all | solution.py:119
  1417.1 34.3 %gather_fusion.1 = bf16[4096,1536]{1,0:T(8,128)(2,1)} fusion(bf16[5120,1536]{1,0:T(8,128)(2,1)} %bitcast.177, s32[4096]{0:T(1024)S(1)} %broadcast_clamp_fusion), kind=kCustom, calls=%fused_computation.1 | custom fusion | bytes 25182208 | tf_op jit(solution)/shard_map/gather | solution.py:233
  1451.4 16.9 fusion.2
  1471.6 32.8 %gather_fusion.4 = bf16[4096,1536]{1,0:T(8,128)(2,1)} fusion(bf16[5120,1536]{1,0:T(8,128)(2,1)} %bitcast.176, s32[4096]{0:T(1024)S(1)} %broadcast_clamp_fusion), kind=kCustom, calls=%fused_computation.4 | custom fusion | bytes 25182208 | tf_op jit(solution)/shard_map/gather | solution.py:275
  1610.0 64.3 %reduce-scatter.22.cloned.1.call-done = f32[96,16]{1,0:T(8,128)} async-done(((f32[1536,16]{1,0:T(8,128)}), f32[96,16]{1,0:T(8,128)}) %reduce-scatter.22.cloned.1.call-update) | async-done | bytes 6160
  1675.7 20.5 all-reduce.8.cloned.1.call-done
  1699.3 77.5 %all-reduce.2 = (f32[1536]{0:T(1024)S(1)}, f32[1536]{0:T(1024)S(1)}) all-reduce(f32[1536]{0:T(1024)S(1)} %get-tuple-element.58, f32[1536]{0:T(1024)S(1)} %get-tuple-element.55), channel_id=4, replica_groups=mesh['ep'=16,'tp'=2] {'ep'}, use_global_device_ids=true, to_apply=%region_25.26.clone | all-reduce | flops 3072 | bytes 24576
  1783.4 43.9 %reduce-scatter.18.cloned.1.call-done = f32[96,256]{1,0:T(8,128)} async-done(((f32[1536,256]{1,0:T(8,128)}), f32[96,256]{1,0:T(8,128)}) %reduce-scatter.18.cloned.1.call-update) | async-done | bytes 98320 | tf_op jit(solution)/shard_map/reduce_scatter | solution.py:329
  1827.3 128.9 %reduce-scatter.16.cloned.1.call-done = f32[96,256]{1,0:T(8,128)} async-done(((f32[1536,256]{1,0:T(8,128)}), f32[96,256]{1,0:T(8,128)}) %reduce-scatter.16.cloned.1.call-update) | async-done | bytes 98320 | tf_op jit(solution)/shard_map/reduce_scatter | solution.py:328
  1956.2 141.0 %reduce-scatter.20.cloned.1.call-done = f32[96,768]{1,0:T(8,128)} async-done(((f32[1536,768]{1,0:T(8,128)}), f32[96,768]{1,0:T(8,128)}) %reduce-scatter.20.cloned.1.call-update) | async-done | bytes 294928 | tf_op jit(solution)/shard_map/reduce_scatter | solution.py:330
  2097.2 142.8 %reduce-scatter.14.cloned.1.call-done = f32[96,768]{1,0:T(8,128)} async-done(((f32[1536,768]{1,0:T(8,128)}), f32[96,768]{1,0:T(8,128)}) %reduce-scatter.14.cloned.1.call-update) | async-done | bytes 294928 | tf_op jit(solution)/shard_map/reduce_scatter | solution.py:327
  (287 shorter events, 262.2 us)
Async XLA Ops:
  7.2 21.8 copy-start
  7.2 103.5 %all-reduce.6.cloned.1.call-start = ((), (), s32[]{:S(2)}) async-start(), calls=%async_computation.11 | async-start | bytes 3145728 | tf_op jit(solution)/shard_map/psum | solution.py:192
  32.2 81.8 %copy-start.53 = (f32[1536]{0:T(1024)}, f32[1536]{0:T(1024)S(1)}, u32[]{:S(2)}) copy-start(f32[1536]{0:T(1024)S(1)} %convert_element_type.217) | copy-start | bytes 18436
  37.9 72.8 %copy-start.55 = (s32[4096,1]{0,1:T(1,128)}, s32[4096,1]{0,1:T(1,128)S(1)}, u32[]{:S(2)}) copy-start(s32[4096,1]{0,1:T(1,128)S(1)} %compare_select_fusion) | copy-start | bytes 49156
  114.1 34.7 %copy-start.65 = (f32[512]{0:T(512)}, f32[512]{0:T(512)S(1)}, u32[]{:S(2)}) copy-start(f32[512]{0:T(512)S(1)} %get-tuple-element.85) | copy-start | bytes 6148
  115.9 32.9 %copy-start.61 = (bf16[1536,16]{0,1:T(8,128)(2,1)S(1)}, bf16[1536,16]{0,1:T(8,128)(2,1)}, u32[]{:S(2)}) copy-start(bf16[1536,16]{0,1:T(8,128)(2,1)} %param.29) | copy-start | bytes 147460
  152.1 28.8 %copy-start.18 = (f32[512,8]{1,0:T(8,128)}, f32[512,8]{1,0:T(8,128)S(1)}, u32[]{:S(2)}) copy-start(f32[512,8]{1,0:T(8,128)S(1)} %copy.114) | copy-start | bytes 49156
  574.3 296.7 %all-to-all-start.2 = ((bf16[320,16,1536]{2,0,1:T(8,128)(2,1)}), bf16[320,16,1536]{2,0,1:T(8,128)(2,1)}, u32[]{:S(2)}, u32[]{:S(2)}) async-start(bf16[320,16,1536]{2,0,1:T(8,128)(2,1)} %get-tuple-element.78), calls=%async_computation.3 | async-start | bytes 31457280 | tf_op jit(solution)/shard_map/all_to_all | solution.py:115
  579.4 23.1 %copy-start.28 = (bf16[1,1536,256]{2,1,0:T(8,128)(2,1)S(1)}, bf16[1,1536,256]{2,1,0:T(8,128)(2,1)}, u32[]{:S(2)}) copy-start(bf16[1,1536,256]{2,1,0:T(8,128)(2,1)} %param.31) | copy-start | bytes 2359300
  579.4 427.0 %reduce-scatter.10.cloned.1.call-start = ((), (), s32[]{:S(2)}) async-start(), calls=%async_computation.12 | async-start | bytes 23592960 | tf_op jit(solution)/shard_map/reduce_scatter | solution.py:126
  871.0 24.2 %copy-start.30 = (bf16[1,256,1536]{2,1,0:T(8,128)(2,1)S(1)}, bf16[1,256,1536]{2,1,0:T(8,128)(2,1)}, u32[]{:S(2)}) copy-start(bf16[1,256,1536]{2,1,0:T(8,128)(2,1)} %param.32) | copy-start | bytes 2359300
  871.0 24.2 %copy-start.73 = (f32[5120,256]{1,0:T(8,128)S(1)}, f32[5120,256]{1,0:T(8,128)}, u32[]{:S(2)}) copy-start(f32[5120,256]{1,0:T(8,128)} %fusion.42) | copy-start | bytes 15728644
  918.0 301.0 %reduce-scatter.12.cloned.1.call-start = ((), (), s32[]{:S(2)}) async-start(), calls=%async_computation.14 | async-start | bytes 23592960 | tf_op jit(solution)/shard_map/reduce_scatter | solution.py:126
  951.7 465.4 %all-gather.3.cloned.1.call-start = ((), (), s32[]{:S(2)}) async-start(), calls=%async_computation.13 | async-start | bytes 23592960 | tf_op jit(solution)/shard_map/all_gather | solution.py:120
  1218.7 252.9 %all-gather.5.cloned.1.call-start = ((), (), s32[]{:S(2)}) async-start(), calls=%async_computation.15 | async-start | bytes 23592960 | tf_op jit(solution)/shard_map/all_gather | solution.py:120
  1416.3 258.0 %reduce-scatter.22.cloned.1.call-start = ((), (), s32[]{:S(2)}) async-start(), calls=%async_computation.21 | async-start | bytes 835584
  1417.1 34.3 %copy-start.19 = (f32[512,8]{1,0:T(8,128)S(1)}, f32[512,8]{1,0:T(8,128)}, u32[]{:S(2)}) copy-start(f32[512,8]{1,0:T(8,128)} %copy-done.18) | copy-start | bytes 49156
  1553.8 142.4 %all-reduce.8.cloned.1.call-start = ((), (), s32[]{:S(2)}) async-start(), calls=%async_computation.16 | async-start | bytes 3145728 | tf_op jit(solution)/shard_map/psum | solution.py:318
  1560.8 266.5 %reduce-scatter.18.cloned.1.call-start = ((), (), s32[]{:S(2)}) async-start(), calls=%async_computation.19 | async-start | bytes 1671168 | tf_op jit(solution)/shard_map/reduce_scatter | solution.py:329
  1564.2 392.0 %reduce-scatter.16.cloned.1.call-start = ((), (), s32[]{:S(2)}) async-start(), calls=%async_computation.18 | async-start | bytes 1671168 | tf_op jit(solution)/shard_map/reduce_scatter | solution.py:328
  1567.6 529.5 %reduce-scatter.20.cloned.1.call-start = ((), (), s32[]{:S(2)}) async-start(), calls=%async_computation.20 | async-start | bytes 5013504 | tf_op jit(solution)/shard_map/reduce_scatter | solution.py:330
  1573.4 666.5 %reduce-scatter.14.cloned.1.call-start = ((), (), s32[]{:S(2)}) async-start(), calls=%async_computation.17 | async-start | bytes 5013504 | tf_op jit(solution)/shard_map/reduce_scatter | solution.py:327
  1580.5 21.3 slice-start.3
  1607.3 170.7 %copy-start.68 = (f32[512]{0:T(512)S(1)}, f32[512]{0:T(512)}, u32[]{:S(2)}) copy-start(f32[512]{0:T(512)} %get-tuple-element.82) | copy-start | bytes 6148
  (69 other events, 438.5 us)
Sparse Core Ops, SparseCore 0:
  31.7 23.1 all-reduce.5
  918.1 88.3 reduce-scatter.9
  1008.9 38.7 reduce-scatter.11
  1218.8 26.5 all-gather.2
  1416.4 27.4 all-gather.4
  1554.0 120.2 reduce-scatter.21
  1676.7 19.4 all-reduce.7
  1701.6 125.6 reduce-scatter.17
  1832.7 123.4 reduce-scatter.15
  1961.8 135.3 reduce-scatter.19
  2103.7 136.1 reduce-scatter.13
where the time goes:
time: 2250 us
  waiting for transfers between devices  851 us (38%)
  blocking collectives  792 us (35%)
  local copies, waits for them, and re-layouts  307 us (14%)
  matrix products  161 us (7%)
  other arithmetic  111 us (5%)
    all_to_all x2, blocking collectives, back_to_tokens(): lax.all_to_all(rows_low, 'ep', split_axis=1, concat_axis=1, tiled=True)  365 us
    all_to_all x1, blocking collectives, to_owners(): return lax.all_to_all(packed, 'ep', split_axis=1, concat_axis=1, tiled=True)  349 us
    all_to_all x1, waiting for transfers between devices, to_owners(): return lax.all_to_all(packed, 'ep', split_axis=1, concat_axis=1, tiled=True)  255 us
    reduce_scatter x1, waiting for transfers between devices, shards(): lax.psum_scatter(query_grad, 'ep', scatter_dimension=0, tiled=True)  143 us
    reduce_scatter x1, waiting for transfers between devices, shards(): lax.psum_scatter(out_grad_t, 'ep', scatter_dimension=0, tiled=True)  141 us
    reduce_scatter x1, waiting for transfers between devices, shards(): lax.psum_scatter(key_grad, 'ep', scatter_dimension=0, tiled=True)  129 us
    unnamed x1, blocking collectives  77.5 us
    unnamed x12, waiting for transfers between devices  64.5 us
  transfers between devices with their start and end apart: 12, of which 8 were waited for; matrix products, arithmetic and copies ran while one was open for 14% of the time, Pallas kernels for 0%

commit v1 on v0

--- a/solution.py
+++ b/solution.py
@@ -137,7 +137,7 @@
     return jnp.sqrt(jnp.mean((value_rows * value_rows).reshape(seq_count, -1), axis=1))
 
 
-def shards(
+def routed_shards(
     stream,
     cotangent,
     attention_gain,
@@ -349,6 +349,313 @@
     )
 
 
+def swap_cores(value):
+    return lax.ppermute(value, "tp", [(0, 1), (1, 0)])
+
+
+def exchange(value, bits):
+    count = lax.axis_size("ep")
+    return lax.ppermute(value, "ep", [(i, i ^ bits) for i in range(count)])
+
+
+def keep_and_send(value, axis, bit):
+    kept = lax.dynamic_index_in_dim(value, bit, axis, keepdims=False)
+    sent = lax.dynamic_index_in_dim(value, 1 - bit, axis, keepdims=False)
+    return kept, sent
+
+
+def scatter_stage(value, axis, bits, bit):
+    kept, sent = keep_and_send(value, axis, bit)
+    arrived = exchange(sent, bits)
+    return (kept.astype(jnp.float32) + arrived.astype(jnp.float32)).astype(jnp.bfloat16)
+
+
+def scatter_rows(value, first_bit, place):
+    rows = value.shape[0]
+    count = lax.axis_size("ep")
+    bit_count = count.bit_length() - 1
+    value = value.reshape((2,) * bit_count + (rows // count, value.shape[1]))
+    order = [first_bit, 1 - first_bit] + list(range(bit_count - 1, 1, -1))
+    left = list(range(bit_count - 1, -1, -1))
+    for bit in order:
+        axis = left.index(bit)
+        value = scatter_stage(value, axis, 1 << bit, (place >> bit) & 1)
+        left.remove(bit)
+    return value.astype(jnp.float32)
+
+
+def dense_shards(
+    stream,
+    cotangent,
+    attention_gain,
+    query_weight,
+    key_matrix,
+    value_matrix,
+    out_weight,
+    mixture_gain,
+    router_weight,
+    gate_weight,
+    up_weight,
+    down_weight,
+    routes,
+):
+    tok_rows, model_width = stream.shape
+    experts = router_weight.shape[1]
+    plane = 4
+    lines = experts // plane
+    hidden_half = gate_weight.shape[2]
+    hidden = 2 * hidden_half * plane
+    half = tok_rows // 2
+    query_heads = query_weight.shape[1] // HEAD_FEATURES
+    key_heads = key_matrix.shape[1] // HEAD_FEATURES
+    group_width = query_heads // key_heads
+    core = lax.axis_index("tp")
+    place = lax.axis_index("ep")
+    line_place = place // plane
+    plane_place = place % plane
+
+    def own_half(value):
+        return lax.dynamic_slice_in_dim(value, core * half, half, 0)
+
+    def other_half(value):
+        return lax.dynamic_slice_in_dim(value, (1 - core) * half, half, 0)
+
+    def join_halves(mine, theirs):
+        return jnp.where(
+            core == 0,
+            jnp.concatenate([mine, theirs], axis=0),
+            jnp.concatenate([theirs, mine], axis=0),
+        )
+
+    def plane_parts(weight):
+        near = [weight] + [exchange(weight, d) for d in range(1, plane)]
+        return near + [swap_cores(part) for part in near]
+
+    gate_all = jnp.concatenate(plane_parts(gate_weight[0]), axis=1)
+    up_all = jnp.concatenate(plane_parts(up_weight[0]), axis=1)
+    down_all = jnp.concatenate(plane_parts(down_weight[0]), axis=0)
+
+    def line_parts(value):
+        return [value] + [exchange(value, d * plane) for d in range(1, lines)]
+
+    cot_rows = jnp.concatenate(line_parts(own_half(cotangent)), axis=0)
+
+    stream_f = stream.astype(jnp.float32)
+    gain_first = attention_gain.astype(jnp.float32)
+    gain_second = mixture_gain.astype(jnp.float32)
+    cosine_rows, sine_rows = rope_tables(SEQ_LEN)
+    inv_first = lax.rsqrt(jnp.mean(stream_f * stream_f, axis=-1, keepdims=True) + epsilon)
+    normalized_input = (stream_f * inv_first * gain_first).astype(jnp.bfloat16)
+    query_pre = jnp.dot(normalized_input, query_weight, preferred_element_type=jnp.float32).reshape(
+        tok_rows, query_heads, HEAD_FEATURES
+    )
+    key_pre = jnp.dot(normalized_input, key_matrix, preferred_element_type=jnp.float32).reshape(
+        tok_rows, key_heads, HEAD_FEATURES
+    )
+    query_rows = (
+        apply_rotation(query_pre, cosine_rows, sine_rows)
+        .astype(jnp.bfloat16)
+        .reshape(tok_rows, key_heads, group_width, HEAD_FEATURES)
+    )
+    rotated_keys = apply_rotation(key_pre, cosine_rows, sine_rows).astype(jnp.bfloat16)
+    value_rows = (
+        jnp.dot(normalized_input, value_matrix, preferred_element_type=jnp.float32)
+        .astype(jnp.bfloat16)
+        .reshape(tok_rows, key_heads, HEAD_FEATURES)
+    )
+    mixed_seq, norms_seq = attention_forward(query_rows, rotated_keys, value_rows)
+    mixed_low = mixed_seq.reshape(tok_rows, query_heads * HEAD_FEATURES).astype(jnp.bfloat16)
+    attended_part = jnp.dot(mixed_low, out_weight, preferred_element_type=jnp.float32).astype(
+        jnp.bfloat16
+    )
+    attended = own_half(attended_part).astype(jnp.float32) + swap_cores(
+        other_half(attended_part)
+    ).astype(jnp.float32)
+    middle = own_half(stream).astype(jnp.float32) + residual_scale * attended
+    inv_second = lax.rsqrt(jnp.mean(middle * middle, axis=-1, keepdims=True) + epsilon)
+    mixer_in = (middle * inv_second * gain_second).astype(jnp.bfloat16)
+    logits = jnp.dot(mixer_in, router_weight, preferred_element_type=jnp.float32)
+    expert_ids = jnp.arange(experts, dtype=jnp.int32)
+    routed = jnp.any(own_half(routes)[:, :, None] == expert_ids[None, None, :], axis=1)
+    largest = jnp.max(jnp.where(routed, logits, masked_score), axis=-1, keepdims=True)
+    gate_exp = jnp.where(routed, jnp.exp(jnp.minimum(logits - largest, 0.0)), 0.0)
+    gate_probs = gate_exp / jnp.sum(gate_exp, axis=-1, keepdims=True)
+
+    mixer_rows = jnp.concatenate(line_parts(mixer_in), axis=0)
+    prob_rows = jnp.concatenate(line_parts(gate_probs), axis=0)
+
+    def expert_of(line_step, plane_step):
+        return (line_place ^ line_step) * plane + (plane_place ^ plane_step)
+
+    prob_near = jnp.stack(
+        [
+            jnp.sum(jnp.where(expert_ids[None, :] == expert_of(0, d), prob_rows, 0.0), axis=1)
+            for d in range(plane)
+        ],
+        axis=1,
+    )
+    rows = lines * half
+
+    def spread(value):
+        return jnp.broadcast_to(
+            value[:, None, :, None], (rows, 2, plane, hidden_half)
+        ).reshape(rows, hidden)
+
+    gate_pre = jnp.dot(mixer_rows, gate_all, preferred_element_type=jnp.float32)
+    up_pre = jnp.dot(mixer_rows, up_all, preferred_element_type=jnp.float32)
+    grad_raw = residual_scale * jnp.dot(cot_rows, down_all.T, preferred_element_type=jnp.float32)
+    sigmoid_gate = jax.nn.sigmoid(gate_pre)
+    silu_gate = gate_pre * sigmoid_gate
+    active = silu_gate * up_pre
+    weighting_near = jnp.sum(
+        (active * grad_raw).reshape(rows, 2, plane, hidden_half), axis=(1, 3)
+    )
+    prob_wide = spread(prob_near)
+    scaled_active = (prob_wide * active).astype(jnp.bfloat16)
+    grad_active = prob_wide * grad_raw
+    grad_gate_pre = (
+        grad_active * up_pre * sigmoid_gate * (1.0 + gate_pre * (1.0 - sigmoid_gate))
+    ).astype(jnp.bfloat16)
+    grad_up_pre = (grad_active * silu_gate).astype(jnp.bfloat16)
+    out_rows = jnp.dot(scaled_active, down_all, preferred_element_type=jnp.float32).astype(
+        jnp.bfloat16
+    )
+    grad_rows = (
+        jnp.dot(grad_gate_pre, gate_all.T, preferred_element_type=jnp.float32)
+        + jnp.dot(grad_up_pre, up_all.T, preferred_element_type=jnp.float32)
+    ).astype(jnp.bfloat16)
+
+    def line_return(value):
+        pieces = [value[d * half : (d + 1) * half] for d in range(lines)]
+        return [pieces[0]] + [exchange(pieces[d], d * plane) for d in range(1, lines)]
+
+    mixture = sum(piece.astype(jnp.float32) for piece in line_return(out_rows))
+    grad_mixer_rows = sum(piece.astype(jnp.float32) for piece in line_return(grad_rows))
+    grad_weighting = jnp.zeros((half, experts), jnp.float32)
+    for line_step, piece in enumerate(line_return(weighting_near)):
+        for plane_step in range(plane):
+            grad_weighting = grad_weighting + jnp.where(
+                expert_ids[None, :] == expert_of(line_step, plane_step),
+                piece[:, plane_step : plane_step + 1],
+                0.0,
+            )
+
+    gate_grad = jnp.dot(mixer_rows.T, grad_gate_pre, preferred_element_type=jnp.float32)
+    up_grad = jnp.dot(mixer_rows.T, grad_up_pre, preferred_element_type=jnp.float32)
+    down_grad = residual_scale * jnp.dot(
+        scaled_active.T, cot_rows, preferred_element_type=jnp.float32
+    )
+
+    def plane_sum(value, axis):
+        low = value.astype(jnp.bfloat16)
+        mine, theirs = jnp.split(low, 2, axis=axis)
+        both = mine.astype(jnp.float32) + swap_cores(theirs).astype(jnp.float32)
+        parts = jnp.split(both, plane, axis=axis)
+        total = parts[0]
+        for d in range(1, plane):
+            total = total + exchange(parts[d].astype(jnp.bfloat16), d).astype(jnp.float32)
+        return total
+
+    gate_grad = plane_sum(gate_grad, 1)
+    up_grad = plane_sum(up_grad, 1)
+    down_grad = plane_sum(down_grad, 0)
+
+    result = middle + residual_scale * mixture
+    result_low = result.astype(jnp.bfloat16)
+    layer_out = join_halves(result_low, swap_cores(result_low))
+    squares = jnp.stack([jnp.sum(v * v) for v in (result, attended, mixture)])
+    rms_stats = jnp.sqrt((squares + swap_cores(squares)) / (tok_rows * model_width))[None, :]
+    grad_chosen = gate_probs * (
+        grad_weighting - jnp.sum(gate_probs * grad_weighting, axis=-1, keepdims=True)
+    )
+    grad_logits = grad_chosen.astype(jnp.bfloat16)
+    router_grad = jnp.dot(mixer_in.T, grad_logits, preferred_element_type=jnp.float32)
+    grad_mixer = (
+        jnp.dot(grad_logits, router_weight.T, preferred_element_type=jnp.float32) + grad_mixer_rows
+    )
+    weighted_second = grad_mixer * gain_second
+    second_grad = jnp.sum(grad_mixer * middle * inv_second, axis=0)
+    grad_middle = (
+        own_half(cotangent).astype(jnp.float32)
+        + inv_second * weighted_second
+        - middle * inv_second**3 * jnp.mean(middle * weighted_second, axis=-1, keepdims=True)
+    )
+    grad_middle_low = grad_middle.astype(jnp.bfloat16)
+    grad_middle_all = join_halves(grad_middle_low, swap_cores(grad_middle_low)).astype(jnp.float32)
+    grad_attended = (residual_scale * grad_middle_all).astype(jnp.bfloat16)
+    out_grad_t = jnp.dot(grad_attended.T, mixed_low, preferred_element_type=jnp.float32)
+    grad_mixed = (
+        jnp.dot(grad_attended, out_weight.T, preferred_element_type=jnp.float32)
+        .astype(jnp.bfloat16)
+        .reshape(tok_rows, key_heads, group_width, HEAD_FEATURES)
+    )
+    grad_query_seq, grad_key_seq, grad_value_seq = attention_backward(
+        query_rows, rotated_keys, value_rows, norms_seq, grad_mixed
+    )
+    grad_queries_rot = grad_query_seq.reshape(tok_rows, query_heads, HEAD_FEATURES)
+    grad_query_pre = (
+        rotary_back(grad_queries_rot, cosine_rows, sine_rows)
+        .astype(jnp.bfloat16)
+        .reshape(tok_rows, query_heads * HEAD_FEATURES)
+    )
+    grad_key_pre = (
+        rotary_back(grad_key_seq, cosine_rows, sine_rows)
+        .astype(jnp.bfloat16)
+        .reshape(tok_rows, key_heads * HEAD_FEATURES)
+    )
+    grad_values_low = grad_value_seq.astype(jnp.bfloat16).reshape(
+        tok_rows, key_heads * HEAD_FEATURES
+    )
+    query_grad = jnp.dot(normalized_input.T, grad_query_pre, preferred_element_type=jnp.float32)
+    key_grad = jnp.dot(normalized_input.T, grad_key_pre, preferred_element_type=jnp.float32)
+    value_grad = jnp.dot(normalized_input.T, grad_values_low, preferred_element_type=jnp.float32)
+    normed_term = jnp.dot(grad_query_pre, query_weight.T, preferred_element_type=jnp.float32)
+    normed_term = normed_term + jnp.dot(
+        grad_key_pre, key_matrix.T, preferred_element_type=jnp.float32
+    )
+    normed_term = normed_term + jnp.dot(
+        grad_values_low, value_matrix.T, preferred_element_type=jnp.float32
+    )
+    normed_low = normed_term.astype(jnp.bfloat16)
+    grad_normed = normed_low.astype(jnp.float32) + swap_cores(normed_low).astype(jnp.float32)
+    weighted_first = grad_normed * gain_first
+    first_grad = jnp.sum(grad_normed * stream_f * inv_first, axis=0)
+    grad_stream = (
+        grad_middle_all
+        + inv_first * weighted_first
+        - stream_f * inv_first**3 * jnp.mean(stream_f * weighted_first, axis=-1, keepdims=True)
+    )
+    small = jnp.concatenate(
+        [router_grad, second_grad[:, None], 0.5 * first_grad[:, None]], axis=1
+    )
+    small = small + swap_cores(small)
+    small = jnp.pad(small, ((0, 0), (0, 128 - small.shape[1])))
+    low = [
+        value.astype(jnp.bfloat16)
+        for value in (out_grad_t, key_grad, query_grad, value_grad, small)
+    ]
+    first_part = scatter_rows(jnp.concatenate(low[:2], axis=1), 0, place)
+    second_part = scatter_rows(jnp.concatenate(low[2:], axis=1), 1, place)
+    query_width = query_weight.shape[1]
+    key_width = key_matrix.shape[1]
+    small_part = second_part[:, query_width + key_width :]
+    return (
+        layer_out,
+        grad_stream,
+        small_part[:, experts + 1],
+        second_part[:, :query_width],
+        first_part[:, query_width:],
+        second_part[:, query_width : query_width + key_width],
+        first_part[:, :query_width].T,
+        small_part[:, experts],
+        small_part[:, :experts],
+        gate_grad[None],
+        up_grad[None],
+        down_grad[None],
+        rms_stats,
+    )
+
+
 def solution(mesh):
     in_specs = (
         P("ep", None),
@@ -380,4 +687,7 @@
         P("ep", "tp", None),
         P("ep", None),
     )
+    ep_size = mesh.shape["ep"]
+    dense = mesh.shape["tp"] == 2 and ep_size <= 2 * TOP and ep_size == 16
+    shards = dense_shards if dense else routed_shards
     return jax.shard_map(shards, mesh=mesh, in_specs=in_specs, out_specs=out_specs, check_vma=False)

time: 2250 us -> 790 us (0.35)
  blocking collectives: 792 us -> 0 us
  waiting for transfers between devices: 851 us -> 333 us
  local copies, waits for them, and re-layouts: 307 us -> 102 us
  starting transfers between devices: 6.14 us -> 108 us
    all_to_all x3 -> x0, blocking collectives: 714 us -> none  [the longest x2 365 us: back_to_tokens(): lax.all_to_all(rows_low, 'ep', split_axis=1, concat_axis=1, tiled=True)]
    reduce_scatter x6 -> x0, waiting for transfers between devices: 511 us -> none  [the longest x1 143 us: shards(): lax.psum_scatter(query_grad, 'ep', scatter_dimension=0, tiled=True)]
    ppermute x0 -> x65, waiting for transfers between devices: none -> 333 us  [the longest x44 329 us: exchange(): return lax.ppermute(value, 'ep', [(i, i ^ bits) for i in range(count)])]
    all_to_all x1 -> x0, waiting for transfers between devices: 255 us -> none  [to_owners(): return lax.all_to_all(packed, 'ep', split_axis=1, concat_axis=1, tiled=True)]
    gather x5 -> x0, local copies, waits for them, and re-layouts: 164 us -> none  [the longest x1 35.8 us: shards(): grad_mix[source_token]]
    ppermute x0 -> x65, starting transfers between devices: none -> 108 us  [the longest x44 103 us: exchange(): return lax.ppermute(value, 'ep', [(i, i ^ bits) for i in range(count)])]
    unnamed x1 -> x0, blocking collectives: 77.5 us -> none
    all_to_all x4 -> x0, local copies, waits for them, and re-layouts: 68.6 us -> none  [the longest x2 47.2 us: to_owners(): return lax.all_to_all(packed, 'ep', split_axis=1, concat_axis=1, tiled=True)]
  transfers between devices with their start and end apart: 12 -> 65, of which waited for: 8 -> 23; matrix products, arithmetic and copies ran while one was open for 14% -> 30% of each run, Pallas kernels for 0% -> 0%
where the time goes in v1:
time: 790 us; the launch traced here: 781 us
  waiting for transfers between devices  333 us (42%)
  matrix products  139 us (18%)
  starting transfers between devices  108 us (14%)
  local copies, waits for them, and re-layouts  102 us (13%)
  other arithmetic  96.7 us (12%)
    ppermute x44, waiting for transfers between devices, exchange(): return lax.ppermute(value, 'ep', [(i, i ^ bits) for i in range(count)])  329 us
    ppermute x44, starting transfers between devices, exchange(): return lax.ppermute(value, 'ep', [(i, i ^ bits) for i in range(count)])  103 us
    unnamed x214, local copies, waits for them, and re-layouts  33.7 us
    another operation x8, other arithmetic  24.9 us
    dot_general x1, matrix products, dense_shards(): jnp.dot(cot_rows, down_all.T, preferred_element_type=jnp.float32)  16.1 us
  transfers between devices with their start and end apart: 65, of which 23 were waited for; matrix products, arithmetic and copies ran while one was open for 30% of the time, Pallas kernels for 0%

profile of v1, /device:TPU:0, one launch (start us, length us, event | category | flops | bytes accessed | tf_op | source)
XLA Modules:
  0.0 781.3 jit_solution(3154302211109533332)
XLA Ops:
  64.6 18.9 %collective-permute-done.8 = bf16[1536,256]{1,0:T(8,128)(2,1)S(1)} collective-permute-done((bf16[1536,256]{1,0:T(8,128)(2,1)S(1)}, bf16[1536,256]{1,0:T(8,128)(2,1)S(1)}, u32[]{:S(2)}, u32[]{:S(2)}) %collective-permute-start.8) | collective-permute-done | bytes 786464 | tf_op jit(solution)/shard_map/ppermute | solution.py:358
  87.0 9.2 %collective-permute-done.21 = bf16[256,1536]{1,0:T(8,128)(2,1)S(1)} collective-permute-done((bf16[256,1536]{1,0:T(8,128)(2,1)S(1)}, bf16[256,1536]{1,0:T(8,128)(2,1)S(1)}, u32[]{:S(2)}, u32[]{:S(2)}) %collective-permute-start.21) | collective-permute-done | bytes 786464 | tf_op jit(solution)/shard_map/ppermute | solution.py:358
  99.4 16.5 %collective-permute-done.22 = bf16[256,1536]{1,0:T(8,128)(2,1)S(1)} collective-permute-done((bf16[256,1536]{1,0:T(8,128)(2,1)S(1)}, bf16[256,1536]{1,0:T(8,128)(2,1)S(1)}, u32[]{:S(2)}, u32[]{:S(2)}) %collective-permute-start.22) | collective-permute-done | bytes 786464 | tf_op jit(solution)/shard_map/ppermute | solution.py:358
  123.1 28.4 %collective-permute-done.5 = bf16[256,1536]{1,0:T(8,128)(2,1)S(1)} collective-permute-done((bf16[256,1536]{1,0:T(8,128)(2,1)S(1)}, bf16[256,1536]{1,0:T(8,128)(2,1)S(1)}, u32[]{:S(2)}, u32[]{:S(2)}) %collective-permute-start.5) | collective-permute-done | bytes 786464 | tf_op jit(solution)/shard_map/ppermute | solution.py:358
  152.1 10.9 %fusion.82 = f32[1024,2048]{1,0:T(8,128)} fusion(bf16[1536,2048]{1,0:T(8,128)(2,1)S(1)} %constant_dynamic-update-slice_fusion.8, bf16[256,1536]{1,0:T(8,128)(2,1)S(1)} %collective-permute-done.6, bf16[256,1536]{1,0:T(8,128)(2,1)S(1)} %collective-permute-done.5, bf16[256,1536]{1,0:T(8,128)(2,1)S(1)} %collective-permute-done.4, ...), kind=kOutput, calls=%fused_computation.249 | convolution fusion | flops 6455033856 | bytes 17825792 | tf_op jit(solution)/shard_map/dot_general | solution.py:505
  163.1 16.6 %collective-permute-start.33 = (bf16[256,1536]{1,0:T(8,128)(2,1)S(1)}, bf16[256,1536]{1,0:T(8,128)(2,1)S(1)}, u32[]{:S(2)}, u32[]{:S(2)}) collective-permute-start(bf16[256,1536]{1,0:T(8,128)(2,1)S(1)} %constant_dynamic-slice_fusion), channel_id=1, source_target_pairs={{0,16},{2,18},{4,20},{6,22},{8,24},{10,26},{12,28},{14,30},{16,0},... | collective-permute-start | bytes 2359304 | tf_op jit(solution)/shard_map/ppermute | solution.py:358
  181.1 11.4 %fusion.83 = f32[1024,2048]{1,0:T(8,128)} fusion(bf16[1536,2048]{1,0:T(8,128)(2,1)S(1)} %constant_dynamic-update-slice_fusion, bf16[256,1536]{1,0:T(8,128)(2,1)S(1)} %collective-permute-done.6, bf16[256,1536]{1,0:T(8,128)(2,1)S(1)} %collective-permute-done.5, bf16[256,1536]{1,0:T(8,128)(2,1)S(1)} %collective-permute-done.4, ...), kind=kOutput, calls=%fused_computation.250 | convolution fusion | flops 6455033856 | bytes 17825792 | tf_op jit(solution)/shard_map/dot_general | solution.py:504
  195.5 36.2 %collective-permute-done.33 = bf16[256,1536]{1,0:T(8,128)(2,1)S(1)} collective-permute-done((bf16[256,1536]{1,0:T(8,128)(2,1)S(1)}, bf16[256,1536]{1,0:T(8,128)(2,1)S(1)}, u32[]{:S(2)}, u32[]{:S(2)}) %collective-permute-start.33) | collective-permute-done | bytes 786464 | tf_op jit(solution)/shard_map/ppermute | solution.py:358
  232.6 16.1 %multiply_multiply_fusion.1 = (f32[1024,2048]{1,0:T(8,128)}, f32[1024,2048]{1,0:T(8,128)}) fusion(f32[1024,2048]{1,0:T(8,128)} %fusion.82, f32[1024,2048]{1,0:T(8,128)} %fusion.83, bf16[2048,1536]{1,0:T(8,128)(2,1)} %constant_dynamic-update-slice_fusion.16, bf16[256,1536]{1,0:T(8,128)(2,1)} %collective-permute-done.34, bf16[256,1536]{1,0:T(8,128)(2,1)} %copy-done.87, ...), kind=kOutput, calls=%fused_computation.18 | convolution fusion | flops 6469713920 | bytes 42991616 | tf_op jit(solution)/shard_map/dot_general | solution.py:506
  248.7 10.8 %reshape.356 = f32[1024,2,4,256]{3,2,1,0:T(4,128)} reshape(f32[1024,2048]{1,0:T(8,128)} %get-tuple-element.199) | data formatting | bytes 16777216 | tf_op jit(solution)/shard_map/reshape | solution.py:511
  266.1 16.5 %collective-permute-start.35 = (f32[256,4]{1,0:T(8,128)S(1)}, f32[256,4]{1,0:T(8,128)S(1)}, u32[]{:S(2)}, u32[]{:S(2)}) collective-permute-start(f32[256,4]{1,0:T(8,128)S(1)} %get-tuple-element.187), channel_id=1, source_target_pairs={{0,8},{2,10},{4,12},{6,14},{8,0},{10,2},{12,4},{14,6},{16,24},{18,... | collective-permute-start | bytes 12296 | tf_op jit(solution)/shard_map/ppermute | solution.py:358
  311.3 10.8 %reshape.355 = f32[1024,2048]{1,0:T(8,128)} reshape(f32[1024,2,4,256]{3,2,1,0:T(4,128)} %broadcast_in_dim.340) | data formatting | bytes 16777216 | tf_op jit(solution)/shard_map/reshape | solution.py:502
  322.1 13.0 %multiply_convert_fusion.2 = (bf16[1024,2048]{1,0:T(8,128)(2,1)S(1)}, bf16[1024,2048]{1,0:T(8,128)(2,1)S(1)}, bf16[1024,2048]{1,0:T(8,128)(2,1)S(1)}) fusion(f32[1024,2048]{1,0:T(8,128)} %fusion.83, f32[1024,2048]{1,0:T(8,128)} %fusion.82, f32[1024,2048]{1,0:T(8,128)} %reshape.355, f32[1024,2048]{1,0:T(8,128)} %get-tuple-element.200), kind=kLoop, calls=%fused_computation.13 | loop fusion | flops 37748736 | bytes 46137344 | tf_op jit(solution)/shard_map/convert_element_type | solution.py:518
  335.0 10.5 %fusion.92 = f32[1024,1536]{1,0:T(8,128)} fusion(bf16[1024,2048]{1,0:T(8,128)(2,1)S(1)} %get-tuple-element.154, bf16[1536,2048]{1,0:T(8,128)(2,1)} %copy-done.62), kind=kOutput, calls=%fused_computation.258 | convolution fusion | flops 6442450944 | bytes 16777216 | tf_op jit(solution)/shard_map/dot_general | solution.py:525
  345.6 10.7 %add_convert_fusion = bf16[1024,1536]{1,0:T(8,128)(2,1)S(1)} fusion(f32[1024,1536]{1,0:T(8,128)} %fusion.92, bf16[1024,2048]{1,0:T(8,128)(2,1)S(1)} %get-tuple-element.153, bf16[1536,2048]{1,0:T(8,128)(2,1)} %copy-done.64), kind=kOutput, calls=%fused_computation.28 | convolution fusion | flops 6445596672 | bytes 19922944 | tf_op jit(solution)/shard_map/dot_general | solution.py:524
  383.9 11.0 %collective-permute-done.38 = bf16[256,1536]{1,0:T(8,128)(2,1)S(1)} collective-permute-done((bf16[256,1536]{1,0:T(8,128)(2,1)S(1)}, bf16[256,1536]{1,0:T(8,128)(2,1)S(1)}, u32[]{:S(2)}, u32[]{:S(2)}) %collective-permute-start.38) | collective-permute-done | bytes 786464 | tf_op jit(solution)/shard_map/ppermute | solution.py:358
  413.9 12.9 %collective-permute-done.28 = bf16[256,1536]{1,0:T(8,128)(2,1)} collective-permute-done((bf16[256,1536]{1,0:T(8,128)(2,1)}, bf16[256,1536]{1,0:T(8,128)(2,1)}, u32[]{:S(2)}, u32[]{:S(2)}) %collective-permute-start.28) | collective-permute-done | bytes 786464 | tf_op jit(solution)/shard_map/ppermute | solution.py:358
  426.8 54.1 %collective-permute-done.29 = bf16[256,1536]{1,0:T(8,128)(2,1)} collective-permute-done((bf16[256,1536]{1,0:T(8,128)(2,1)}, bf16[256,1536]{1,0:T(8,128)(2,1)}, u32[]{:S(2)}, u32[]{:S(2)}) %collective-permute-start.29) | collective-permute-done | bytes 786464 | tf_op jit(solution)/shard_map/ppermute | solution.py:358
  512.0 11.0 %fusion = (f32[4,3,512]{2,1,0:T(4,128)S(1)}, f32[4,512,512,3]{2,1,3,0:T(8,128)}) fusion(f32[4,3,512]{2,1,0:T(4,128)S(1)} %copy-done.54, f32[4,512,512,3]{2,1,3,0:T(8,128)} %copy-done.1, pred[512,512]{0,1:T(8,128)(4,1)S(1)} %copy-done.13, bf16[512,4,64,1]{0,2,3,1:T(8,128)(2,1)} %bitcast.215, bf16[512,4,3,64]{0,3,2,1:T(8,128)(2,1)S(1)} %bitcast.190), kind=kOutput, calls=%fused_computation.2 | convolution fusion | flops 418375680 | bytes 26525696 | tf_op jit(solution)/shard_map/qhgd,khd->hgqk/dot_general | solution.py:91
  639.1 45.0 %collective-permute-done.44 = bf16[2,2,2,96,1152]{4,3,2,1,0:T(8,128)(2,1)S(1)} collective-permute-done((bf16[2,2,2,96,1152]{4,3,2,1,0:T(8,128)(2,1)S(1)}, bf16[2,2,2,96,1152]{4,3,2,1,0:T(8,128)(2,1)S(1)}, u32[]{:S(2)}, u32[]{:S(2)}) %collective-permute-start.44) | collective-permute-done | bytes 1769504 | tf_op jit(solution)/shard_map/ppermute | solution.py:358
  687.2 30.6 %collective-permute-done.58 = bf16[1536,256]{1,0:T(8,128)(2,1)S(1)} collective-permute-done((bf16[1536,256]{1,0:T(8,128)(2,1)S(1)}, bf16[1536,256]{1,0:T(8,128)(2,1)S(1)}, u32[]{:S(2)}, u32[]{:S(2)}) %collective-permute-start.58) | collective-permute-done | bytes 786464 | tf_op jit(solution)/shard_map/ppermute | solution.py:358
  717.8 15.6 %collective-permute-start.50 = (bf16[2,96,1024]{2,1,0:T(8,128)(2,1)S(1)}, bf16[2,96,1024]{2,1,0:T(8,128)(2,1)S(1)}, u32[]{:S(2)}, u32[]{:S(2)}) collective-permute-start(bf16[2,96,1024]{2,1,0:T(8,128)(2,1)S(1)} %dynamic-slice_bitcast_fusion.5), channel_id=1, source_target_pairs={{0,16},{2,18},{4,20},{6,22},{8,24},{10,26},{12,28},{14,30},{16,0},... | collective-permute-start | bytes 1179656 | tf_op jit(solution)/shard_map/ppermute | solution.py:358
  737.3 11.4 %collective-permute-done.50 = bf16[2,96,1024]{2,1,0:T(8,128)(2,1)S(1)} collective-permute-done((bf16[2,96,1024]{2,1,0:T(8,128)(2,1)S(1)}, bf16[2,96,1024]{2,1,0:T(8,128)(2,1)S(1)}, u32[]{:S(2)}, u32[]{:S(2)}) %collective-permute-start.50) | collective-permute-done | bytes 393248 | tf_op jit(solution)/shard_map/ppermute | solution.py:358
  756.9 14.9 %collective-permute-done.46 = bf16[2,96,1152]{2,1,0:T(8,128)(2,1)S(1)} collective-permute-done((bf16[2,96,1152]{2,1,0:T(8,128)(2,1)S(1)}, bf16[2,96,1152]{2,1,0:T(8,128)(2,1)S(1)}, u32[]{:S(2)}, u32[]{:S(2)}) %collective-permute-start.46) | collective-permute-done | bytes 442400 | tf_op jit(solution)/shard_map/ppermute | solution.py:358
  (459 shorter events, 335.5 us)
Async XLA Ops:
  62.5 53.4 %collective-permute-start.22 = (bf16[256,1536]{1,0:T(8,128)(2,1)S(1)}, bf16[256,1536]{1,0:T(8,128)(2,1)S(1)}, u32[]{:S(2)}, u32[]{:S(2)}) collective-permute-start(bf16[256,1536]{1,0:T(8,128)(2,1)S(1)} %bitcast.210), channel_id=1, source_target_pairs={{0,4},{2,6},{4,0},{6,2},{8,12},{10,14},{12,8},{14,10},{16,20},{18,... | collective-permute-start | bytes 2359304 | tf_op jit(solution)/shard_map/ppermute | solution.py:358
  96.3 55.3 %collective-permute-start.5 = (bf16[256,1536]{1,0:T(8,128)(2,1)S(1)}, bf16[256,1536]{1,0:T(8,128)(2,1)S(1)}, u32[]{:S(2)}, u32[]{:S(2)}) collective-permute-start(bf16[256,1536]{1,0:T(8,128)(2,1)S(1)} %multiply_convert_fusion.4), channel_id=1, source_target_pairs={{0,16},{2,18},{4,20},{6,22},{8,24},{10,26},{12,28},{14,30},{16,0},... | collective-permute-start | bytes 2359304 | tf_op jit(solution)/shard_map/ppermute | solution.py:358
  122.2 73.3 %collective-permute-start.32 = (bf16[256,1536]{1,0:T(8,128)(2,1)S(1)}, bf16[256,1536]{1,0:T(8,128)(2,1)S(1)}, u32[]{:S(2)}, u32[]{:S(2)}) collective-permute-start(bf16[256,1536]{1,0:T(8,128)(2,1)S(1)} %constant_dynamic-slice_fusion), channel_id=1, source_target_pairs={{0,8},{2,10},{4,12},{6,14},{8,0},{10,2},{12,4},{14,6},{16,24},{18,... | collective-permute-start | bytes 2359304 | tf_op jit(solution)/shard_map/ppermute | solution.py:358
  122.6 57.2 %collective-permute-start.12 = (bf16[1536,256]{1,0:T(8,128)(2,1)S(1)}, bf16[1536,256]{1,0:T(8,128)(2,1)S(1)}, u32[]{:S(2)}, u32[]{:S(2)}) collective-permute-start(bf16[1536,256]{1,0:T(8,128)(2,1)S(1)} %collective-permute-done.8), channel_id=1, source_target_pairs={{0,1},{1,0},{2,3},{3,2},{4,5},{5,4},{6,7},{7,6},{8,9},{9,8},{10,11... | collective-permute-start | bytes 2359304 | tf_op jit(solution)/shard_map/ppermute | solution.py:353
  163.1 68.6 %collective-permute-start.33 = (bf16[256,1536]{1,0:T(8,128)(2,1)S(1)}, bf16[256,1536]{1,0:T(8,128)(2,1)S(1)}, u32[]{:S(2)}, u32[]{:S(2)}) collective-permute-start(bf16[256,1536]{1,0:T(8,128)(2,1)S(1)} %constant_dynamic-slice_fusion), channel_id=1, source_target_pairs={{0,16},{2,18},{4,20},{6,22},{8,24},{10,26},{12,28},{14,30},{16,0},... | collective-permute-start | bytes 2359304 | tf_op jit(solution)/shard_map/ppermute | solution.py:358
  179.8 52.8 %collective-permute-start.34 = (bf16[256,1536]{1,0:T(8,128)(2,1)S(1)}, bf16[256,1536]{1,0:T(8,128)(2,1)}, u32[]{:S(2)}, u32[]{:S(2)}) collective-permute-start(bf16[256,1536]{1,0:T(8,128)(2,1)S(1)} %constant_dynamic-slice_fusion), channel_id=1, source_target_pairs={{0,24},{2,26},{4,28},{6,30},{8,16},{10,18},{12,20},{14,22},{16,8},... | collective-permute-start | bytes 2359304 | tf_op jit(solution)/shard_map/ppermute | solution.py:358
  358.1 55.3 %collective-permute-start.39 = (bf16[256,1536]{1,0:T(8,128)(2,1)}, bf16[256,1536]{1,0:T(8,128)(2,1)S(1)}, u32[]{:S(2)}, u32[]{:S(2)}) collective-permute-start(bf16[256,1536]{1,0:T(8,128)(2,1)} %get-tuple-element.174), channel_id=1, source_target_pairs={{0,16},{2,18},{4,20},{6,22},{8,24},{10,26},{12,28},{14,30},{16,0},... | collective-permute-start | bytes 2359304 | tf_op jit(solution)/shard_map/ppermute | solution.py:358
  360.7 52.7 %collective-permute-start.40 = (bf16[256,1536]{1,0:T(8,128)(2,1)}, bf16[256,1536]{1,0:T(8,128)(2,1)S(1)}, u32[]{:S(2)}, u32[]{:S(2)}) collective-permute-start(bf16[256,1536]{1,0:T(8,128)(2,1)} %get-tuple-element.173), channel_id=1, source_target_pairs={{0,24},{2,26},{4,28},{6,30},{8,16},{10,18},{12,20},{14,22},{16,8},... | collective-permute-start | bytes 2359304 | tf_op jit(solution)/shard_map/ppermute | solution.py:358
  372.3 54.5 %collective-permute-start.28 = (bf16[256,1536]{1,0:T(8,128)(2,1)}, bf16[256,1536]{1,0:T(8,128)(2,1)}, u32[]{:S(2)}, u32[]{:S(2)}) collective-permute-start(bf16[256,1536]{1,0:T(8,128)(2,1)} %get-tuple-element.175), channel_id=1, source_target_pairs={{0,8},{2,10},{4,12},{6,14},{8,0},{10,2},{12,4},{14,6},{16,24},{18,... | collective-permute-start | bytes 2359304 | tf_op jit(solution)/shard_map/ppermute | solution.py:358
  373.3 107.6 %collective-permute-start.29 = (bf16[256,1536]{1,0:T(8,128)(2,1)}, bf16[256,1536]{1,0:T(8,128)(2,1)}, u32[]{:S(2)}, u32[]{:S(2)}) collective-permute-start(bf16[256,1536]{1,0:T(8,128)(2,1)} %get-tuple-element.177), channel_id=1, source_target_pairs={{0,16},{2,18},{4,20},{6,22},{8,24},{10,26},{12,28},{14,30},{16,0},... | collective-permute-start | bytes 2359304 | tf_op jit(solution)/shard_map/ppermute | solution.py:358
  394.9 86.1 %collective-permute-start.30 = (bf16[256,1536]{1,0:T(8,128)(2,1)}, bf16[256,1536]{1,0:T(8,128)(2,1)}, u32[]{:S(2)}, u32[]{:S(2)}) collective-permute-start(bf16[256,1536]{1,0:T(8,128)(2,1)} %get-tuple-element.176), channel_id=1, source_target_pairs={{0,24},{2,26},{4,28},{6,30},{8,16},{10,18},{12,20},{14,22},{16,8},... | collective-permute-start | bytes 2359304 | tf_op jit(solution)/shard_map/ppermute | solution.py:358
  413.4 152.4 %collective-permute-start.60 = (bf16[1024,1536]{1,0:T(8,128)(2,1)}, bf16[1024,1536]{1,0:T(8,128)(2,1)}, u32[]{:S(2)}, u32[]{:S(2)}) collective-permute-start(bf16[1024,1536]{1,0:T(8,128)(2,1)} %split.94), channel_id=1, source_target_pairs={{0,1},{1,0},{2,3},{3,2},{4,5},{5,4},{6,7},{7,6},{8,9},{9,8},{10,11... | collective-permute-start | bytes 9437192 | tf_op jit(solution)/shard_map/ppermute | solution.py:353
  413.4 178.3 %collective-permute-start.56 = (bf16[1536,1024]{1,0:T(8,128)(2,1)}, bf16[1536,1024]{1,0:T(8,128)(2,1)}, u32[]{:S(2)}, u32[]{:S(2)}) collective-permute-start(bf16[1536,1024]{1,0:T(8,128)(2,1)} %split.88), channel_id=1, source_target_pairs={{0,1},{1,0},{2,3},{3,2},{4,5},{5,4},{6,7},{7,6},{8,9},{9,8},{10,11... | collective-permute-start | bytes 9437192 | tf_op jit(solution)/shard_map/ppermute | solution.py:353
  498.9 100.6 %collective-permute-start.52 = (bf16[1536,1024]{1,0:T(8,128)(2,1)}, bf16[1536,1024]{1,0:T(8,128)(2,1)}, u32[]{:S(2)}, u32[]{:S(2)}) collective-permute-start(bf16[1536,1024]{1,0:T(8,128)(2,1)} %split.82), channel_id=1, source_target_pairs={{0,1},{1,0},{2,3},{3,2},{4,5},{5,4},{6,7},{7,6},{8,9},{9,8},{10,11... | collective-permute-start | bytes 9437192 | tf_op jit(solution)/shard_map/ppermute | solution.py:353
  504.6 57.6 %collective-permute-start.31 = (bf16[256,1536]{1,0:T(8,128)(2,1)}, bf16[256,1536]{1,0:T(8,128)(2,1)}, u32[]{:S(2)}, u32[]{:S(2)}) collective-permute-start(bf16[256,1536]{1,0:T(8,128)(2,1)} %get-tuple-element.162), channel_id=1, source_target_pairs={{0,1},{1,0},{2,3},{3,2},{4,5},{5,4},{6,7},{7,6},{8,9},{9,8},{10,11... | collective-permute-start | bytes 2359304 | tf_op jit(solution)/shard_map/ppermute | solution.py:353
  574.0 57.9 %collective-permute-start.61 = (bf16[256,1536]{1,0:T(8,128)(2,1)}, bf16[256,1536]{1,0:T(8,128)(2,1)}, u32[]{:S(2)}, u32[]{:S(2)}) collective-permute-start(bf16[256,1536]{1,0:T(8,128)(2,1)} %get-tuple-element.163), channel_id=1, source_target_pairs={{0,2},{2,0},{4,6},{6,4},{8,10},{10,8},{12,14},{14,12},{16,18},{18,... | collective-permute-start | bytes 2359304 | tf_op jit(solution)/shard_map/ppermute | solution.py:358
  574.5 59.0 %collective-permute-start.62 = (bf16[256,1536]{1,0:T(8,128)(2,1)}, bf16[256,1536]{1,0:T(8,128)(2,1)}, u32[]{:S(2)}, u32[]{:S(2)}) collective-permute-start(bf16[256,1536]{1,0:T(8,128)(2,1)} %get-tuple-element.165), channel_id=1, source_target_pairs={{0,4},{2,6},{4,0},{6,2},{8,12},{10,14},{12,8},{14,10},{16,20},{18,... | collective-permute-start | bytes 2359304 | tf_op jit(solution)/shard_map/ppermute | solution.py:358
  621.9 62.2 %collective-permute-start.44 = (bf16[2,2,2,96,1152]{4,3,2,1,0:T(8,128)(2,1)S(1)}, bf16[2,2,2,96,1152]{4,3,2,1,0:T(8,128)(2,1)S(1)}, u32[]{:S(2)}, u32[]{:S(2)}) collective-permute-start(bf16[2,2,2,96,1152]{4,3,2,1,0:T(8,128)(2,1)S(1)} %dynamic-slice_bitcast_fusion), channel_id=1, source_target_pairs={{0,4},{2,6},{4,0},{6,2},{8,12},{10,14},{12,8},{14,10},{16,20},{18,... | collective-permute-start | bytes 5308424 | tf_op jit(solution)/shard_map/ppermute | solution.py:358
  629.5 56.2 %collective-permute-start.57 = (bf16[1536,256]{1,0:T(8,128)(2,1)S(1)}, bf16[1536,256]{1,0:T(8,128)(2,1)S(1)}, u32[]{:S(2)}, u32[]{:S(2)}) collective-permute-start(bf16[1536,256]{1,0:T(8,128)(2,1)S(1)} %get-tuple-element.166), channel_id=1, source_target_pairs={{0,2},{2,0},{4,6},{6,4},{8,10},{10,8},{12,14},{14,12},{16,18},{18,... | collective-permute-start | bytes 2359304 | tf_op jit(solution)/shard_map/ppermute | solution.py:358
  631.9 85.9 %collective-permute-start.58 = (bf16[1536,256]{1,0:T(8,128)(2,1)S(1)}, bf16[1536,256]{1,0:T(8,128)(2,1)S(1)}, u32[]{:S(2)}, u32[]{:S(2)}) collective-permute-start(bf16[1536,256]{1,0:T(8,128)(2,1)S(1)} %get-tuple-element.168), channel_id=1, source_target_pairs={{0,4},{2,6},{4,0},{6,2},{8,12},{10,14},{12,8},{14,10},{16,20},{18,... | collective-permute-start | bytes 2359304 | tf_op jit(solution)/shard_map/ppermute | solution.py:358
  633.5 99.9 %collective-permute-start.59 = (bf16[1536,256]{1,0:T(8,128)(2,1)S(1)}, bf16[1536,256]{1,0:T(8,128)(2,1)S(1)}, u32[]{:S(2)}, u32[]{:S(2)}) collective-permute-start(bf16[1536,256]{1,0:T(8,128)(2,1)S(1)} %get-tuple-element.167), channel_id=1, source_target_pairs={{0,6},{2,4},{4,2},{6,0},{8,14},{10,12},{12,10},{14,8},{16,22},{18,... | collective-permute-start | bytes 2359304 | tf_op jit(solution)/shard_map/ppermute | solution.py:358
  634.5 118.7 %collective-permute-start.53 = (bf16[1536,256]{1,0:T(8,128)(2,1)S(1)}, bf16[1536,256]{1,0:T(8,128)(2,1)S(1)}, u32[]{:S(2)}, u32[]{:S(2)}) collective-permute-start(bf16[1536,256]{1,0:T(8,128)(2,1)S(1)} %get-tuple-element.169), channel_id=1, source_target_pairs={{0,2},{2,0},{4,6},{6,4},{8,10},{10,8},{12,14},{14,12},{16,18},{18,... | collective-permute-start | bytes 2359304 | tf_op jit(solution)/shard_map/ppermute | solution.py:358
  684.1 69.1 %collective-permute-start.54 = (bf16[1536,256]{1,0:T(8,128)(2,1)S(1)}, bf16[1536,256]{1,0:T(8,128)(2,1)S(1)}, u32[]{:S(2)}, u32[]{:S(2)}) collective-permute-start(bf16[1536,256]{1,0:T(8,128)(2,1)S(1)} %get-tuple-element.171), channel_id=1, source_target_pairs={{0,4},{2,6},{4,0},{6,2},{8,12},{10,14},{12,8},{14,10},{16,20},{18,... | collective-permute-start | bytes 2359304 | tf_op jit(solution)/shard_map/ppermute | solution.py:358
  685.7 67.5 %collective-permute-start.55 = (bf16[1536,256]{1,0:T(8,128)(2,1)S(1)}, bf16[1536,256]{1,0:T(8,128)(2,1)S(1)}, u32[]{:S(2)}, u32[]{:S(2)}) collective-permute-start(bf16[1536,256]{1,0:T(8,128)(2,1)S(1)} %get-tuple-element.170), channel_id=1, source_target_pairs={{0,6},{2,4},{4,2},{6,0},{8,14},{10,12},{12,10},{14,8},{16,22},{18,... | collective-permute-start | bytes 2359304 | tf_op jit(solution)/shard_map/ppermute | solution.py:358
  (137 other events, 2432.2 us)

commit v2 on v1

--- a/solution.py
+++ b/solution.py
@@ -1,6 +1,10 @@
+import functools
+
 import jax
 import jax.numpy as jnp
 from jax import lax
+from jax.experimental import pallas as pl
+from jax.experimental.pallas import tpu as pltpu
 from jax.sharding import PartitionSpec as P
 
 HEAD_FEATURES = 64
@@ -358,30 +362,438 @@
     return lax.ppermute(value, "ep", [(i, i ^ bits) for i in range(count)])
 
 
-def keep_and_send(value, axis, bit):
-    kept = lax.dynamic_index_in_dim(value, bit, axis, keepdims=False)
-    sent = lax.dynamic_index_in_dim(value, 1 - bit, axis, keepdims=False)
-    return kept, sent
-
-
-def scatter_stage(value, axis, bits, bit):
-    kept, sent = keep_and_send(value, axis, bit)
-    arrived = exchange(sent, bits)
-    return (kept.astype(jnp.float32) + arrived.astype(jnp.float32)).astype(jnp.bfloat16)
-
-
-def scatter_rows(value, first_bit, place):
-    rows = value.shape[0]
-    count = lax.axis_size("ep")
-    bit_count = count.bit_length() - 1
-    value = value.reshape((2,) * bit_count + (rows // count, value.shape[1]))
-    order = [first_bit, 1 - first_bit] + list(range(bit_count - 1, 1, -1))
-    left = list(range(bit_count - 1, -1, -1))
-    for bit in order:
-        axis = left.index(bit)
-        value = scatter_stage(value, axis, 1 << bit, (place >> bit) & 1)
-        left.remove(bit)
-    return value.astype(jnp.float32)
+MESH = pl.DeviceIdType.MESH
+PLANE = 4
+LINES = 4
+
+
+def flip(place, unit):
+    return place + unit * (1 - 2 * lax.rem(lax.div(place, unit), 2))
+
+
+def flip_line(place, step):
+    if step % 2:
+        place = flip(place, PLANE)
+    if step // 2:
+        place = flip(place, 2 * PLANE)
+    return place
+
+
+def matmul(left, right):
+    return jnp.dot(left, right, preferred_element_type=jnp.float32)
+
+
+def matmul_nt(left, right):
+    return lax.dot_general(
+        left, right, (((1,), (1,)), ((), ())), preferred_element_type=jnp.float32
+    )
+
+
+def matmul_tn(left, right):
+    return lax.dot_general(
+        left, right, (((0,), (0,)), ((), ())), preferred_element_type=jnp.float32
+    )
+
+
+def expert_kernel(*refs):
+    tiles = 2 * PLANE
+    refs = list(refs)
+
+    def take(count):
+        taken = refs[:count]
+        del refs[:count]
+        return taken
+
+    mixer_parts, cot_parts, prob_parts = take(LINES), take(LINES), take(LINES)
+    gate_parts, up_parts, down_parts = take(tiles), take(tiles), take(tiles)
+    out_parts = take(LINES)
+    grow_sum, weighting_sum, gate_out, up_out, down_out = take(5)
+    mixer, cots, probs, gates, ups, downs = take(6)
+    scaled, ggate, gup, grow, grow_in, outs, weighting, weighting_in = take(8)
+    load_sem, tile_sem, store_sem, tile_out_sem = take(4)
+    grow_send, grow_recv, weighting_send, weighting_recv = take(4)
+    half, width = mixer_parts[0].shape
+    rows = LINES * half
+    span = gates.shape[2]
+    column_tiles = width // span
+
+    place = lax.axis_index("ep")
+    core = lax.axis_index("tp")
+    partners = [flip_line(place, step) for step in range(LINES)]
+    barrier = pltpu.get_barrier_semaphore()
+    for step in range(1, LINES):
+        pl.semaphore_signal(
+            barrier, inc=1, device_id=(partners[step], core), device_id_type=MESH
+        )
+
+    loads = []
+    for step in range(LINES):
+        part = pl.ds(step * half, half)
+        for kind, (source, target) in enumerate(
+            ((mixer_parts, mixer), (cot_parts, cots), (prob_parts, probs))
+        ):
+            loads.append(
+                pltpu.make_async_copy(source[step], target.at[part], load_sem.at[kind, step])
+            )
+    for copy in loads:
+        copy.start()
+    for tile in range(tiles):
+        for kind, (source, target) in enumerate(
+            ((gate_parts, gates), (up_parts, ups), (down_parts, downs))
+        ):
+            pltpu.make_async_copy(source[tile], target.at[tile], tile_sem.at[kind, tile]).start()
+    pl.semaphore_wait(barrier, LINES - 1)
+    for copy in loads:
+        copy.wait()
+    weighting[...] = jnp.zeros_like(weighting)
+    line_place = lax.div(place, PLANE)
+    lanes = lax.broadcasted_iota(jnp.int32, (rows, 128), 1)
+
+    def hidden_tile(tile, carry):
+        for kind, (source, target) in enumerate(
+            ((gate_parts, gates), (up_parts, ups), (down_parts, downs))
+        ):
+            pltpu.make_async_copy(source[0], target.at[tile], tile_sem.at[kind, tile]).wait()
+        step = lax.rem(tile, PLANE)
+        owner = lax.rem(place, PLANE)
+        owner = jnp.where(lax.rem(step, 2) == 1, flip(owner, 1), owner)
+        owner = jnp.where(lax.div(step, 2) == 1, flip(owner, 2), owner)
+        chosen = lanes == line_place * PLANE + owner
+        prob = jnp.sum(jnp.where(chosen, probs[...], 0.0), axis=1, keepdims=True)
+        gate_pre = matmul(mixer[...], gates[tile])
+        up_pre = matmul(mixer[...], ups[tile])
+        grad_raw = residual_scale * matmul_nt(cots[...], downs[tile])
+        sigmoid_gate = 1.0 / (1.0 + jnp.exp(-gate_pre))
+        silu_gate = gate_pre * sigmoid_gate
+        active = silu_gate * up_pre
+        share = jnp.sum(active * grad_raw, axis=1, keepdims=True)
+        weighting[...] += jnp.where(chosen, share, 0.0)
+        grad_active = prob * grad_raw
+        scaled[tile] = (prob * active).astype(jnp.bfloat16)
+        ggate[tile] = (
+            grad_active * up_pre * sigmoid_gate * (1.0 + gate_pre * (1.0 - sigmoid_gate))
+        ).astype(jnp.bfloat16)
+        gup[tile] = (grad_active * silu_gate).astype(jnp.bfloat16)
+        return carry
+
+    lax.fori_loop(0, tiles, hidden_tile, 0)
+
+    def weighting_copy(step):
+        return pltpu.make_async_remote_copy(
+            src_ref=weighting.at[pl.ds(step * half, half)],
+            dst_ref=weighting_in.at[step - 1],
+            send_sem=weighting_send.at[step - 1],
+            recv_sem=weighting_recv.at[step - 1],
+            device_id=(partners[step], core),
+            device_id_type=MESH,
+        )
+
+    def grow_copy(step, column):
+        return pltpu.make_async_remote_copy(
+            src_ref=grow.at[column, pl.ds(step * half, half)],
+            dst_ref=grow_in.at[step - 1, column],
+            send_sem=grow_send.at[step - 1, column],
+            recv_sem=grow_recv.at[step - 1, column],
+            device_id=(partners[step], core),
+            device_id_type=MESH,
+        )
+
+    for step in range(1, LINES):
+        weighting_copy(step).start()
+
+    def grow_tile(column, carry):
+        here = pl.ds(pl.multiple_of(column * span, span), span)
+        total = matmul_nt(ggate[0], gates[0, here, :])
+        for tile in range(1, tiles):
+            total = total + matmul_nt(ggate[tile], gates[tile, here, :])
+        for tile in range(tiles):
+            total = total + matmul_nt(gup[tile], ups[tile, here, :])
+        grow[column] = total.astype(jnp.bfloat16)
+        for step in range(1, LINES):
+            grow_copy(step, column).start()
+        return carry
+
+    lax.fori_loop(0, column_tiles, grow_tile, 0)
+
+    def out_tile(column, carry):
+        here = pl.ds(pl.multiple_of(column * span, span), span)
+        total = matmul(scaled[0], downs[0, :, here])
+        for tile in range(1, tiles):
+            total = total + matmul(scaled[tile], downs[tile, :, here])
+        outs[:, here] = total.astype(jnp.bfloat16)
+        return carry
+
+    lax.fori_loop(0, column_tiles, out_tile, 0)
+    stores = [
+        pltpu.make_async_copy(
+            outs.at[pl.ds(step * half, half)], out_parts[step], store_sem.at[step]
+        )
+        for step in range(LINES)
+    ]
+    for copy in stores:
+        copy.start()
+
+    def tile_copies(tile):
+        return [
+            pltpu.make_async_copy(source.at[tile], target.at[tile], tile_out_sem.at[kind, tile])
+            for kind, (source, target) in enumerate(
+                ((gates, gate_out), (ups, up_out), (downs, down_out))
+            )
+        ]
+
+    def weight_tile(tile, carry):
+        gates[tile] = matmul_tn(mixer[...], ggate[tile]).astype(jnp.bfloat16)
+        ups[tile] = matmul_tn(mixer[...], gup[tile]).astype(jnp.bfloat16)
+        downs[tile] = (residual_scale * matmul_tn(scaled[tile], cots[...])).astype(jnp.bfloat16)
+        for copy in tile_copies(tile):
+            copy.start()
+        return carry
+
+    lax.fori_loop(0, tiles, weight_tile, 0)
+    for step in range(1, LINES):
+        weighting_copy(step).wait()
+    total = weighting[pl.ds(0, half), :]
+    for step in range(1, LINES):
+        total = total + weighting_in[step - 1]
+    weighting_sum[...] = total
+    for column in range(column_tiles):
+        here = pl.ds(column * span, span)
+        for step in range(1, LINES):
+            grow_copy(step, column).wait()
+        total = grow[column, pl.ds(0, half), :].astype(jnp.float32)
+        for step in range(1, LINES):
+            total = total + grow_in[step - 1, column].astype(jnp.float32)
+        grow_sum[:, here] = total
+    for copy in stores:
+        copy.wait()
+
+    def drain(tile, carry):
+        for copy in tile_copies(tile):
+            copy.wait()
+        return carry
+
+    lax.fori_loop(0, tiles, drain, 0)
+
+
+def run_experts(mixer_parts, cot_parts, prob_parts, gate_parts, up_parts, down_parts):
+    tiles = 2 * PLANE
+    half, width = mixer_parts[0].shape
+    span = gate_parts[0].shape[1]
+    rows = LINES * half
+    low, wide = jnp.bfloat16, jnp.float32
+    shape = jax.ShapeDtypeStruct
+    far = pl.BlockSpec(memory_space=pl.ANY)
+    near = pl.BlockSpec(memory_space=pltpu.VMEM)
+    operands = [*mixer_parts, *cot_parts, *prob_parts, *gate_parts, *up_parts, *down_parts]
+    dma = pltpu.SemaphoreType.DMA
+    flops = 18 * rows * width * span * tiles
+    results = pl.pallas_call(
+        expert_kernel,
+        name="experts",
+        out_shape=(
+            *[shape((half, width), low)] * LINES,
+            shape((half, width), wide),
+            shape((half, 128), wide),
+            shape((tiles, width, span), low),
+            shape((tiles, width, span), low),
+            shape((tiles, span, width), low),
+        ),
+        in_specs=[far] * len(operands),
+        out_specs=(*[far] * LINES, near, near, far, far, far),
+        scratch_shapes=[
+            pltpu.VMEM((rows, width), low),
+            pltpu.VMEM((rows, width), low),
+            pltpu.VMEM((rows, 128), wide),
+            pltpu.VMEM((tiles, width, span), low),
+            pltpu.VMEM((tiles, width, span), low),
+            pltpu.VMEM((tiles, span, width), low),
+            pltpu.VMEM((tiles, rows, span), low),
+            pltpu.VMEM((tiles, rows, span), low),
+            pltpu.VMEM((tiles, rows, span), low),
+            pltpu.VMEM((width // span, rows, span), low),
+            pltpu.VMEM((LINES - 1, width // span, half, span), low),
+            pltpu.VMEM((rows, width), low),
+            pltpu.VMEM((rows, 128), wide),
+            pltpu.VMEM((LINES - 1, half, 128), wide),
+            dma((3, LINES)),
+            dma((3, tiles)),
+            dma((LINES,)),
+            dma((3, tiles)),
+            dma((LINES - 1, width // span)),
+            dma((LINES - 1, width // span)),
+            dma((LINES - 1,)),
+            dma((LINES - 1,)),
+        ],
+        compiler_params=pltpu.CompilerParams(
+            collective_id=0, has_side_effects=True, vmem_limit_bytes=63 << 20
+        ),
+        cost_estimate=pl.CostEstimate(
+            flops=flops, bytes_accessed=12 * width * span * tiles, transcendentals=0
+        ),
+    )(*operands)
+    return results[:LINES], *results[LINES:]
+
+
+def scatter_kernel(widths, *refs):
+    count = len(widths)
+    sources, results = refs[:count], refs[count : 2 * count]
+    scratch = refs[2 * count :]
+    per = 7
+    place = lax.axis_index("ep")
+    core = lax.axis_index("tp")
+    line_place = lax.div(place, PLANE)
+    slab = results[0].shape[0]
+    bits = [lax.rem(place, 2), lax.rem(lax.div(place, 2), 2)]
+    neighbours = [flip(place, 1), flip(place, 2)]
+    partners = [flip_line(place, step) for step in range(LINES)]
+
+    barrier = pltpu.get_barrier_semaphore()
+    for other in neighbours + partners[1:]:
+        pl.semaphore_signal(barrier, inc=1, device_id=(other, core), device_id_type=MESH)
+
+    order = [3, 2, 1, 0]
+
+    def rows_of(step, first, second_same, first_same):
+        line = lax.div(partners[step], PLANE)
+        second = 1 - first
+        first_bit = bits[first] if first_same else 1 - bits[first]
+        second_bit = bits[second] if second_same else 1 - bits[second]
+        index = line * PLANE + first_bit * (1 << first) + second_bit * (1 << second)
+        return pl.ds(pl.multiple_of(index * slab, slab), slab)
+
+    def remote(source, target, sems, index, other):
+        return pltpu.make_async_remote_copy(
+            src_ref=source,
+            dst_ref=target,
+            send_sem=sems[0].at[index],
+            recv_sem=sems[1].at[index],
+            device_id=(other, core),
+            device_id_type=MESH,
+        )
+
+    plans = []
+    for number in range(count):
+        own, first_in, second_out, second_in, line_out, line_in, sems = scratch[
+            per * number : per * number + per
+        ]
+        plans.append((sources[number], own, first_in, second_out, second_in, line_out, line_in, sems))
+
+    def first_copy(number, step, same):
+        source, own, first_in, _, _, _, _, sems = plans[number]
+        first = number % 2
+        index = step * 2 + same
+        return remote(
+            source.at[rows_of(step, first, same, False)],
+            first_in.at[index],
+            (sems.at[0], sems.at[1]),
+            index,
+            neighbours[first],
+        )
+
+    def own_copy(number, step, same):
+        source, own, _, _, _, _, _, sems = plans[number]
+        index = step * 2 + same
+        return pltpu.make_async_copy(
+            source.at[rows_of(step, number % 2, same, True)], own.at[index], sems.at[2, index]
+        )
+
+    def second_copy(number, step):
+        _, _, _, second_out, second_in, _, _, sems = plans[number]
+        return remote(
+            second_out.at[step],
+            second_in.at[step],
+            (sems.at[3], sems.at[4]),
+            step,
+            neighbours[1 - number % 2],
+        )
+
+    def line_copy(number, step):
+        _, _, _, _, _, line_out, line_in, sems = plans[number]
+        return remote(
+            line_out.at[step],
+            line_in.at[step],
+            (sems.at[5], sems.at[6]),
+            step,
+            partners[step],
+        )
+
+    for step in order:
+        for same in (0, 1):
+            for number in range(count):
+                own_copy(number, step, same).start()
+    pl.semaphore_wait(barrier, 2 + LINES - 1)
+    for step in order:
+        for same in (0, 1):
+            for number in range(count):
+                first_copy(number, step, same).start()
+
+    def add_first(number, step, same):
+        _, own, first_in, _, _, _, _, _ = plans[number]
+        own_copy(number, step, same).wait()
+        first_copy(number, step, same).wait()
+        index = step * 2 + same
+        return own[index].astype(jnp.float32) + first_in[index].astype(jnp.float32)
+
+    def finish_first(step):
+        for number in range(count):
+            second_out = plans[number][3]
+            second_out[step] = add_first(number, step, 0).astype(jnp.bfloat16)
+            second_copy(number, step).start()
+
+    def finish_second(step):
+        for number in range(count):
+            _, own, _, _, second_in, line_out, _, _ = plans[number]
+            total = add_first(number, step, 1)
+            second_copy(number, step).wait()
+            total = total + second_in[step].astype(jnp.float32)
+            if step:
+                line_out[step] = total.astype(jnp.bfloat16)
+                line_copy(number, step).start()
+            else:
+                results[number][...] = total
+
+    for position, step in enumerate(order):
+        finish_first(step)
+        if position:
+            finish_second(order[position - 1])
+    finish_second(order[-1])
+    for step in order[:-1]:
+        for number in range(count):
+            line_copy(number, step).wait()
+            results[number][...] += plans[number][6][step].astype(jnp.float32)
+
+
+def run_scatter(values, collective_id):
+    rows = values[0].shape[0]
+    slab = rows // (PLANE * LINES)
+    low = jnp.bfloat16
+    scratch = []
+    for value in values:
+        width = value.shape[1]
+        scratch += [
+            pltpu.VMEM((2 * LINES, slab, width), low),
+            pltpu.VMEM((2 * LINES, slab, width), low),
+            pltpu.VMEM((LINES, slab, width), low),
+            pltpu.VMEM((LINES, slab, width), low),
+            pltpu.VMEM((LINES, slab, width), low),
+            pltpu.VMEM((LINES, slab, width), low),
+            pltpu.SemaphoreType.DMA((7, 2 * LINES)),
+        ]
+    far = pl.BlockSpec(memory_space=pl.ANY)
+    near = pl.BlockSpec(memory_space=pltpu.VMEM)
+    return pl.pallas_call(
+        functools.partial(scatter_kernel, [value.shape[1] for value in values]),
+        name="scatter",
+        out_shape=tuple(
+            jax.ShapeDtypeStruct((slab, value.shape[1]), jnp.float32) for value in values
+        ),
+        in_specs=[far] * len(values),
+        out_specs=(near,) * len(values),
+        scratch_shapes=scratch,
+        compiler_params=pltpu.CompilerParams(
+            collective_id=collective_id, has_side_effects=True, vmem_limit_bytes=60 << 20
+        ),
+    )(*values)
 
 
 def dense_shards(
@@ -401,10 +813,7 @@
 ):
     tok_rows, model_width = stream.shape
     experts = router_weight.shape[1]
-    plane = 4
-    lines = experts // plane
-    hidden_half = gate_weight.shape[2]
-    hidden = 2 * hidden_half * plane
+    plane, lines = PLANE, LINES
     half = tok_rows // 2
     query_heads = query_weight.shape[1] // HEAD_FEATURES
     key_heads = key_matrix.shape[1] // HEAD_FEATURES
@@ -431,14 +840,14 @@
         near = [weight] + [exchange(weight, d) for d in range(1, plane)]
         return near + [swap_cores(part) for part in near]
 
-    gate_all = jnp.concatenate(plane_parts(gate_weight[0]), axis=1)
-    up_all = jnp.concatenate(plane_parts(up_weight[0]), axis=1)
-    down_all = jnp.concatenate(plane_parts(down_weight[0]), axis=0)
+    gate_parts = plane_parts(gate_weight[0])
+    up_parts = plane_parts(up_weight[0])
+    down_parts = plane_parts(down_weight[0])
 
     def line_parts(value):
         return [value] + [exchange(value, d * plane) for d in range(1, lines)]
 
-    cot_rows = jnp.concatenate(line_parts(own_half(cotangent)), axis=0)
+    cot_parts = line_parts(own_half(cotangent))
 
     stream_f = stream.astype(jnp.float32)
     gain_first = attention_gain.astype(jnp.float32)
@@ -481,84 +890,26 @@
     gate_exp = jnp.where(routed, jnp.exp(jnp.minimum(logits - largest, 0.0)), 0.0)
     gate_probs = gate_exp / jnp.sum(gate_exp, axis=-1, keepdims=True)
 
-    mixer_rows = jnp.concatenate(line_parts(mixer_in), axis=0)
-    prob_rows = jnp.concatenate(line_parts(gate_probs), axis=0)
-
-    def expert_of(line_step, plane_step):
-        return (line_place ^ line_step) * plane + (plane_place ^ plane_step)
-
-    prob_near = jnp.stack(
-        [
-            jnp.sum(jnp.where(expert_ids[None, :] == expert_of(0, d), prob_rows, 0.0), axis=1)
-            for d in range(plane)
-        ],
-        axis=1,
-    )
-    rows = lines * half
-
-    def spread(value):
-        return jnp.broadcast_to(
-            value[:, None, :, None], (rows, 2, plane, hidden_half)
-        ).reshape(rows, hidden)
-
-    gate_pre = jnp.dot(mixer_rows, gate_all, preferred_element_type=jnp.float32)
-    up_pre = jnp.dot(mixer_rows, up_all, preferred_element_type=jnp.float32)
-    grad_raw = residual_scale * jnp.dot(cot_rows, down_all.T, preferred_element_type=jnp.float32)
-    sigmoid_gate = jax.nn.sigmoid(gate_pre)
-    silu_gate = gate_pre * sigmoid_gate
-    active = silu_gate * up_pre
-    weighting_near = jnp.sum(
-        (active * grad_raw).reshape(rows, 2, plane, hidden_half), axis=(1, 3)
-    )
-    prob_wide = spread(prob_near)
-    scaled_active = (prob_wide * active).astype(jnp.bfloat16)
-    grad_active = prob_wide * grad_raw
-    grad_gate_pre = (
-        grad_active * up_pre * sigmoid_gate * (1.0 + gate_pre * (1.0 - sigmoid_gate))
-    ).astype(jnp.bfloat16)
-    grad_up_pre = (grad_active * silu_gate).astype(jnp.bfloat16)
-    out_rows = jnp.dot(scaled_active, down_all, preferred_element_type=jnp.float32).astype(
-        jnp.bfloat16
-    )
-    grad_rows = (
-        jnp.dot(grad_gate_pre, gate_all.T, preferred_element_type=jnp.float32)
-        + jnp.dot(grad_up_pre, up_all.T, preferred_element_type=jnp.float32)
-    ).astype(jnp.bfloat16)
-
-    def line_return(value):
-        pieces = [value[d * half : (d + 1) * half] for d in range(lines)]
-        return [pieces[0]] + [exchange(pieces[d], d * plane) for d in range(1, lines)]
-
-    mixture = sum(piece.astype(jnp.float32) for piece in line_return(out_rows))
-    grad_mixer_rows = sum(piece.astype(jnp.float32) for piece in line_return(grad_rows))
-    grad_weighting = jnp.zeros((half, experts), jnp.float32)
-    for line_step, piece in enumerate(line_return(weighting_near)):
-        for plane_step in range(plane):
-            grad_weighting = grad_weighting + jnp.where(
-                expert_ids[None, :] == expert_of(line_step, plane_step),
-                piece[:, plane_step : plane_step + 1],
-                0.0,
-            )
-
-    gate_grad = jnp.dot(mixer_rows.T, grad_gate_pre, preferred_element_type=jnp.float32)
-    up_grad = jnp.dot(mixer_rows.T, grad_up_pre, preferred_element_type=jnp.float32)
-    down_grad = residual_scale * jnp.dot(
-        scaled_active.T, cot_rows, preferred_element_type=jnp.float32
-    )
-
-    def plane_sum(value, axis):
-        low = value.astype(jnp.bfloat16)
-        mine, theirs = jnp.split(low, 2, axis=axis)
-        both = mine.astype(jnp.float32) + swap_cores(theirs).astype(jnp.float32)
-        parts = jnp.split(both, plane, axis=axis)
-        total = parts[0]
+    mixer_parts = line_parts(mixer_in)
+    prob_parts = line_parts(jnp.pad(gate_probs, ((0, 0), (0, 128 - experts))))
+    out_parts, grad_mixer_rows, weighting_sum, gate_grad, up_grad, down_grad = run_experts(
+        mixer_parts, cot_parts, prob_parts, gate_parts, up_parts, down_parts
+    )
+    grad_weighting = weighting_sum[:, :experts]
+    mixture = out_parts[0].astype(jnp.float32)
+    for d in range(1, lines):
+        mixture = mixture + exchange(out_parts[d], d * plane).astype(jnp.float32)
+
+    def plane_sum(low):
+        both = low[:plane].astype(jnp.float32) + swap_cores(low[plane:]).astype(jnp.float32)
+        total = both[0]
         for d in range(1, plane):
-            total = total + exchange(parts[d].astype(jnp.bfloat16), d).astype(jnp.float32)
+            total = total + exchange(both[d].astype(jnp.bfloat16), d).astype(jnp.float32)
         return total
 
-    gate_grad = plane_sum(gate_grad, 1)
-    up_grad = plane_sum(up_grad, 1)
-    down_grad = plane_sum(down_grad, 0)
+    gate_grad = plane_sum(gate_grad)
+    up_grad = plane_sum(up_grad)
+    down_grad = plane_sum(down_grad)
 
     result = middle + residual_scale * mixture
     result_low = result.astype(jnp.bfloat16)
@@ -634,8 +985,9 @@
         value.astype(jnp.bfloat16)
         for value in (out_grad_t, key_grad, query_grad, value_grad, small)
     ]
-    first_part = scatter_rows(jnp.concatenate(low[:2], axis=1), 0, place)
-    second_part = scatter_rows(jnp.concatenate(low[2:], axis=1), 1, place)
+    first_part, second_part = run_scatter(
+        [jnp.concatenate(low[:2], axis=1), jnp.concatenate(low[2:], axis=1)], 1
+    )
     query_width = query_weight.shape[1]
     key_width = key_matrix.shape[1]
     small_part = second_part[:, query_width + key_width :]

time: 790 us -> 693 us (0.88)
  Pallas kernels: 0 us -> 229 us
  matrix products: 139 us -> 45.7 us
  waiting for transfers between devices: 333 us -> 260 us
  local copies, waits for them, and re-layouts: 102 us -> 32.7 us
  starting transfers between devices: 108 us -> 45.7 us
  other arithmetic: 96.7 us -> 69.6 us
    pallas_call x0 -> x2, Pallas kernels: none -> 229 us  [the longest x1 119 us: run_scatter(): pl.pallas_call(functools.partial(scatter_kernel, [value.shape[1] for valu...]
    dot_general x9 -> x0, matrix products: 93.4 us -> none  [the longest x1 16.1 us: dense_shards(): jnp.dot(cot_rows, down_all.T, preferred_element_type=jnp.float32)]
    ppermute x44 -> x30, waiting for transfers between devices: 329 us -> 257 us  [exchange(): return lax.ppermute(value, 'ep', [(i, i ^ bits) for i in range(count)])]
    ppermute x44 -> x30, starting transfers between devices: 103 us -> 41.3 us  [exchange(): return lax.ppermute(value, 'ep', [(i, i ^ bits) for i in range(count)])]
    unnamed x214 -> x171, local copies, waits for them, and re-layouts: 33.7 us -> 9.94 us
    reshape x2 -> x0, local copies, waits for them, and re-layouts: 21.6 us -> none  [the longest x1 10.8 us: dense_shards(): (active * grad_raw).reshape(rows, 2, plane, hidden_half)]
    convert_element_type x9 -> x0, other arithmetic: 17.5 us -> none  [the longest x1 13 us: dense_shards(): grad_gate_pre = (grad_active * up_pre * sigmoid_gate * (1.0 + gate_pre *...]
    concatenate x5 -> x0, local copies, waits for them, and re-layouts: 11.8 us -> none  [the longest x1 5.98 us: dense_shards(): second_part = scatter_rows(jnp.concatenate(low[2:], axis=1), 1, place)]
  transfers between devices with their start and end apart: 65 -> 51, of which waited for: 23 -> 20; matrix products, arithmetic and copies ran while one was open for 30% -> 19% of each run, Pallas kernels for 0% -> 17%
where the time goes in v2:
time: 693 us; the launch traced here: 685 us
  waiting for transfers between devices  260 us (38%)
  Pallas kernels  229 us (33%)
  other arithmetic  69.6 us (10%)
  starting transfers between devices  45.7 us (7%)
  matrix products  45.7 us (7%)
  local copies, waits for them, and re-layouts  32.7 us (5%)
    ppermute x30, waiting for transfers between devices, exchange(): return lax.ppermute(value, 'ep', [(i, i ^ bits) for i in range(count)])  257 us
    pallas_call x1, Pallas kernels, run_scatter(): pl.pallas_call(functools.partial(scatter_kernel, [value.shape[1] for valu...  119 us
    pallas_call x1, Pallas kernels, run_experts(): pl.pallas_call(expert_kernel, name='experts', out_shape=(*[shape((half, w...  110 us
    ppermute x30, starting transfers between devices, exchange(): return lax.ppermute(value, 'ep', [(i, i ^ bits) for i in range(count)])  41.3 us
    another operation x7, other arithmetic  17.8 us
  transfers between devices with their start and end apart: 51, of which 20 were waited for; matrix products, arithmetic and copies ran while one was open for 19% of the time, Pallas kernels for 17%

profile of v2, /device:TPU:0, one launch (start us, length us, event | category | flops | bytes accessed | tf_op | source)
XLA Modules:
  0.0 685.2 jit_solution(14475226586258207256)
XLA Ops:
  2.9 5.0 collective-permute-start.6
  25.2 5.0 fusion.35
  35.4 40.1 %collective-permute-done.5.refs_6_ = bf16[256,1536]{1,0:T(8,128)(2,1)} collective-permute-done((bf16[256,1536]{1,0:T(8,128)(2,1)}, bf16[256,1536]{1,0:T(8,128)(2,1)}, u32[]{:S(2)}, u32[]{:S(2)}) %collective-permute-start.5) | collective-permute-done | bytes 786464 | tf_op jit(solution)/shard_map/ppermute | solution.py:362
  79.5 16.5 %collective-permute-done.10.refs_13_ = bf16[1536,256]{1,0:T(8,128)(2,1)S(1)} collective-permute-done((bf16[1536,256]{1,0:T(8,128)(2,1)S(1)}, bf16[1536,256]{1,0:T(8,128)(2,1)S(1)}, u32[]{:S(2)}, u32[]{:S(2)}) %collective-permute-start.10) | collective-permute-done | bytes 786464 | tf_op jit(solution)/shard_map/ppermute | solution.py:362
  102.7 11.3 %collective-permute-done.19.refs_23_ = bf16[1536,256]{1,0:T(8,128)(2,1)} collective-permute-done((bf16[1536,256]{1,0:T(8,128)(2,1)}, bf16[1536,256]{1,0:T(8,128)(2,1)}, u32[]{:S(2)}, u32[]{:S(2)}) %collective-permute-start.19) | collective-permute-done | bytes 786464 | tf_op jit(solution)/shard_map/ppermute | solution.py:362
  118.1 11.7 %collective-permute-done.17.refs_21_ = bf16[1536,256]{1,0:T(8,128)(2,1)} collective-permute-done((bf16[1536,256]{1,0:T(8,128)(2,1)}, bf16[1536,256]{1,0:T(8,128)(2,1)}, u32[]{:S(2)}, u32[]{:S(2)}) %collective-permute-start.17) | collective-permute-done | bytes 786464 | tf_op jit(solution)/shard_map/ppermute | solution.py:362
  131.4 16.3 %collective-permute-done.26.refs_31_ = bf16[256,1536]{1,0:T(8,128)(2,1)} collective-permute-done((bf16[256,1536]{1,0:T(8,128)(2,1)}, bf16[256,1536]{1,0:T(8,128)(2,1)}, u32[]{:S(2)}, u32[]{:S(2)}) %collective-permute-start.26) | collective-permute-done | bytes 786464 | tf_op jit(solution)/shard_map/ppermute | solution.py:362
  150.2 11.5 %collective-permute-done.24.refs_29_ = bf16[256,1536]{1,0:T(8,128)(2,1)} collective-permute-done((bf16[256,1536]{1,0:T(8,128)(2,1)}, bf16[256,1536]{1,0:T(8,128)(2,1)}, u32[]{:S(2)}, u32[]{:S(2)}) %collective-permute-start.24) | collective-permute-done | bytes 786464 | tf_op jit(solution)/shard_map/ppermute | solution.py:362
  173.8 15.9 %collective-permute-done.3.refs_3_ = bf16[256,1536]{1,0:T(8,128)(2,1)S(1)} collective-permute-done((bf16[256,1536]{1,0:T(8,128)(2,1)S(1)}, bf16[256,1536]{1,0:T(8,128)(2,1)S(1)}, u32[]{:S(2)}, u32[]{:S(2)}) %collective-permute-start.3) | collective-permute-done | bytes 786464 | tf_op jit(solution)/shard_map/ppermute | solution.py:362
  189.7 47.6 %collective-permute-done.2.refs_2_ = bf16[256,1536]{1,0:T(8,128)(2,1)S(1)} collective-permute-done((bf16[256,1536]{1,0:T(8,128)(2,1)S(1)}, bf16[256,1536]{1,0:T(8,128)(2,1)S(1)}, u32[]{:S(2)}, u32[]{:S(2)}) %collective-permute-start.2) | collective-permute-done | bytes 786464 | tf_op jit(solution)/shard_map/ppermute | solution.py:362
  238.3 110.1 %experts.1 = (bf16[256,1536]{1,0:T(8,128)(2,1)}, bf16[256,1536]{1,0:T(8,128)(2,1)}, bf16[256,1536]{1,0:T(8,128)(2,1)}, bf16[256,1536]{1,0:T(8,128)(2,1)}, f32[25...) custom-call(bf16[256,1536]{1,0:T(8,128)(2,1)} %copy-done.7, ...), custom_call_target="tpu_custom_call" | custom-call | flops 57982058496 | bytes 37748736 | tf_op jit(solution)/shard_map/experts/pallas_call | solution.py:590
  356.7 26.9 %collective-permute-done.31 = bf16[256,1536]{1,0:T(8,128)(2,1)S(1)} collective-permute-done((bf16[256,1536]{1,0:T(8,128)(2,1)}, bf16[256,1536]{1,0:T(8,128)(2,1)S(1)}, u32[]{:S(2)}, u32[]{:S(2)}) %collective-permute-start.31) | collective-permute-done | bytes 786464 | tf_op jit(solution)/shard_map/ppermute | solution.py:362
  383.5 22.7 %collective-permute-done.32 = bf16[256,1536]{1,0:T(8,128)(2,1)} collective-permute-done((bf16[256,1536]{1,0:T(8,128)(2,1)}, bf16[256,1536]{1,0:T(8,128)(2,1)}, u32[]{:S(2)}, u32[]{:S(2)}) %collective-permute-start.32) | collective-permute-done | bytes 786464 | tf_op jit(solution)/shard_map/ppermute | solution.py:362
  406.3 5.0 multiply_reduce_fusion.2
  430.3 7.1 %fusion.43 = bf16[4,64,512]{2,1,0:T(8,128)(2,1)} fusion(bf16[512,4,3,64]{0,3,2,1:T(8,128)(2,1)S(1)} %bitcast.181, f32[4,3,512]{2,1,0:T(4,128)S(1)} %log_add_fusion, f32[4,512,512,3]{2,1,3,0:T(8,128)} %copy-done.1, pred[512,512]{0,1:T(8,128)(4,1)S(1)} %copy-done.10), kind=kOutput, calls=%fused_computation.84 | convolution fusion | flops 415367168 | bytes 13918208 | tf_op jit(solution)/shard_map/hgqk,qhgd->khd/dot_general | solution.py:113
  437.4 6.8 fusion
  444.3 5.5 fusion.2
  473.1 6.2 fusion.63
  484.3 5.7 fusion.62
  494.4 5.2 fusion.61
  511.5 118.9 %scatter.1 = (f32[96,1024]{1,0:T(8,128)}, f32[96,1152]{1,0:T(8,128)}) custom-call(bf16[1536,1024]{1,0:T(8,128)(2,1)} %pad_maximum_fusion.refs_0_, bf16[1536,1152]{1,0:T(8,128)(2,1)} %fusion.11.refs_1_), custom_call_target="tpu_custom_call" | custom-call | tf_op jit(solution)/shard_map/scatter/pallas_call | solution.py:784
  654.7 7.6 %collective-permute-done.39 = bf16[1536,256]{1,0:T(8,128)(2,1)S(1)} collective-permute-done((bf16[1536,256]{1,0:T(8,128)(2,1)}, bf16[1536,256]{1,0:T(8,128)(2,1)S(1)}, u32[]{:S(2)}, u32[]{:S(2)}) %collective-permute-start.39) | collective-permute-done | bytes 786464 | tf_op jit(solution)/shard_map/ppermute | solution.py:362
  662.3 13.7 %collective-permute-done.41 = bf16[1536,256]{1,0:T(8,128)(2,1)S(1)} collective-permute-done((bf16[1536,256]{1,0:T(8,128)(2,1)S(1)}, bf16[1536,256]{1,0:T(8,128)(2,1)S(1)}, u32[]{:S(2)}, u32[]{:S(2)}) %collective-permute-start.41) | collective-permute-done | bytes 786464 | tf_op jit(solution)/shard_map/ppermute | solution.py:362
  676.0 5.8 collective-permute-done.40
  (346 shorter events, 154.6 us)
Async XLA Ops:
  8.0 67.6 %collective-permute-start.5 = (bf16[256,1536]{1,0:T(8,128)(2,1)}, bf16[256,1536]{1,0:T(8,128)(2,1)}, u32[]{:S(2)}, u32[]{:S(2)}) collective-permute-start(bf16[256,1536]{1,0:T(8,128)(2,1)} %constant_dynamic-slice_fusion.1.refs_4_), channel_id=1, source_target_pairs={{0,16},{2,18},{4,20},{6,22},{8,24},{10,26},{12,28},{14,30},{16,0},... | collective-permute-start | bytes 2359304 | tf_op jit(solution)/shard_map/ppermute | solution.py:362
  8.0 69.1 %collective-permute-start.4 = (bf16[256,1536]{1,0:T(8,128)(2,1)}, bf16[256,1536]{1,0:T(8,128)(2,1)}, u32[]{:S(2)}, u32[]{:S(2)}) collective-permute-start(bf16[256,1536]{1,0:T(8,128)(2,1)} %constant_dynamic-slice_fusion.1.refs_4_), channel_id=1, source_target_pairs={{0,8},{2,10},{4,12},{6,14},{8,0},{10,2},{12,4},{14,6},{16,24},{18,... | collective-permute-start | bytes 2359304 | tf_op jit(solution)/shard_map/ppermute | solution.py:362
  8.5 68.5 %collective-permute-start.13 = (bf16[1536,256]{1,0:T(8,128)(2,1)}, bf16[1536,256]{1,0:T(8,128)(2,1)}, u32[]{:S(2)}, u32[]{:S(2)}) collective-permute-start(bf16[1536,256]{1,0:T(8,128)(2,1)} %bitcast.199), channel_id=1, source_target_pairs={{0,1},{1,0},{2,3},{3,2},{4,5},{5,4},{6,7},{7,6},{8,9},{9,8},{10,11... | collective-permute-start | bytes 2359304 | tf_op jit(solution)/shard_map/ppermute | solution.py:357
  8.5 69.0 %collective-permute-start.12 = (bf16[1536,256]{1,0:T(8,128)(2,1)}, bf16[1536,256]{1,0:T(8,128)(2,1)}, u32[]{:S(2)}, u32[]{:S(2)}) collective-permute-start(bf16[1536,256]{1,0:T(8,128)(2,1)} %bitcast.200), channel_id=1, source_target_pairs={{0,6},{2,4},{4,2},{6,0},{8,14},{10,12},{12,10},{14,8},{16,22},{18,... | collective-permute-start | bytes 2359304 | tf_op jit(solution)/shard_map/ppermute | solution.py:362
  34.9 44.2 %collective-permute-start.11 = (bf16[1536,256]{1,0:T(8,128)(2,1)S(1)}, bf16[1536,256]{1,0:T(8,128)(2,1)}, u32[]{:S(2)}, u32[]{:S(2)}) collective-permute-start(bf16[1536,256]{1,0:T(8,128)(2,1)S(1)} %bitcast.202), channel_id=1, source_target_pairs={{0,4},{2,6},{4,0},{6,2},{8,12},{10,14},{12,8},{14,10},{16,20},{18,... | collective-permute-start | bytes 2359304 | tf_op jit(solution)/shard_map/ppermute | solution.py:362
  79.0 37.6 %collective-permute-start.18 = (bf16[1536,256]{1,0:T(8,128)(2,1)}, bf16[1536,256]{1,0:T(8,128)(2,1)}, u32[]{:S(2)}, u32[]{:S(2)}) collective-permute-start(bf16[1536,256]{1,0:T(8,128)(2,1)} %bitcast.13.refs_20_), channel_id=1, source_target_pairs={{0,4},{2,6},{4,0},{6,2},{8,12},{10,14},{12,8},{14,10},{16,20},{18,... | collective-permute-start | bytes 2359304 | tf_op jit(solution)/shard_map/ppermute | solution.py:362
  100.9 46.8 %collective-permute-start.26 = (bf16[256,1536]{1,0:T(8,128)(2,1)}, bf16[256,1536]{1,0:T(8,128)(2,1)}, u32[]{:S(2)}, u32[]{:S(2)}) collective-permute-start(bf16[256,1536]{1,0:T(8,128)(2,1)} %bitcast.14.refs_28_), channel_id=1, source_target_pairs={{0,6},{2,4},{4,2},{6,0},{8,14},{10,12},{12,10},{14,8},{16,22},{18,... | collective-permute-start | bytes 2359304 | tf_op jit(solution)/shard_map/ppermute | solution.py:362
  116.6 45.1 %collective-permute-start.24 = (bf16[256,1536]{1,0:T(8,128)(2,1)}, bf16[256,1536]{1,0:T(8,128)(2,1)}, u32[]{:S(2)}, u32[]{:S(2)}) collective-permute-start(bf16[256,1536]{1,0:T(8,128)(2,1)} %bitcast.14.refs_28_), channel_id=1, source_target_pairs={{0,2},{2,0},{4,6},{6,4},{8,10},{10,8},{12,14},{14,12},{16,18},{18,... | collective-permute-start | bytes 2359304 | tf_op jit(solution)/shard_map/ppermute | solution.py:362
  129.9 36.9 %collective-permute-start.16 = (bf16[1536,256]{1,0:T(8,128)(2,1)}, bf16[1536,256]{1,0:T(8,128)(2,1)}, u32[]{:S(2)}, u32[]{:S(2)}) collective-permute-start(bf16[1536,256]{1,0:T(8,128)(2,1)} %collective-permute-done.12.refs_15_), channel_id=1, source_target_pairs={{0,1},{1,0},{2,3},{3,2},{4,5},{5,4},{6,7},{7,6},{8,9},{9,8},{10,11... | collective-permute-start | bytes 2359304 | tf_op jit(solution)/shard_map/ppermute | solution.py:357
  129.9 37.5 %collective-permute-start.15 = (bf16[1536,256]{1,0:T(8,128)(2,1)}, bf16[1536,256]{1,0:T(8,128)(2,1)}, u32[]{:S(2)}, u32[]{:S(2)}) collective-permute-start(bf16[1536,256]{1,0:T(8,128)(2,1)} %collective-permute-done.11.refs_14_), channel_id=1, source_target_pairs={{0,1},{1,0},{2,3},{3,2},{4,5},{5,4},{6,7},{7,6},{8,9},{9,8},{10,11... | collective-permute-start | bytes 2359304 | tf_op jit(solution)/shard_map/ppermute | solution.py:357
  170.4 66.9 %collective-permute-start.2 = (bf16[256,1536]{1,0:T(8,128)(2,1)S(1)}, bf16[256,1536]{1,0:T(8,128)(2,1)S(1)}, u32[]{:S(2)}, u32[]{:S(2)}) collective-permute-start(bf16[256,1536]{1,0:T(8,128)(2,1)S(1)} %multiply_convert_fusion.refs_0_), channel_id=1, source_target_pairs={{0,16},{2,18},{4,20},{6,22},{8,24},{10,26},{12,28},{14,30},{16,0},... | collective-permute-start | bytes 2359304 | tf_op jit(solution)/shard_map/ppermute | solution.py:362
  171.6 66.7 %collective-permute-start.1 = (bf16[256,1536]{1,0:T(8,128)(2,1)S(1)}, bf16[256,1536]{1,0:T(8,128)(2,1)}, u32[]{:S(2)}, u32[]{:S(2)}) collective-permute-start(bf16[256,1536]{1,0:T(8,128)(2,1)S(1)} %multiply_convert_fusion.refs_0_), channel_id=1, source_target_pairs={{0,8},{2,10},{4,12},{6,14},{8,0},{10,2},{12,4},{14,6},{16,24},{18,... | collective-permute-start | bytes 2359304 | tf_op jit(solution)/shard_map/ppermute | solution.py:362
  350.8 55.4 %collective-permute-start.32 = (bf16[256,1536]{1,0:T(8,128)(2,1)}, bf16[256,1536]{1,0:T(8,128)(2,1)}, u32[]{:S(2)}, u32[]{:S(2)}) collective-permute-start(bf16[256,1536]{1,0:T(8,128)(2,1)} %get-tuple-element.66), channel_id=1, source_target_pairs={{0,16},{2,18},{4,20},{6,22},{8,24},{10,26},{12,28},{14,30},{16,0},... | collective-permute-start | bytes 2359304 | tf_op jit(solution)/shard_map/ppermute | solution.py:362
  351.7 54.5 %collective-permute-start.33 = (bf16[256,1536]{1,0:T(8,128)(2,1)}, bf16[256,1536]{1,0:T(8,128)(2,1)}, u32[]{:S(2)}, u32[]{:S(2)}) collective-permute-start(bf16[256,1536]{1,0:T(8,128)(2,1)} %get-tuple-element.67), channel_id=1, source_target_pairs={{0,24},{2,26},{4,28},{6,30},{8,16},{10,18},{12,20},{14,22},{16,8},... | collective-permute-start | bytes 2359304 | tf_op jit(solution)/shard_map/ppermute | solution.py:362
  419.2 53.4 %collective-permute-start.46 = (bf16[4,256,1536]{2,1,0:T(8,128)(2,1)}, bf16[4,256,1536]{2,1,0:T(8,128)(2,1)}, u32[]{:S(2)}, u32[]{:S(2)}) collective-permute-start(bf16[4,256,1536]{2,1,0:T(8,128)(2,1)} %slice.182), channel_id=1, source_target_pairs={{0,1},{1,0},{2,3},{3,2},{4,5},{5,4},{6,7},{7,6},{8,9},{9,8},{10,11... | collective-permute-start | bytes 9437192 | tf_op jit(solution)/shard_map/ppermute | solution.py:357
  419.2 64.5 %collective-permute-start.42 = (bf16[4,1536,256]{2,1,0:T(8,128)(2,1)}, bf16[4,1536,256]{2,1,0:T(8,128)(2,1)}, u32[]{:S(2)}, u32[]{:S(2)}) collective-permute-start(bf16[4,1536,256]{2,1,0:T(8,128)(2,1)} %slice.176), channel_id=1, source_target_pairs={{0,1},{1,0},{2,3},{3,2},{4,5},{5,4},{6,7},{7,6},{8,9},{9,8},{10,11... | collective-permute-start | bytes 9437192 | tf_op jit(solution)/shard_map/ppermute | solution.py:357
  419.8 74.6 %collective-permute-start.38 = (bf16[4,1536,256]{2,1,0:T(8,128)(2,1)}, bf16[4,1536,256]{2,1,0:T(8,128)(2,1)}, u32[]{:S(2)}, u32[]{:S(2)}) collective-permute-start(bf16[4,1536,256]{2,1,0:T(8,128)(2,1)} %slice.170), channel_id=1, source_target_pairs={{0,1},{1,0},{2,3},{3,2},{4,5},{5,4},{6,7},{7,6},{8,9},{9,8},{10,11... | collective-permute-start | bytes 9437192 | tf_op jit(solution)/shard_map/ppermute | solution.py:357
  424.9 38.2 %collective-permute-start.34 = (bf16[256,1536]{1,0:T(8,128)(2,1)}, bf16[256,1536]{1,0:T(8,128)(2,1)}, u32[]{:S(2)}, u32[]{:S(2)}) collective-permute-start(bf16[256,1536]{1,0:T(8,128)(2,1)} %get-tuple-element.158), channel_id=1, source_target_pairs={{0,1},{1,0},{2,3},{3,2},{4,5},{5,4},{6,7},{7,6},{8,9},{9,8},{10,11... | collective-permute-start | bytes 2359304 | tf_op jit(solution)/shard_map/ppermute | solution.py:357
  480.8 149.7 %collective-permute-start.47 = (bf16[256,1536]{1,0:T(8,128)(2,1)}, bf16[256,1536]{1,0:T(8,128)(2,1)}, u32[]{:S(2)}, u32[]{:S(2)}) collective-permute-start(bf16[256,1536]{1,0:T(8,128)(2,1)} %get-tuple-element.159), channel_id=1, source_target_pairs={{0,2},{2,0},{4,6},{6,4},{8,10},{10,8},{12,14},{14,12},{16,18},{18,... | collective-permute-start | bytes 2359304 | tf_op jit(solution)/shard_map/ppermute | solution.py:362
  482.3 159.3 %collective-permute-start.49 = (bf16[256,1536]{1,0:T(8,128)(2,1)}, bf16[256,1536]{1,0:T(8,128)(2,1)}, u32[]{:S(2)}, u32[]{:S(2)}) collective-permute-start(bf16[256,1536]{1,0:T(8,128)(2,1)} %get-tuple-element.160), channel_id=1, source_target_pairs={{0,6},{2,4},{4,2},{6,0},{8,14},{10,12},{12,10},{14,8},{16,22},{18,... | collective-permute-start | bytes 2359304 | tf_op jit(solution)/shard_map/ppermute | solution.py:362
  483.8 159.3 %collective-permute-start.48 = (bf16[256,1536]{1,0:T(8,128)(2,1)}, bf16[256,1536]{1,0:T(8,128)(2,1)}, u32[]{:S(2)}, u32[]{:S(2)}) collective-permute-start(bf16[256,1536]{1,0:T(8,128)(2,1)} %get-tuple-element.161), channel_id=1, source_target_pairs={{0,4},{2,6},{4,0},{6,2},{8,12},{10,14},{12,8},{14,10},{16,20},{18,... | collective-permute-start | bytes 2359304 | tf_op jit(solution)/shard_map/ppermute | solution.py:362
  491.5 152.1 %collective-permute-start.43 = (bf16[1536,256]{1,0:T(8,128)(2,1)}, bf16[1536,256]{1,0:T(8,128)(2,1)}, u32[]{:S(2)}, u32[]{:S(2)}) collective-permute-start(bf16[1536,256]{1,0:T(8,128)(2,1)} %get-tuple-element.162), channel_id=1, source_target_pairs={{0,2},{2,0},{4,6},{6,4},{8,10},{10,8},{12,14},{14,12},{16,18},{18,... | collective-permute-start | bytes 2359304 | tf_op jit(solution)/shard_map/ppermute | solution.py:362
  505.4 143.3 %collective-permute-start.45 = (bf16[1536,256]{1,0:T(8,128)(2,1)}, bf16[1536,256]{1,0:T(8,128)(2,1)}, u32[]{:S(2)}, u32[]{:S(2)}) collective-permute-start(bf16[1536,256]{1,0:T(8,128)(2,1)} %get-tuple-element.163), channel_id=1, source_target_pairs={{0,6},{2,4},{4,2},{6,0},{8,14},{10,12},{12,10},{14,8},{16,22},{18,... | collective-permute-start | bytes 2359304 | tf_op jit(solution)/shard_map/ppermute | solution.py:362
  643.6 38.2 %collective-permute-start.40 = (bf16[1536,256]{1,0:T(8,128)(2,1)S(1)}, bf16[1536,256]{1,0:T(8,128)(2,1)S(1)}, u32[]{:S(2)}, u32[]{:S(2)}) collective-permute-start(bf16[1536,256]{1,0:T(8,128)(2,1)S(1)} %copy-done.28), channel_id=1, source_target_pairs={{0,4},{2,6},{4,0},{6,2},{8,12},{10,14},{12,8},{14,10},{16,20},{18,... | collective-permute-start | bytes 2359304 | tf_op jit(solution)/shard_map/ppermute | solution.py:362
  (112 other events, 2521.9 us)

commit v3 on v0

--- a/solution.py
+++ b/solution.py
@@ -1,6 +1,10 @@
+import functools
+
 import jax
 import jax.numpy as jnp
 from jax import lax
+from jax.experimental import pallas as pl
+from jax.experimental.pallas import tpu as pltpu
 from jax.sharding import PartitionSpec as P
 
 HEAD_FEATURES = 64
@@ -137,7 +141,7 @@
     return jnp.sqrt(jnp.mean((value_rows * value_rows).reshape(seq_count, -1), axis=1))
 
 
-def shards(
+def routed_shards(
     stream,
     cotangent,
     attention_gain,
@@ -349,6 +353,1318 @@
     )
 
 
+MESH = pl.DeviceIdType.MESH
+PLANE = 4
+LINES = 4
+
+
+def flip(place, unit):
+    return place + unit * (1 - 2 * lax.rem(lax.div(place, unit), 2))
+
+
+def flip_line(place, step):
+    if step % 2:
+        place = flip(place, PLANE)
+    if step // 2:
+        place = flip(place, 2 * PLANE)
+    return place
+
+
+def matmul(left, right):
+    return jnp.dot(left, right, preferred_element_type=jnp.float32)
+
+
+def matmul_nt(left, right):
+    return lax.dot_general(
+        left, right, (((1,), (1,)), ((), ())), preferred_element_type=jnp.float32
+    )
+
+
+def matmul_tn(left, right):
+    return lax.dot_general(
+        left, right, (((0,), (0,)), ((), ())), preferred_element_type=jnp.float32
+    )
+
+
+def lane_halves(value):
+    lane = lax.broadcasted_iota(jnp.int32, value.shape, 1)
+    low = jnp.where(lane < HEAD_FEATURES, value, 0.0)
+    high = jnp.where(lane < HEAD_FEATURES, 0.0, value)
+    return low, high
+
+
+def partner_lanes(value):
+    width = value.shape[1]
+    quarter = HEAD_FEATURES // 2
+    lane = lax.broadcasted_iota(jnp.int32, value.shape, 1)
+    ahead = pltpu.roll(value, width - quarter, 1)
+    behind = pltpu.roll(value, quarter, 1)
+    return jnp.where(lax.rem(lane, HEAD_FEATURES) < quarter, ahead, behind)
+
+
+def causal_scores(query_block, key_block, row_start):
+    scores = score_scale * matmul_nt(query_block, key_block)
+    row = lax.broadcasted_iota(jnp.int32, scores.shape, 0) + row_start
+    column = lax.broadcasted_iota(jnp.int32, scores.shape, 1)
+    return jnp.where(row >= column, scores, masked_score)
+
+
+def store_slots(slots, values):
+    for group in range(values.shape[1] // HEAD_FEATURES):
+        pair = group // 2
+        low, high = lane_halves(values[:, pair * 128 : pair * 128 + 128])
+        if group % 2:
+            low = pltpu.roll(high, HEAD_FEATURES, 1)
+        else:
+            high = pltpu.roll(low, HEAD_FEATURES, 1)
+        slots[2 * group] = low.astype(jnp.bfloat16)
+        slots[2 * group + 1] = high.astype(jnp.bfloat16)
+
+
+def front_kernel(*refs):
+    refs = list(refs)
+
+    def take(count):
+        taken = refs[:count]
+        del refs[:count]
+        return taken
+
+    stream, cotangent, gain_first, gain_second, query_weight, key_weight = take(6)
+    value_weight, out_weight, router, routes, cosine, sine = take(6)
+    weights = take(3)
+    weights_all = take(3)
+    mixer_all, cot_all, probs_all = take(3)
+    normed, queries, keys, values, mixed, attended = take(6)
+    stream_v, query_v, key_v, value_v, out_v = take(5)
+    key_slots, value_slots, part_send, part_recv, mixer, probs = take(6)
+    load_sem, own_sem, weight_send, weight_recv = take(4)
+    relay_send, relay_recv, probs_send, probs_recv, part_sem = take(5)
+    tokens, width = stream_v.shape
+    half = tokens // 2
+
+    place = lax.axis_index("ep")
+    core = lax.axis_index("tp")
+    line = lax.div(place, PLANE)
+    across = [flip(place, 1), flip(place, 2)]
+    partners = [flip_line(place, step) for step in range(LINES)]
+    own_rows = pl.ds(pl.multiple_of(core * half, half), half)
+    other_rows = pl.ds(pl.multiple_of((1 - core) * half, half), half)
+
+    barrier = pltpu.get_barrier_semaphore()
+    for other in across + partners[1:]:
+        pl.semaphore_signal(barrier, inc=1, device_id=(other, core), device_id_type=MESH)
+    pl.semaphore_signal(barrier, inc=1, device_id=(place, 1 - core), device_id_type=MESH)
+
+    loads = [
+        pltpu.make_async_copy(source, target, load_sem.at[index])
+        for index, (source, target) in enumerate(
+            (
+                (stream, stream_v),
+                (query_weight, query_v),
+                (key_weight, key_v),
+                (value_weight, value_v),
+                (out_weight, out_v),
+            )
+        )
+    ]
+    for copy in loads:
+        copy.start()
+    pl.semaphore_wait(barrier, LINES + 2)
+
+    def send(source, target, sems, index, device):
+        return pltpu.make_async_remote_copy(
+            src_ref=source,
+            dst_ref=target,
+            send_sem=sems[0].at[index],
+            recv_sem=sems[1].at[index],
+            device_id=device,
+            device_id_type=MESH,
+        )
+
+    sibling = (place, 1 - core)
+    sems = (weight_send, weight_recv)
+
+    def direct(kind, axis):
+        return send(
+            weights[kind],
+            weights_all[kind].at[axis + 1],
+            sems,
+            (kind, axis),
+            (across[axis], core),
+        )
+
+    def to_sibling(kind, slot):
+        source = weights[kind] if slot == 0 else weights_all[kind].at[slot]
+        return send(source, weights_all[kind].at[PLANE + slot], sems, (kind, 2 + slot), sibling)
+
+    def onward(kind, axis):
+        gathered = weights_all[kind]
+        source, target = gathered.at[2 - axis], gathered.at[3]
+        if kind == 1:
+            part = pl.ds(axis * (width // 2), width // 2)
+            source, target = gathered.at[2 - axis, part], gathered.at[3, part]
+        return send(source, target, sems, (kind, 6 + axis), (across[axis], core))
+
+    onwards = {0: (0,), 1: (0, 1), 2: (1,)}
+
+    def relay(array, hop, downward):
+        gathered = (cot_all, mixer_all)[array]
+        shift = -1 if downward else 1
+        block = jnp.clip(line - shift * hop, 0, LINES - 1)
+        if hop == 0:
+            source = mixer if array else cotangent.at[own_rows]
+        else:
+            source = gathered.at[block]
+        return send(
+            source,
+            gathered.at[block],
+            (relay_send, relay_recv),
+            (array, downward, hop),
+            (place + shift * PLANE, core),
+        )
+
+    def relay_sends(hop, downward):
+        if downward:
+            return jnp.logical_and(line > 0, line + hop < LINES)
+        return jnp.logical_and(line < LINES - 1, line - hop >= 0)
+
+    def relay_receives(hop, downward):
+        if downward:
+            return line + 1 + hop < LINES
+        return line - 1 - hop >= 0
+
+    def start_relay(array, hop):
+        for downward in (0, 1):
+
+            @pl.when(relay_sends(hop, downward))
+            def _():
+                relay(array, hop, downward).start()
+
+    def receive_relay(array, hop):
+        for downward in (0, 1):
+
+            @pl.when(relay_receives(hop, downward))
+            def _():
+                relay(array, hop, downward).wait_recv()
+
+    def finish_relay(array, hop):
+        for downward in (0, 1):
+
+            @pl.when(relay_sends(hop, downward))
+            def _():
+                relay(array, hop, downward).wait_send()
+
+    for kind in range(3):
+        for axis in (0, 1):
+            direct(kind, axis).start()
+    start_relay(0, 0)
+    own_copies = [
+        pltpu.make_async_copy(weights[kind], weights_all[kind].at[0], own_sem.at[kind])
+        for kind in range(3)
+    ]
+    own_copies.append(
+        pltpu.make_async_copy(cotangent.at[own_rows], cot_all.at[line], own_sem.at[3])
+    )
+    for kind in range(3):
+        to_sibling(kind, 0).start()
+    for copy in own_copies:
+        copy.start()
+
+    loads[0].wait()
+    stream_f = stream_v[...].astype(jnp.float32)
+    inverse = lax.rsqrt(jnp.mean(stream_f * stream_f, axis=-1, keepdims=True) + epsilon)
+    normed[...] = (stream_f * inverse * gain_first[...]).astype(jnp.bfloat16)
+    for copy in loads[1:4]:
+        copy.wait()
+    span = cosine.shape[1]
+
+    def rotated(pre):
+        return pre * cosine[...] + partner_lanes(pre) * sine[...]
+
+    for start in range(0, query_v.shape[1], span):
+        here = slice(start, start + span)
+        queries[:, here] = rotated(matmul(normed[...], query_v[:, here])).astype(jnp.bfloat16)
+    key_rows = rotated(matmul(normed[...], key_v[...])).astype(jnp.bfloat16)
+    keys[...] = key_rows
+    store_slots(key_slots, key_rows.astype(jnp.float32))
+    value_rows = matmul(normed[...], value_v[...]).astype(jnp.bfloat16)
+    values[...] = value_rows
+    store_slots(value_slots, value_rows.astype(jnp.float32))
+    group = query_v.shape[1] // key_v.shape[1]
+    blocks = 2
+    block_rows = tokens // blocks
+
+    def head_pair(pair, carry):
+        here = pl.ds(pl.multiple_of(pair * 128, 128), 128)
+        for block in range(blocks):
+            rows = slice(block * block_rows, (block + 1) * block_rows)
+            reach = (block + 1) * block_rows
+            total = jnp.zeros((block_rows, 128), jnp.float32)
+            for parity in range(2):
+                slot = 2 * lax.div(2 * pair + parity, group) + parity
+                scores = causal_scores(
+                    queries[rows, here], key_slots[slot, :reach, :], block * block_rows
+                )
+                weight = jnp.exp(scores - jnp.max(scores, axis=-1, keepdims=True))
+                weight = weight / jnp.sum(weight, axis=-1, keepdims=True)
+                total = total + matmul(
+                    weight.astype(jnp.bfloat16), value_slots[slot, :reach, :]
+                )
+            mixed[rows, here] = total.astype(jnp.bfloat16)
+        return carry
+
+    lax.fori_loop(0, query_v.shape[1] // 128, head_pair, 0)
+    receive_relay(0, 0)
+    start_relay(0, 1)
+    loads[4].wait()
+    part_send[...] = matmul(mixed[other_rows, :], out_v[...]).astype(jnp.bfloat16)
+    part_copy = pltpu.make_async_remote_copy(
+        src_ref=part_send,
+        dst_ref=part_recv,
+        send_sem=part_sem.at[0],
+        recv_sem=part_sem.at[1],
+        device_id=sibling,
+        device_id_type=MESH,
+    )
+    part_copy.start()
+    own_part = matmul(mixed[own_rows, :], out_v[...])
+    part_copy.wait()
+    attended_half = own_part + part_recv[...].astype(jnp.float32)
+    attended[...] = attended_half.astype(jnp.bfloat16)
+    middle = stream_v[own_rows, :].astype(jnp.float32) + residual_scale * attended_half
+    inverse = lax.rsqrt(jnp.mean(middle * middle, axis=-1, keepdims=True) + epsilon)
+    mixer[...] = (middle * inverse * gain_second[...]).astype(jnp.bfloat16)
+    start_relay(1, 0)
+    logits = matmul(mixer[...], router[...])
+    lane = lax.broadcasted_iota(jnp.int32, logits.shape, 1)
+    routed = lane < 0
+    for entry in range(TOP):
+        routed = jnp.logical_or(routed, lane == routes[own_rows, entry : entry + 1])
+    largest = jnp.max(jnp.where(routed, logits, masked_score), axis=-1, keepdims=True)
+    gate_exp = jnp.where(routed, jnp.exp(jnp.minimum(logits - largest, 0.0)), 0.0)
+    probs[...] = gate_exp / jnp.sum(gate_exp, axis=-1, keepdims=True)
+
+    def probs_copy(step):
+        return send(
+            probs,
+            probs_all.at[line],
+            (probs_send, probs_recv),
+            (step - 1,),
+            (partners[step], core),
+        )
+
+    for step in range(1, LINES):
+        probs_copy(step).start()
+    own_copies.append(pltpu.make_async_copy(probs, probs_all.at[line], own_sem.at[4]))
+    own_copies.append(pltpu.make_async_copy(mixer, mixer_all.at[line], own_sem.at[5]))
+    for copy in own_copies[4:]:
+        copy.start()
+
+    def pass_on(kind):
+        for axis in (0, 1):
+            direct(kind, axis).wait_recv()
+        for axis in onwards[kind]:
+            onward(kind, axis).start()
+        for slot in (1, 2):
+            to_sibling(kind, slot).start()
+
+    pass_on(0)
+    receive_relay(1, 0)
+    start_relay(1, 1)
+    receive_relay(0, 1)
+    start_relay(0, 2)
+    pass_on(1)
+    pass_on(2)
+    receive_relay(1, 1)
+    start_relay(1, 2)
+    for kind in range(3):
+        for axis in onwards[kind]:
+            onward(kind, axis).wait_recv()
+        to_sibling(kind, 3).start()
+    receive_relay(0, 2)
+    receive_relay(1, 2)
+    for step in range(1, LINES):
+        probs_copy(step).wait()
+    for copy in own_copies:
+        copy.wait()
+    for kind in range(3):
+        for slot in range(PLANE):
+            to_sibling(kind, slot).wait()
+        for axis in (0, 1):
+            direct(kind, axis).wait_send()
+        for axis in onwards[kind]:
+            onward(kind, axis).wait_send()
+    for array in (0, 1):
+        for hop in range(LINES - 1):
+            finish_relay(array, hop)
+
+
+def run_front(operands, weights):
+    low, wide = jnp.bfloat16, jnp.float32
+    shape = jax.ShapeDtypeStruct
+    far = pl.BlockSpec(memory_space=pl.ANY)
+    near = pl.BlockSpec(memory_space=pltpu.VMEM)
+    tokens, width = operands[0].shape
+    half = tokens // 2
+    query_width, key_width = operands[4].shape[1], operands[5].shape[1]
+    span = weights[0].shape[1]
+    tiles = 2 * PLANE
+    dma = pltpu.SemaphoreType.DMA
+    slots = 2 * key_width // HEAD_FEATURES
+    return pl.pallas_call(
+        front_kernel,
+        name="front",
+        out_shape=(
+            shape((tiles, width, span), low),
+            shape((tiles, width, span), low),
+            shape((tiles, span, width), low),
+            shape((LINES, half, width), low),
+            shape((LINES, half, width), low),
+            shape((LINES, half, 128), wide),
+            shape((tokens, width), low),
+            shape((tokens, query_width), low),
+            shape((tokens, key_width), low),
+            shape((tokens, key_width), low),
+            shape((tokens, query_width), low),
+            shape((half, width), low),
+        ),
+        in_specs=[far, far, near, near, far, far, far, far, near, near, near, near] + [far] * 3,
+        out_specs=(far,) * 6 + (near,) * 6,
+        scratch_shapes=[
+            pltpu.VMEM((tokens, width), low),
+            pltpu.VMEM((width, query_width), low),
+            pltpu.VMEM((width, key_width), low),
+            pltpu.VMEM((width, key_width), low),
+            pltpu.VMEM((query_width, width), low),
+            pltpu.VMEM((slots, tokens, 128), low),
+            pltpu.VMEM((slots, tokens, 128), low),
+            pltpu.VMEM((half, width), low),
+            pltpu.VMEM((half, width), low),
+            pltpu.VMEM((half, width), low),
+            pltpu.VMEM((half, 128), wide),
+            dma((5,)),
+            dma((6,)),
+            dma((3, 8)),
+            dma((3, 8)),
+            dma((2, 2, LINES - 1)),
+            dma((2, 2, LINES - 1)),
+            dma((LINES - 1,)),
+            dma((LINES - 1,)),
+            dma((2,)),
+        ],
+        compiler_params=pltpu.CompilerParams(
+            collective_id=2, has_side_effects=True, vmem_limit_bytes=60 << 20
+        ),
+    )(*operands, *weights)
+
+
+def expert_kernel(*refs):
+    tiles = 2 * PLANE
+    refs = list(refs)
+
+    def take(count):
+        taken = refs[:count]
+        del refs[:count]
+        return taken
+
+    mixer_all, cot_all, probs_all, gate_all, up_all, down_all = take(6)
+    out_parts = take(LINES)
+    grow_sum, weighting_sum = take(2)
+    kept = take(3)
+    landed = take(3)
+    mixer, cots, probs, gates, ups, downs = take(6)
+    scaled, ggate, gup, grow, grow_in, outs, weighting, weighting_in = take(8)
+    load_sem, tile_sem, store_sem, kept_sem = take(4)
+    grow_send, grow_recv, weighting_send, weighting_recv = take(4)
+    core_send, core_recv, plane_send, plane_recv, ready_sem = take(5)
+    half, width = mixer_all.shape[1:]
+    rows = LINES * half
+    span = gates.shape[2]
+    column_tiles = width // span
+
+    place = lax.axis_index("ep")
+    core = lax.axis_index("tp")
+    partners = [flip_line(place, step) for step in range(LINES)]
+    barrier = pltpu.get_barrier_semaphore()
+    for step in range(1, LINES):
+        pl.semaphore_signal(
+            barrier, inc=1, device_id=(partners[step], core), device_id_type=MESH
+        )
+    sibling = (place, 1 - core)
+    across = [(flip(place, 1), core), (flip(place, 2), core)]
+    for other in across + [sibling]:
+        pl.semaphore_signal(barrier, inc=1, device_id=other, device_id_type=MESH)
+
+    loads = []
+    for step in range(LINES):
+        part = pl.ds(step * half, half)
+        for kind, (source, target) in enumerate(
+            ((mixer_all, mixer), (cot_all, cots), (probs_all, probs))
+        ):
+            loads.append(
+                pltpu.make_async_copy(source.at[step], target.at[part], load_sem.at[kind, step])
+            )
+    for copy in loads:
+        copy.start()
+    for tile in range(tiles):
+        for kind, (source, target) in enumerate(
+            ((gate_all, gates), (up_all, ups), (down_all, downs))
+        ):
+            pltpu.make_async_copy(source.at[tile], target.at[tile], tile_sem.at[kind, tile]).start()
+    pl.semaphore_wait(barrier, LINES + 2)
+    for copy in loads:
+        copy.wait()
+    weighting[...] = jnp.zeros_like(weighting)
+    line_place = lax.div(place, PLANE)
+    lanes = lax.broadcasted_iota(jnp.int32, (rows, 128), 1)
+
+    def hidden_tile(tile, carry):
+        for kind, (source, target) in enumerate(
+            ((gate_all, gates), (up_all, ups), (down_all, downs))
+        ):
+            pltpu.make_async_copy(source.at[tile], target.at[tile], tile_sem.at[kind, tile]).wait()
+        step = lax.rem(tile, PLANE)
+        owner = lax.rem(place, PLANE)
+        owner = jnp.where(lax.rem(step, 2) == 1, flip(owner, 1), owner)
+        owner = jnp.where(lax.div(step, 2) == 1, flip(owner, 2), owner)
+        chosen = lanes == line_place * PLANE + owner
+        prob = jnp.sum(jnp.where(chosen, probs[...], 0.0), axis=1, keepdims=True)
+        gate_pre = matmul(mixer[...], gates[tile])
+        up_pre = matmul(mixer[...], ups[tile])
+        grad_raw = residual_scale * matmul_nt(cots[...], downs[tile])
+        sigmoid_gate = 1.0 / (1.0 + jnp.exp(-gate_pre))
+        silu_gate = gate_pre * sigmoid_gate
+        active = silu_gate * up_pre
+        share = jnp.sum(active * grad_raw, axis=1, keepdims=True)
+        weighting[...] += jnp.where(chosen, share, 0.0)
+        grad_active = prob * grad_raw
+        scaled[tile] = (prob * active).astype(jnp.bfloat16)
+        ggate[tile] = (
+            grad_active * up_pre * sigmoid_gate * (1.0 + gate_pre * (1.0 - sigmoid_gate))
+        ).astype(jnp.bfloat16)
+        gup[tile] = (grad_active * silu_gate).astype(jnp.bfloat16)
+        return carry
+
+    lax.fori_loop(0, tiles, hidden_tile, 0)
+
+    def rows_for(step):
+        return pl.ds(pl.multiple_of(lax.div(partners[step], PLANE) * half, half), half)
+
+    def weighting_copy(step):
+        return pltpu.make_async_remote_copy(
+            src_ref=weighting.at[rows_for(step)],
+            dst_ref=weighting_in.at[step - 1],
+            send_sem=weighting_send.at[step - 1],
+            recv_sem=weighting_recv.at[step - 1],
+            device_id=(partners[step], core),
+            device_id_type=MESH,
+        )
+
+    def grow_copy(step, column):
+        return pltpu.make_async_remote_copy(
+            src_ref=grow.at[column, rows_for(step)],
+            dst_ref=grow_in.at[step - 1, column],
+            send_sem=grow_send.at[step - 1, column],
+            recv_sem=grow_recv.at[step - 1, column],
+            device_id=(partners[step], core),
+            device_id_type=MESH,
+        )
+
+    for step in range(1, LINES):
+        weighting_copy(step).start()
+
+    def grow_tile(column, carry):
+        here = pl.ds(pl.multiple_of(column * span, span), span)
+        total = matmul_nt(ggate[0], gates[0, here, :])
+        for tile in range(1, tiles):
+            total = total + matmul_nt(ggate[tile], gates[tile, here, :])
+        for tile in range(tiles):
+            total = total + matmul_nt(gup[tile], ups[tile, here, :])
+        grow[column] = total.astype(jnp.bfloat16)
+        for step in range(1, LINES):
+            grow_copy(step, column).start()
+        return carry
+
+    lax.fori_loop(0, column_tiles, grow_tile, 0)
+
+    def out_tile(column, carry):
+        here = pl.ds(pl.multiple_of(column * span, span), span)
+        total = matmul(scaled[0], downs[0, :, here])
+        for tile in range(1, tiles):
+            total = total + matmul(scaled[tile], downs[tile, :, here])
+        outs[:, here] = total.astype(jnp.bfloat16)
+        return carry
+
+    lax.fori_loop(0, column_tiles, out_tile, 0)
+    stores = [
+        pltpu.make_async_copy(
+            outs.at[rows_for(step)], out_parts[step], store_sem.at[step]
+        )
+        for step in range(LINES)
+    ]
+    for copy in stores:
+        copy.start()
+
+    pl.semaphore_signal(ready_sem, inc=1, device_id=sibling, device_id_type=MESH)
+    pl.semaphore_wait(ready_sem, 1)
+    held = (gates, ups, downs)
+
+    def tile_order(index):
+        return jnp.where(index == 0, 3, jnp.where(index == 3, 0, index))
+
+    def tile_grads(tile):
+        yield matmul_tn(mixer[...], ggate[tile])
+        yield matmul_tn(mixer[...], gup[tile])
+        yield residual_scale * matmul_tn(scaled[tile], cots[...])
+
+    def core_copy(kind, step):
+        return pltpu.make_async_remote_copy(
+            src_ref=held[kind].at[PLANE + step],
+            dst_ref=held[kind].at[step],
+            send_sem=core_send.at[kind, step],
+            recv_sem=core_recv.at[kind, step],
+            device_id=sibling,
+            device_id_type=MESH,
+        )
+
+    def sibling_tile(index, carry):
+        step = tile_order(index)
+        for kind, grad in enumerate(tile_grads(PLANE + step)):
+            held[kind][PLANE + step] = grad.astype(jnp.bfloat16)
+            core_copy(kind, step).start()
+        return carry
+
+    lax.fori_loop(0, PLANE, sibling_tile, 0)
+
+    def plane_copy(kind, axis, passing):
+        span_rows = held[kind].shape[1] // 2
+        step = 3 if passing else axis + 1
+        return pltpu.make_async_remote_copy(
+            src_ref=held[kind].at[step, pl.ds(axis * span_rows, span_rows)],
+            dst_ref=landed[kind].at[axis, passing],
+            send_sem=plane_send.at[kind, axis, passing],
+            recv_sem=plane_recv.at[kind, axis, passing],
+            device_id=across[axis],
+            device_id_type=MESH,
+        )
+
+    def kept_copy(kind, step):
+        return pltpu.make_async_copy(
+            held[kind].at[step], kept[kind].at[step], kept_sem.at[kind, step]
+        )
+
+    def own_tile(index, carry):
+        step = tile_order(index)
+        for kind, grad in enumerate(tile_grads(step)):
+            core_copy(kind, step).wait_recv()
+            held[kind][step] = (grad + held[kind][step].astype(jnp.float32)).astype(jnp.bfloat16)
+
+            @pl.when(step == 3)
+            def _():
+                for axis in (0, 1):
+                    plane_copy(kind, axis, 1).start()
+
+            for axis in (0, 1):
+
+                @pl.when(step == axis + 1)
+                def _():
+                    plane_copy(kind, axis, 0).start()
+
+            @pl.when(step < 3)
+            def _():
+                kept_copy(kind, step).start()
+
+        return carry
+
+    lax.fori_loop(0, PLANE, own_tile, 0)
+    for step in range(1, LINES):
+        weighting_copy(step).wait()
+    total = weighting[rows_for(0), :]
+    for step in range(1, LINES):
+        total = total + weighting_in[step - 1]
+    weighting_sum[...] = total
+    for column in range(column_tiles):
+        here = pl.ds(column * span, span)
+        for step in range(1, LINES):
+            grow_copy(step, column).wait()
+        total = grow[column, rows_for(0), :].astype(jnp.float32)
+        for step in range(1, LINES):
+            total = total + grow_in[step - 1, column].astype(jnp.float32)
+        grow_sum[:, here] = total
+    for copy in stores:
+        copy.wait()
+
+    for kind in range(3):
+        for step in range(PLANE):
+            core_copy(kind, step).wait_send()
+        for step in range(3):
+            kept_copy(kind, step).wait()
+        for axis in (0, 1):
+            for passing in (0, 1):
+                plane_copy(kind, axis, passing).wait()
+
+
+def run_experts(mixer_all, cot_all, probs_all, gate_all, up_all, down_all):
+    tiles = 2 * PLANE
+    half, width = mixer_all.shape[1:]
+    span = gate_all.shape[2]
+    rows = LINES * half
+    low, wide = jnp.bfloat16, jnp.float32
+    shape = jax.ShapeDtypeStruct
+    far = pl.BlockSpec(memory_space=pl.ANY)
+    near = pl.BlockSpec(memory_space=pltpu.VMEM)
+    operands = [mixer_all, cot_all, probs_all, gate_all, up_all, down_all]
+    dma = pltpu.SemaphoreType.DMA
+    flops = 18 * rows * width * span * tiles
+    results = pl.pallas_call(
+        expert_kernel,
+        name="experts",
+        out_shape=(
+            *[shape((half, width), low)] * LINES,
+            shape((half, width), wide),
+            shape((half, 128), wide),
+            shape((3, width, span), low),
+            shape((3, width, span), low),
+            shape((3, span, width), low),
+            shape((2, 2, width // 2, span), low),
+            shape((2, 2, width // 2, span), low),
+            shape((2, 2, span // 2, width), low),
+        ),
+        in_specs=[far] * len(operands),
+        out_specs=(*[far] * LINES, near, near, *[far] * 6),
+        scratch_shapes=[
+            pltpu.VMEM((rows, width), low),
+            pltpu.VMEM((rows, width), low),
+            pltpu.VMEM((rows, 128), wide),
+            pltpu.VMEM((tiles, width, span), low),
+            pltpu.VMEM((tiles, width, span), low),
+            pltpu.VMEM((tiles, span, width), low),
+            pltpu.VMEM((tiles, rows, span), low),
+            pltpu.VMEM((tiles, rows, span), low),
+            pltpu.VMEM((tiles, rows, span), low),
+            pltpu.VMEM((width // span, rows, span), low),
+            pltpu.VMEM((LINES - 1, width // span, half, span), low),
+            pltpu.VMEM((rows, width), low),
+            pltpu.VMEM((rows, 128), wide),
+            pltpu.VMEM((LINES - 1, half, 128), wide),
+            dma((3, LINES)),
+            dma((3, tiles)),
+            dma((LINES,)),
+            dma((3, 3)),
+            dma((LINES - 1, width // span)),
+            dma((LINES - 1, width // span)),
+            dma((LINES - 1,)),
+            dma((LINES - 1,)),
+            dma((3, PLANE)),
+            dma((3, PLANE)),
+            dma((3, 2, 2)),
+            dma((3, 2, 2)),
+            pltpu.SemaphoreType.REGULAR,
+        ],
+        compiler_params=pltpu.CompilerParams(
+            collective_id=0, has_side_effects=True, vmem_limit_bytes=63 << 20
+        ),
+        cost_estimate=pl.CostEstimate(
+            flops=flops, bytes_accessed=12 * width * span * tiles, transcendentals=0
+        ),
+    )(*operands)
+    return results
+
+
+def back_kernel(*refs):
+    refs = list(refs)
+
+    def take(count):
+        taken = refs[:count]
+        del refs[:count]
+        return taken
+
+    out_parts = take(LINES)
+    grow_sum, weighting_sum = take(2)
+    kept, landed = take(3), take(3)
+    stream, cotangent, gain_first, gain_second, query_weight, key_weight = take(6)
+    value_weight, out_weight, router, cosine, sine = take(5)
+    mixer_all, probs_all, normed, queries, keys, values, mixed, attended = take(8)
+    layer_out, grad_stream, out_result_a, out_result_b, query_result, rest_result = take(6)
+    expert_grads = take(3)
+    small_out = take(1)[0]
+    stream_v, cot_v, query_v, key_v, value_v, out_v, normed_v, queries_v = take(8)
+    mixed_v, grow_v, attended_v, out_in, layer_v = take(5)
+    key_v2, value_v2, mixer_v, probs_v, weighting_v = take(5)
+    key_slots, value_slots, key_totals, value_totals = take(4)
+    middle_grads, attended_grads, mixed_grads = take(3)
+    key_grads, value_grads, normed_recv = take(3)
+    normed_send, first_terms = attended_grads, layer_v
+    second_terms, query_grads = cot_v, mixed_v
+    own_parts, landed_v, plane_in = take(3), take(3), take(3)
+    out_source_a, out_source_b, query_source, rest_source = take(4)
+    scatter_scratch = [take(5) for _ in range(4)]
+    last_send, last_recv = take(2)
+    load_sem, part_sem, out_send, out_recv, pair_sem, plane_send, plane_recv = take(7)
+    store_sem = take(1)[0]
+    tokens, width = stream_v.shape
+    half = tokens // 2
+
+    place = lax.axis_index("ep")
+    core = lax.axis_index("tp")
+    line = lax.div(place, PLANE)
+    sibling = (place, 1 - core)
+    across = [flip(place, 1), flip(place, 2)]
+    partners = [flip_line(place, step) for step in range(LINES)]
+    bits = [lax.rem(place, 2), lax.rem(lax.div(place, 2), 2)]
+    own_rows = pl.ds(pl.multiple_of(core * half, half), half)
+
+    barrier = pltpu.get_barrier_semaphore()
+    for other in across + partners[1:]:
+        pl.semaphore_signal(barrier, inc=1, device_id=(other, core), device_id_type=MESH)
+    pl.semaphore_signal(barrier, inc=1, device_id=sibling, device_id_type=MESH)
+
+    pairs = [
+        (grow_sum, grow_v),
+        (weighting_sum, weighting_v),
+        (attended, attended_v),
+        (probs_all.at[line], probs_v),
+        (stream, stream_v),
+        (cotangent.at[own_rows], cot_v),
+        (out_weight, out_v),
+        (mixed, mixed_v),
+        (queries, queries_v),
+        (keys, key_v2),
+        (values, value_v2),
+        (normed, normed_v),
+        (query_weight, query_v),
+        (key_weight, key_v),
+        (value_weight, value_v),
+        (mixer_all.at[line], mixer_v),
+        (out_parts[0], mixer_v),
+    ]
+    loads = [
+        pltpu.make_async_copy(source, target, load_sem.at[index])
+        for index, (source, target) in enumerate(pairs)
+    ]
+
+    def part_copies(kind, final):
+        rows = own_parts[kind].shape[1]
+        low, high = pl.ds(0, rows), pl.ds(rows, rows)
+        first, second = (0, 0) if final else (2, 1)
+        return [
+            pltpu.make_async_copy(source, target, part_sem.at[kind, index])
+            for index, (source, target) in enumerate(
+                (
+                    (kept[kind].at[first, low], own_parts[kind].at[0]),
+                    (kept[kind].at[second, high], own_parts[kind].at[1]),
+                )
+            )
+        ]
+
+    def landed_copy(kind):
+        return pltpu.make_async_copy(landed[kind], landed_v[kind], part_sem.at[kind, 2])
+
+    for copy in loads[:6]:
+        copy.start()
+    for kind in range(3):
+        landed_copy(kind).start()
+        for copy in part_copies(kind, False):
+            copy.start()
+    for copy in loads[6:-1]:
+        copy.start()
+    pl.semaphore_wait(barrier, LINES + 2)
+
+    def send(source, target, sems, index, device):
+        return pltpu.make_async_remote_copy(
+            src_ref=source,
+            dst_ref=target,
+            send_sem=sems[0].at[index],
+            recv_sem=sems[1].at[index],
+            device_id=device,
+            device_id_type=MESH,
+        )
+
+    def out_copy(step):
+        return send(
+            out_parts[step],
+            out_in.at[step - 1],
+            (out_send, out_recv),
+            (step - 1,),
+            (partners[step], core),
+        )
+
+    for step in (3, 2, 1):
+        out_copy(step).start()
+
+    for copy in loads[:6]:
+        copy.wait()
+    middle = stream_v[own_rows, :].astype(jnp.float32) + residual_scale * attended_v[...].astype(jnp.float32)
+    inverse = lax.rsqrt(jnp.mean(middle * middle, axis=-1, keepdims=True) + epsilon)
+    probs = probs_v[...]
+    weighting = weighting_v[...]
+    grad_chosen = probs * (weighting - jnp.sum(probs * weighting, axis=-1, keepdims=True))
+    grad_logits = grad_chosen.astype(jnp.bfloat16)
+    grad_mixer = matmul_nt(grad_logits, router[...]) + grow_v[...]
+    weighted = grad_mixer * gain_second[...]
+    grad_middle = (
+        cot_v[...].astype(jnp.float32)
+        + inverse * weighted
+        - middle * (inverse * inverse * inverse)
+        * jnp.mean(middle * weighted, axis=-1, keepdims=True)
+    )
+    middle_grads[own_rows, :] = grad_middle.astype(jnp.bfloat16)
+    second_terms[...] = (grad_mixer * middle * inverse).astype(jnp.bfloat16)
+
+    def pair_copy(source, target, index):
+        return pltpu.make_async_remote_copy(
+            src_ref=source,
+            dst_ref=target,
+            send_sem=pair_sem.at[0, index],
+            recv_sem=pair_sem.at[1, index],
+            device_id=sibling,
+            device_id_type=MESH,
+        )
+
+    middle_copy = pair_copy(middle_grads.at[own_rows], middle_grads.at[own_rows], 0)
+    middle_copy.start()
+
+    def plane_copy(kind, axis):
+        return send(
+            landed_v[kind].at[axis, 1],
+            plane_in[kind].at[axis],
+            (plane_send, plane_recv),
+            (kind, axis),
+            (across[1 - axis], core),
+        )
+
+    for kind in range(3):
+        landed_copy(kind).wait()
+        for copy in part_copies(kind, False):
+            copy.wait()
+        for axis in (0, 1):
+            landed_v[kind][axis, 1] = (
+                own_parts[kind][axis].astype(jnp.float32)
+                + landed_v[kind][axis, 1].astype(jnp.float32)
+            ).astype(jnp.bfloat16)
+            plane_copy(kind, axis).start()
+        for copy in part_copies(kind, True):
+            copy.start()
+
+    slab = out_result_a.shape[0]
+    order = (3, 2, 1, 0)
+    plans = list(
+        zip(
+            (out_source_a, out_source_b, query_source, rest_source),
+            (out_result_a, out_result_b, query_result, rest_result),
+            scatter_scratch,
+        )
+    )
+
+    def rows_of(step, first, second_same, first_same):
+        other_line = lax.div(partners[step], PLANE)
+        first_bit = bits[first] if first_same else 1 - bits[first]
+        second_bit = bits[1 - first] if second_same else 1 - bits[1 - first]
+        index = other_line * PLANE + first_bit * (1 + first) + second_bit * (2 - first)
+        return pl.ds(pl.multiple_of(index * slab, slab), slab)
+
+    def first_copy(number, step, same):
+        source, _, scratch = plans[number]
+        first = number % 2
+        index = step * 2 + same
+        return send(
+            source.at[rows_of(step, first, same, False)],
+            scratch[0].at[index],
+            (scratch[4].at[0], scratch[4].at[1]),
+            (index,),
+            (across[first], core),
+        )
+
+    def second_copy(number, step):
+        scratch = plans[number][2]
+        return send(
+            scratch[1].at[step],
+            scratch[2].at[step],
+            (scratch[4].at[2], scratch[4].at[3]),
+            (step,),
+            (across[1 - number % 2], core),
+        )
+
+    def line_copy(number, step):
+        scratch = plans[number][2]
+        return send(
+            scratch[1].at[step],
+            scratch[3].at[step],
+            (scratch[4].at[4], scratch[4].at[5]),
+            (step,),
+            (partners[step], core),
+        )
+
+    def start_scatter(number):
+        for step in order:
+            for same in (0, 1):
+                first_copy(number, step, same).start()
+
+    def add_first(number, step, same):
+        source, _, scratch = plans[number]
+        first_copy(number, step, same).wait()
+        mine = source[rows_of(step, number % 2, same, True), :].astype(jnp.float32)
+        return mine + scratch[0][step * 2 + same].astype(jnp.float32)
+
+    def finish_first(number, step):
+        plans[number][2][1][step] = add_first(number, step, 0).astype(jnp.bfloat16)
+        second_copy(number, step).start()
+
+    def finish_second(number, step):
+        _, result, scratch = plans[number]
+        total = add_first(number, step, 1)
+        second_copy(number, step).wait()
+        total = total + scratch[2][step].astype(jnp.float32)
+        if step:
+            scratch[1][step] = total.astype(jnp.bfloat16)
+            line_copy(number, step).start()
+        else:
+            result[...] = total
+
+    def finish_line(number):
+        _, result, scratch = plans[number]
+        for step in order[:-1]:
+            line_copy(number, step).wait()
+            result[...] += scratch[3][step].astype(jnp.float32)
+
+    middle_copy.wait()
+    attended_grads[...] = (residual_scale * middle_grads[...].astype(jnp.float32)).astype(
+        jnp.bfloat16
+    )
+    loads[6].wait()
+    loads[7].wait()
+    columns = out_source_a.shape[1]
+    out_source_a[...] = matmul_tn(attended_grads[...], mixed_v[:, :columns]).astype(jnp.bfloat16)
+    start_scatter(0)
+    out_source_b[...] = matmul_tn(attended_grads[...], mixed_v[:, columns:]).astype(jnp.bfloat16)
+    start_scatter(1)
+    mixed_grads[...] = matmul_nt(attended_grads[...], out_v[...]).astype(jnp.bfloat16)
+    for copy in loads[8:11]:
+        copy.wait()
+    store_slots(key_slots, key_v2[...].astype(jnp.float32))
+    store_slots(value_slots, value_v2[...].astype(jnp.float32))
+    key_totals[...] = jnp.zeros_like(key_totals)
+    value_totals[...] = jnp.zeros_like(value_totals)
+    group = query_v.shape[1] // key_v.shape[1]
+    blocks = 2
+    block_rows = tokens // blocks
+
+    def turned_back(value, cosines, sines):
+        return (value * cosines - partner_lanes(value) * sines).astype(jnp.bfloat16)
+
+    def head_pair(pair, carry):
+        here = pl.ds(pl.multiple_of(pair * 128, 128), 128)
+        for block in range(blocks):
+            rows = slice(block * block_rows, (block + 1) * block_rows)
+            reach = (block + 1) * block_rows
+            total = jnp.zeros((block_rows, 128), jnp.float32)
+            query_block = queries_v[rows, here]
+            grad_block = mixed_grads[rows, here]
+            for parity in range(2):
+                slot = 2 * lax.div(2 * pair + parity, group) + parity
+                key_block = key_slots[slot, :reach, :]
+                scores = causal_scores(query_block, key_block, block * block_rows)
+                weight = jnp.exp(scores - jnp.max(scores, axis=-1, keepdims=True))
+                weight = weight / jnp.sum(weight, axis=-1, keepdims=True)
+                grad_probs = matmul_nt(grad_block, value_slots[slot, :reach, :])
+                inner = jnp.sum(weight * grad_probs, axis=-1, keepdims=True)
+                grad_scores = (weight * (grad_probs - inner)).astype(jnp.bfloat16)
+                total = total + matmul(grad_scores, key_block)
+                key_totals[slot, :reach, :] += matmul_tn(grad_scores, query_block)
+                value_totals[slot, :reach, :] += matmul_tn(
+                    weight.astype(jnp.bfloat16), grad_block
+                )
+            query_grads[rows, here] = turned_back(
+                score_scale * total, cosine[rows, :128], sine[rows, :128]
+            )
+        return carry
+
+    lax.fori_loop(0, query_v.shape[1] // 128, head_pair, 0)
+
+    def gathered_pairs(totals):
+        found = []
+        for pair in range(key_v.shape[1] // 128):
+            first, second = 4 * pair, 4 * pair + 2
+            low = lane_halves(totals[first])[0] + pltpu.roll(
+                lane_halves(totals[first + 1])[1], HEAD_FEATURES, 1
+            )
+            high = lane_halves(totals[second + 1])[1] + pltpu.roll(
+                lane_halves(totals[second])[0], HEAD_FEATURES, 1
+            )
+            found.append(low + high)
+        return jnp.concatenate(found, axis=1)
+
+    key_grads[...] = turned_back(
+        score_scale * gathered_pairs(key_totals), cosine[...], sine[...]
+    )
+    value_grads[...] = gathered_pairs(value_totals).astype(jnp.bfloat16)
+    for copy in loads[11:-1]:
+        copy.wait()
+    query_source[...] = matmul_tn(normed_v[...], query_grads[...]).astype(jnp.bfloat16)
+    start_scatter(2)
+    normed_send[...] = (
+        matmul_nt(query_grads[...], query_v[...])
+        + matmul_nt(key_grads[...], key_v[...])
+        + matmul_nt(value_grads[...], value_v[...])
+    ).astype(jnp.bfloat16)
+    normed_copy = pair_copy(normed_send, normed_recv, 1)
+    normed_copy.start()
+    key_width = key_grads.shape[1]
+    rest_source[:, :key_width] = matmul_tn(normed_v[...], key_grads[...]).astype(jnp.bfloat16)
+    rest_source[:, key_width : 2 * key_width] = matmul_tn(
+        normed_v[...], value_grads[...]
+    ).astype(jnp.bfloat16)
+    for step in order:
+        finish_first(0, step)
+        finish_first(1, step)
+    normed_copy.wait()
+
+    def stream_rows(rows):
+        grad_normed = normed_send[rows, :].astype(jnp.float32) + normed_recv[rows, :].astype(
+            jnp.float32
+        )
+        stream_f = stream_v[rows, :].astype(jnp.float32)
+        inverse = lax.rsqrt(jnp.mean(stream_f * stream_f, axis=-1, keepdims=True) + epsilon)
+        weighted = grad_normed * gain_first[...]
+        total = (
+            middle_grads[rows, :].astype(jnp.float32)
+            + inverse * weighted
+            - stream_f * (inverse * inverse * inverse)
+            * jnp.mean(stream_f * weighted, axis=-1, keepdims=True)
+        )
+        return grad_normed * stream_f * inverse, total
+
+    first_terms[...] = stream_rows(own_rows)[0].astype(jnp.bfloat16)
+    lane = lax.broadcasted_iota(jnp.int32, (half, 128), 1)
+    experts = LINES * PLANE
+    rest_source[:, 2 * key_width :] = (
+        matmul_tn(mixer_v[...], grad_logits)
+        + matmul_tn(second_terms[...], (lane == experts).astype(jnp.bfloat16))
+        + matmul_tn(first_terms[...], (lane == experts + 1).astype(jnp.bfloat16))
+    ).astype(jnp.bfloat16)
+    loads[-1].start()
+    start_scatter(3)
+    for position in range(2):
+        rows = slice(position * half, position * half + half)
+        normed_recv[rows, :] = stream_rows(rows)[1].astype(jnp.bfloat16)
+    stream_copy = pltpu.make_async_copy(normed_recv, grad_stream, store_sem.at[4])
+    stream_copy.start()
+    for step in order:
+        finish_second(0, step)
+        finish_second(1, step)
+    for step in order:
+        finish_first(2, step)
+        finish_first(3, step)
+    for step in (1, 2, 3):
+        out_copy(step).wait()
+    loads[-1].wait()
+    mixture = mixer_v[...].astype(jnp.float32)
+    for step in range(1, LINES):
+        mixture = mixture + out_in[step - 1].astype(jnp.float32)
+    middle = stream_v[own_rows, :].astype(jnp.float32) + residual_scale * attended_v[...].astype(jnp.float32)
+    result = middle + residual_scale * mixture
+    layer_v[...] = result.astype(jnp.bfloat16)
+    layer_pair = pair_copy(layer_v, layer_out.at[own_rows], 2)
+    layer_pair.start()
+    layer_own = pltpu.make_async_copy(layer_v, layer_out.at[own_rows], store_sem.at[0])
+    layer_own.start()
+    row_lane = lax.broadcasted_iota(jnp.int32, (8, 128), 1)
+    squares = jnp.zeros((8, 128), jnp.float32)
+    for index, value in enumerate((result, attended_v[...].astype(jnp.float32), mixture)):
+        total = jnp.sum(jnp.sum(value * value, axis=1, keepdims=True), axis=0, keepdims=True)
+        squares = jnp.where(row_lane == index, total, squares)
+    for step in order:
+        finish_second(2, step)
+        finish_second(3, step)
+    def expert_copy(kind):
+        return pltpu.make_async_copy(own_parts[kind], expert_grads[kind], store_sem.at[1 + kind])
+
+    for kind in range(3):
+        for copy in part_copies(kind, True):
+            copy.wait()
+        for axis in (0, 1):
+            plane_copy(kind, axis).wait()
+            own_parts[kind][axis] = (
+                own_parts[kind][axis].astype(jnp.float32)
+                + landed_v[kind][axis, 0].astype(jnp.float32)
+                + plane_in[kind][axis].astype(jnp.float32)
+            ).astype(jnp.bfloat16)
+        expert_copy(kind).start()
+    finish_line(3)
+    last_send[:slab, :] = rest_result[:, 2 * key_width :]
+    last_send[slab:, :] = squares
+    last_copy = pair_copy(last_send, last_recv, 3)
+    last_copy.start()
+    for number in range(3):
+        finish_line(number)
+    last_copy.wait()
+    small_out[...] = last_send[...] + last_recv[...]
+    layer_pair.wait()
+    layer_own.wait()
+    stream_copy.wait()
+    for kind in range(3):
+        expert_copy(kind).wait()
+
+
+def run_back(expert_results, operands, front_results):
+    low, wide = jnp.bfloat16, jnp.float32
+    shape = jax.ShapeDtypeStruct
+    vmem = pltpu.VMEM
+    far = pl.BlockSpec(memory_space=pl.ANY)
+    near = pl.BlockSpec(memory_space=pltpu.VMEM)
+    tokens, width = operands[0].shape
+    half = tokens // 2
+    query_width, key_width = operands[4].shape[1], operands[5].shape[1]
+    kept = expert_results[LINES + 2 : LINES + 5]
+    tile_shapes = [value.shape[1:] for value in kept]
+    half_shapes = [(value[0] // 2, value[1]) for value in tile_shapes]
+    slab = width // (LINES * PLANE)
+    slots = 2 * key_width // HEAD_FEATURES
+    rest_width = 2 * key_width + 128
+    widths = (query_width // 2, query_width // 2, query_width, rest_width)
+    dma = pltpu.SemaphoreType.DMA
+    scatter_scratch = []
+    for columns in widths:
+        scatter_scratch += [
+            vmem((2 * LINES, slab, columns), low),
+            vmem((LINES, slab, columns), low),
+            vmem((LINES, slab, columns), low),
+            vmem((LINES, slab, columns), low),
+            dma((6, 2 * LINES)),
+        ]
+    return pl.pallas_call(
+        back_kernel,
+        name="back",
+        out_shape=(
+            shape((tokens, width), low),
+            shape((tokens, width), low),
+            *[shape((slab, columns), wide) for columns in widths],
+            *[shape((2, *value), low) for value in half_shapes],
+            shape((slab + 8, 128), wide),
+        ),
+        in_specs=[far] * (LINES + 8)
+        + [far, far, near, near, far, far, far, far, near, near, near]
+        + [far] * 8,
+        out_specs=(far,) * 2 + (near,) * 4 + (far,) * 3 + (near,),
+        scratch_shapes=[
+            vmem((tokens, width), low),
+            vmem((half, width), low),
+            vmem((width, query_width), low),
+            vmem((width, key_width), low),
+            vmem((width, key_width), low),
+            vmem((query_width, width), low),
+            vmem((tokens, width), low),
+            vmem((tokens, query_width), low),
+            vmem((tokens, query_width), low),
+            vmem((half, width), wide),
+            vmem((half, width), low),
+            vmem((LINES - 1, half, width), low),
+            vmem((half, width), low),
+            vmem((tokens, key_width), low),
+            vmem((tokens, key_width), low),
+            vmem((half, width), low),
+            vmem((half, 128), wide),
+            vmem((half, 128), wide),
+            vmem((slots, tokens, 128), low),
+            vmem((slots, tokens, 128), low),
+            vmem((slots, tokens, 128), wide),
+            vmem((slots, tokens, 128), wide),
+            vmem((tokens, width), low),
+            vmem((tokens, width), low),
+            vmem((tokens, query_width), low),
+            vmem((tokens, key_width), low),
+            vmem((tokens, key_width), low),
+            vmem((tokens, width), low),
+            *[vmem((2, *value), low) for value in half_shapes],
+            *[vmem((2, 2, *value), low) for value in half_shapes],
+            *[vmem((2, *value), low) for value in half_shapes],
+            *[vmem((width, columns), low) for columns in widths],
+            *scatter_scratch,
+            vmem((slab + 8, 128), wide),
+            vmem((slab + 8, 128), wide),
+            dma((17,)),
+            dma((3, 3)),
+            dma((LINES - 1,)),
+            dma((LINES - 1,)),
+            dma((2, 4)),
+            dma((3, 2)),
+            dma((3, 2)),
+            dma((5,)),
+        ],
+        compiler_params=pltpu.CompilerParams(
+            collective_id=1, has_side_effects=True, vmem_limit_bytes=63 << 20
+        ),
+    )(*expert_results, *operands, *front_results)
+
+
+def dense_shards(
+    stream,
+    cotangent,
+    attention_gain,
+    query_weight,
+    key_matrix,
+    value_matrix,
+    out_weight,
+    mixture_gain,
+    router_weight,
+    gate_weight,
+    up_weight,
+    down_weight,
+    routes,
+):
+    tok_rows, model_width = stream.shape
+    experts = router_weight.shape[1]
+    query_width = query_weight.shape[1]
+    key_width = key_matrix.shape[1]
+    cosine_rows, sine_rows = rope_tables(SEQ_LEN)
+    operands = [
+        stream,
+        cotangent,
+        attention_gain.astype(jnp.float32)[None, :],
+        mixture_gain.astype(jnp.float32)[None, :],
+        query_weight,
+        key_matrix,
+        value_matrix,
+        out_weight,
+        jnp.pad(router_weight, ((0, 0), (0, 128 - experts))),
+        routes,
+        jnp.tile(cosine_rows, (1, 8)),
+        jnp.tile(jnp.concatenate([-sine_rows, sine_rows], axis=1), (1, 4)),
+    ]
+    front = run_front(operands, [gate_weight[0], up_weight[0], down_weight[0]])
+    gate_all, up_all, down_all, mixer_all, cot_all, probs_all = front[:6]
+    expert_results = run_experts(mixer_all, cot_all, probs_all, gate_all, up_all, down_all)
+    (
+        layer_out,
+        grad_stream,
+        out_first,
+        out_second,
+        query_grad,
+        rest_grad,
+        gate_grad,
+        up_grad,
+        down_grad,
+        small,
+    ) = run_back(expert_results, operands[:9] + operands[10:], [mixer_all, *front[5:]])
+    slab = query_grad.shape[0]
+    rms_stats = jnp.sqrt(small[slab : slab + 1, :3] / (tok_rows * model_width))
+    return (
+        layer_out,
+        grad_stream.astype(jnp.float32),
+        small[:slab, experts + 1],
+        query_grad,
+        rest_grad[:, :key_width],
+        rest_grad[:, key_width : 2 * key_width],
+        jnp.concatenate([out_first, out_second], axis=1).T,
+        small[:slab, experts],
+        small[:slab, :experts],
+        gate_grad.astype(jnp.float32).reshape(gate_weight.shape),
+        up_grad.astype(jnp.float32).reshape(up_weight.shape),
+        down_grad.astype(jnp.float32).reshape(down_weight.shape),
+        rms_stats,
+    )
+
+
 def solution(mesh):
     in_specs = (
         P("ep", None),
@@ -380,4 +1696,7 @@
         P("ep", "tp", None),
         P("ep", None),
     )
+    ep_size = mesh.shape["ep"]
+    dense = mesh.shape["tp"] == 2 and ep_size <= 2 * TOP and ep_size == 16
+    shards = dense_shards if dense else routed_shards
     return jax.shard_map(shards, mesh=mesh, in_specs=in_specs, out_specs=out_specs, check_vma=False)

time: 2250 us -> 391 us (0.17)
  waiting for transfers between devices: 851 us -> 0 us
  blocking collectives: 792 us -> 0 us
  Pallas kernels: 0 us -> 364 us
  local copies, waits for them, and re-layouts: 307 us -> 13.9 us
  matrix products: 161 us -> 0 us
  other arithmetic: 111 us -> 8.74 us
    all_to_all x3 -> x0, blocking collectives: 714 us -> none  [the longest x2 365 us: back_to_tokens(): lax.all_to_all(rows_low, 'ep', split_axis=1, concat_axis=1, tiled=True)]
    reduce_scatter x6 -> x0, waiting for transfers between devices: 511 us -> none  [the longest x1 143 us: shards(): lax.psum_scatter(query_grad, 'ep', scatter_dimension=0, tiled=True)]
    pallas_call x0 -> x3, Pallas kernels: none -> 364 us  [the longest x1 130 us: run_experts(): pl.pallas_call(expert_kernel, name='experts', out_shape=(*[shape((half, w...]
    all_to_all x1 -> x0, waiting for transfers between devices: 255 us -> none  [to_owners(): return lax.all_to_all(packed, 'ep', split_axis=1, concat_axis=1, tiled=True)]
    gather x5 -> x0, local copies, waits for them, and re-layouts: 164 us -> none  [the longest x1 35.8 us: shards(): grad_mix[source_token]]
    dot_general x29 -> x0, matrix products: 158 us -> none  [the longest x1 18.1 us: input_term(): jnp.dot(grad_up_pre, up_matrix.T, preferred_element_type=jnp.float32)]
    unnamed x1 -> x0, blocking collectives: 77.5 us -> none
    all_to_all x4 -> x0, local copies, waits for them, and re-layouts: 68.6 us -> none  [the longest x2 47.2 us: to_owners(): return lax.all_to_all(packed, 'ep', split_axis=1, concat_axis=1, tiled=True)]
  transfers between devices with their start and end apart: 12 -> 0, of which waited for: 8 -> 0; matrix products, arithmetic and copies ran while one was open for 14% -> 0% of each run, Pallas kernels for 0% -> 0%
where the time goes in v3:
time: 391 us; the launch traced here: 387 us
  Pallas kernels  364 us (93%)
  local copies, waits for them, and re-layouts  13.9 us (4%)
  other arithmetic  8.74 us (2%)
    pallas_call x1, Pallas kernels, run_experts(): pl.pallas_call(expert_kernel, name='experts', out_shape=(*[shape((half, w...  130 us
    pallas_call x1, Pallas kernels, run_front(): pl.pallas_call(front_kernel, name='front', out_shape=(shape((tiles, width...  122 us
    pallas_call x1, Pallas kernels, run_back(): pl.pallas_call(back_kernel, name='back', out_shape=(shape((tokens, width)...  112 us

profile of v3, /device:TPU:0, one launch (start us, length us, event | category | flops | bytes accessed | tf_op | source)
XLA Modules:
  0.0 387.4 jit_solution(3442291599187308884)
XLA Ops:
  0.7 1.3 reshape.96.refs_2_.refs_14_
  2.0 1.3 reshape.97.refs_3_.refs_15_
  3.2 0.3 fusion
  3.6 1.6 copy.30.refs_9_
  5.2 1.0 copy.32.refs_11_.refs_22_
  6.2 0.2 copy.29
  6.4 0.8 pad.4.refs_8_.refs_20_
  7.3 1.0 copy.31.refs_10_.refs_21_
  8.3 121.9 %front.1 = (bf16[8,1536,256]{2,1,0:T(8,128)(2,1)}, bf16[8,1536,256]{2,1,0:T(8,128)(2,1)}, bf16[8,256,1536]{2,1,0:T(8,128)(2,1)}, bf16[4,256,1536]{2,1,0:T(8,128)...) custom-call(bf16[512,1536]{1,0:T(8,128)(2,1)} %refs_12_.1, ...), custom_call_target="tpu_custom_call" | custom-call | tf_op jit(solution)/shard_map/front/pallas_call | solution.py:714
  130.2 129.6 %experts.1 = (bf16[256,1536]{1,0:T(8,128)(2,1)}, bf16[256,1536]{1,0:T(8,128)(2,1)}, bf16[256,1536]{1,0:T(8,128)(2,1)}, bf16[256,1536]{1,0:T(8,128)(2,1)}, f32[25...) custom-call(bf16[4,256,1536]{2,1,0:T(8,128)(2,1)} %get-tuple-element, ...), custom_call_target="tpu_custom_call" | custom-call | flops 57982058496 | bytes 37748736 | tf_op jit(solution)/shard_map/experts/pallas_call | solution.py:1019
  259.8 112.4 %back.1 = (bf16[512,1536]{1,0:T(8,128)(2,1)}, bf16[512,1536]{1,0:T(8,128)(2,1)}, f32[96,384]{1,0:T(8,128)}, f32[96,384]{1,0:T(8,128)}, f32[96,768]{1,0:T(8,128)}...) custom-call(bf16[256,1536]{1,0:T(8,128)(2,1)} %get-tuple-element.53., ...), custom_call_target="tpu_custom_call" | custom-call | tf_op jit(solution)/shard_map/back/pallas_call | solution.py:1535
  372.2 1.3 multiply_sqrt_fusion
  373.5 1.6 slice_reduce_fusion
  375.1 0.8 slice.22
  375.9 0.7 copy.35
  376.5 1.6 fusion.1
  378.2 1.8 maximum_bitcast_fusion
  380.0 0.0 copy-done.4
  380.0 1.3 bitcast_convert_fusion
  381.3 2.1 convert_element_type.38
  383.4 1.9 bitcast_convert_fusion.1
  385.3 0.0 copy-done
  385.3 1.1 copy.38
  386.5 0.7 copy.39
  (17 shorter events, 0.1 us)
Async XLA Ops:
  0.6 5.5 %copy-start.6 = (bf16[1536,16]{0,1:T(8,128)(2,1)S(1)}, bf16[1536,16]{0,1:T(8,128)(2,1)}, u32[]{:S(2)}) copy-start(bf16[1536,16]{0,1:T(8,128)(2,1)} %param.21) | copy-start | bytes 147460
  372.2 7.8 %copy-start.4 = (bf16[2,128,1536]{2,1,0:T(8,128)(2,1)S(1)}, bf16[2,128,1536]{2,1,0:T(8,128)(2,1)}, u32[]{:S(2)}) copy-start(bf16[2,128,1536]{2,1,0:T(8,128)(2,1)} %get-tuple-element.80) | copy-start | bytes 2359300
  378.2 3.2 copy-start.1
  381.3 2.1 copy-start.2
  381.3 2.1 copy-start.3
  383.4 1.9 copy-start
  385.3 1.1 copy-start.5

commit v4 on v3

--- a/solution.py
+++ b/solution.py
@@ -2,6 +2,7 @@
 
 import jax
 import jax.numpy as jnp
+import numpy as np
 from jax import lax
 from jax.experimental import pallas as pl
 from jax.experimental.pallas import tpu as pltpu
@@ -422,6 +423,7 @@
 
 
 def front_kernel(*refs):
+    tiles = 2 * PLANE
     refs = list(refs)
 
     def take(count):
@@ -432,42 +434,72 @@
     stream, cotangent, gain_first, gain_second, query_weight, key_weight = take(6)
     value_weight, out_weight, router, routes, cosine, sine = take(6)
     weights = take(3)
-    weights_all = take(3)
-    mixer_all, cot_all, probs_all = take(3)
-    normed, queries, keys, values, mixed, attended = take(6)
-    stream_v, query_v, key_v, value_v, out_v = take(5)
-    key_slots, value_slots, part_send, part_recv, mixer, probs = take(6)
+    out_parts = take(LINES)
+    grow_sum, weighting_sum = take(2)
+    kept = take(3)
+    landed = take(3)
+    mixer_own, probs_own, normed_out, queries_out, keys_out, values_out, mixed_out = take(7)
+    attended = take(1)[0]
+    mixer, cots, probs, gates, ups, downs = take(6)
+    scaled, ggate, gup, grow, grow_in, outs, weighting, weighting_in = take(8)
+    part_send, part_recv = take(2)
     load_sem, own_sem, weight_send, weight_recv = take(4)
     relay_send, relay_recv, probs_send, probs_recv, part_sem = take(5)
-    tokens, width = stream_v.shape
-    half = tokens // 2
+    result_sem, store_sem, kept_sem = take(3)
+    grow_send, grow_recv, weighting_send, weighting_recv = take(4)
+    core_send, core_recv, plane_send, plane_recv, ready_sem = take(5)
+    held = (gates, ups, downs)
+    rows_all, width = mixer.shape
+    half = rows_all // LINES
+    tokens = 2 * half
+    span = gates.shape[2]
+    column_tiles = width // span
+    heads_width = query_weight.shape[1]
+    pieces = heads_width // span
+    tall = scaled.shape[1]
 
     place = lax.axis_index("ep")
     core = lax.axis_index("tp")
     line = lax.div(place, PLANE)
-    across = [flip(place, 1), flip(place, 2)]
-    partners = [flip_line(place, step) for step in range(LINES)]
+    sibling = (place, 1 - core)
+    across = [(flip(place, 1), core), (flip(place, 2), core)]
+    partners = [(flip_line(place, step), core) for step in range(LINES)]
     own_rows = pl.ds(pl.multiple_of(core * half, half), half)
-    other_rows = pl.ds(pl.multiple_of((1 - core) * half, half), half)
+    stream_v, normed = outs.at[pl.ds(0, tokens)], outs.at[pl.ds(tokens, tokens)]
+
+    def block_rows_of(block):
+        return pl.ds(pl.multiple_of(block * half, half), half)
+
+    line_rows = block_rows_of(line)
 
     barrier = pltpu.get_barrier_semaphore()
-    for other in across + partners[1:]:
-        pl.semaphore_signal(barrier, inc=1, device_id=(other, core), device_id_type=MESH)
-    pl.semaphore_signal(barrier, inc=1, device_id=(place, 1 - core), device_id_type=MESH)
-
-    loads = [
-        pltpu.make_async_copy(source, target, load_sem.at[index])
-        for index, (source, target) in enumerate(
-            (
-                (stream, stream_v),
-                (query_weight, query_v),
-                (key_weight, key_v),
-                (value_weight, value_v),
-                (out_weight, out_v),
+    for other in across + partners[1:] + [sibling]:
+        pl.semaphore_signal(barrier, inc=1, device_id=other, device_id_type=MESH)
+
+    def tall_loads(source, column, target, tile, index):
+        return [
+            pltpu.make_async_copy(
+                source.at[pl.ds(start, size), pl.ds(column * span, span)],
+                target.at[tile + part, pl.ds(0, size)],
+                load_sem.at[index + part],
             )
-        )
+            for part, (start, size) in enumerate(((0, tall), (tall, width - tall)))
+        ]
+
+    loads = [pltpu.make_async_copy(stream, stream_v, load_sem.at[0])]
+    for piece in range(pieces):
+        loads += tall_loads(query_weight, piece, scaled, 2 * piece, 1 + 2 * piece)
+    loads += tall_loads(key_weight, 0, ggate, 0, 1 + 2 * pieces)
+    loads += tall_loads(value_weight, 0, ggate, tiles - 2, 3 + 2 * pieces)
+    out_loads = [
+        pltpu.make_async_copy(
+            out_weight.at[:, pl.ds(column * span, span)],
+            grow.at[column, pl.ds(0, heads_width)],
+            load_sem.at[5 + 2 * pieces + column],
+        )
+        for column in range(column_tiles)
     ]
-    for copy in loads:
+    for copy in loads + out_loads:
         copy.start()
     pl.semaphore_wait(barrier, LINES + 2)
 
@@ -481,40 +513,33 @@
             device_id_type=MESH,
         )
 
-    sibling = (place, 1 - core)
-    sems = (weight_send, weight_recv)
+    weight_sems = (weight_send, weight_recv)
 
     def direct(kind, axis):
         return send(
-            weights[kind],
-            weights_all[kind].at[axis + 1],
-            sems,
-            (kind, axis),
-            (across[axis], core),
+            weights[kind], held[kind].at[axis + 1], weight_sems, (kind, axis), across[axis]
         )
 
     def to_sibling(kind, slot):
-        source = weights[kind] if slot == 0 else weights_all[kind].at[slot]
-        return send(source, weights_all[kind].at[PLANE + slot], sems, (kind, 2 + slot), sibling)
+        source = weights[kind] if slot == 0 else held[kind].at[slot]
+        return send(source, held[kind].at[PLANE + slot], weight_sems, (kind, 2 + slot), sibling)
 
     def onward(kind, axis):
-        gathered = weights_all[kind]
-        source, target = gathered.at[2 - axis], gathered.at[3]
+        source, target = held[kind].at[2 - axis], held[kind].at[3]
         if kind == 1:
             part = pl.ds(axis * (width // 2), width // 2)
-            source, target = gathered.at[2 - axis, part], gathered.at[3, part]
-        return send(source, target, sems, (kind, 6 + axis), (across[axis], core))
+            source, target = held[kind].at[2 - axis, part], held[kind].at[3, part]
+        return send(source, target, weight_sems, (kind, 6 + axis), across[axis])
 
     onwards = {0: (0,), 1: (0, 1), 2: (1,)}
 
     def relay(array, hop, downward):
-        gathered = (cot_all, mixer_all)[array]
+        gathered = (cots, mixer)[array]
         shift = -1 if downward else 1
-        block = jnp.clip(line - shift * hop, 0, LINES - 1)
-        if hop == 0:
-            source = mixer if array else cotangent.at[own_rows]
-        else:
-            source = gathered.at[block]
+        block = block_rows_of(jnp.clip(line - shift * hop, 0, LINES - 1))
+        source = gathered.at[block]
+        if hop == 0 and array == 0:
+            source = cotangent.at[own_rows]
         return send(
             source,
             gathered.at[block],
@@ -523,6 +548,18 @@
             (place + shift * PLANE, core),
         )
 
+    def arriving(array, hop, downward):
+        gathered = (cots, mixer)[array]
+        shift = -1 if downward else 1
+        block = block_rows_of(jnp.clip(line - shift * (hop + 1), 0, LINES - 1))
+        return send(
+            gathered.at[block],
+            gathered.at[block],
+            (relay_send, relay_recv),
+            (array, downward, hop),
+            (place + shift * PLANE, core),
+        )
+
     def relay_sends(hop, downward):
         if downward:
             return jnp.logical_and(line > 0, line + hop < LINES)
@@ -545,7 +582,7 @@
 
             @pl.when(relay_receives(hop, downward))
             def _():
-                relay(array, hop, downward).wait_recv()
+                arriving(array, hop, downward).wait_recv()
 
     def finish_relay(array, hop):
         for downward in (0, 1):
@@ -559,65 +596,128 @@
             direct(kind, axis).start()
     start_relay(0, 0)
     own_copies = [
-        pltpu.make_async_copy(weights[kind], weights_all[kind].at[0], own_sem.at[kind])
+        pltpu.make_async_copy(weights[kind], held[kind].at[0], own_sem.at[kind])
         for kind in range(3)
     ]
     own_copies.append(
-        pltpu.make_async_copy(cotangent.at[own_rows], cot_all.at[line], own_sem.at[3])
+        pltpu.make_async_copy(cotangent.at[own_rows], cots.at[line_rows], own_sem.at[3])
     )
     for kind in range(3):
         to_sibling(kind, 0).start()
     for copy in own_copies:
         copy.start()
+    weighting[...] = jnp.zeros_like(weighting)
 
     loads[0].wait()
     stream_f = stream_v[...].astype(jnp.float32)
     inverse = lax.rsqrt(jnp.mean(stream_f * stream_f, axis=-1, keepdims=True) + epsilon)
     normed[...] = (stream_f * inverse * gain_first[...]).astype(jnp.bfloat16)
-    for copy in loads[1:4]:
+    for copy in loads[1:]:
         copy.wait()
-    span = cosine.shape[1]
+
+    def projected(target, tile):
+        return matmul(normed[:, :tall], target[tile]) + matmul(
+            normed[:, tall:], target[tile + 1, : width - tall, :]
+        )
 
     def rotated(pre):
-        return pre * cosine[...] + partner_lanes(pre) * sine[...]
-
-    for start in range(0, query_v.shape[1], span):
-        here = slice(start, start + span)
-        queries[:, here] = rotated(matmul(normed[...], query_v[:, here])).astype(jnp.bfloat16)
-    key_rows = rotated(matmul(normed[...], key_v[...])).astype(jnp.bfloat16)
-    keys[...] = key_rows
-    store_slots(key_slots, key_rows.astype(jnp.float32))
-    value_rows = matmul(normed[...], value_v[...]).astype(jnp.bfloat16)
-    values[...] = value_rows
-    store_slots(value_slots, value_rows.astype(jnp.float32))
-    group = query_v.shape[1] // key_v.shape[1]
+        turned = []
+        for pair in range(span // 128):
+            part = pre[:, pair * 128 : pair * 128 + 128]
+            turned.append(part * cosine[...] + partner_lanes(part) * sine[...])
+        return jnp.concatenate(turned, axis=1).astype(jnp.bfloat16)
+
+    low_rows, high_rows = pl.ds(0, tokens), pl.ds(tokens, tokens)
+    for piece in range(pieces):
+        ggate[3 + piece, low_rows, :] = rotated(projected(scaled, 2 * piece))
+    key_rows = rotated(projected(ggate, 0))
+    ggate[2, low_rows, :] = key_rows
+    value_rows = projected(ggate, tiles - 2).astype(jnp.bfloat16)
+    ggate[2, high_rows, :] = value_rows
+
+    def store_overlaid(values, rows):
+        for group in range(values.shape[1] // HEAD_FEATURES):
+            pair = group // 2
+            low, high = lane_halves(values[:, pair * 128 : pair * 128 + 128].astype(jnp.float32))
+            if group % 2:
+                low = pltpu.roll(high, HEAD_FEATURES, 1)
+            else:
+                high = pltpu.roll(low, HEAD_FEATURES, 1)
+            gup[2 * group, rows, :128] = low.astype(jnp.bfloat16)
+            gup[2 * group + 1, rows, :128] = high.astype(jnp.bfloat16)
+
+    store_overlaid(key_rows, low_rows)
+    store_overlaid(value_rows, high_rows)
+    results = [
+        pltpu.make_async_copy(normed, normed_out, result_sem.at[0]),
+        pltpu.make_async_copy(ggate.at[2, low_rows], keys_out, result_sem.at[1]),
+        pltpu.make_async_copy(ggate.at[2, high_rows], values_out, result_sem.at[2]),
+    ]
+    for piece in range(pieces):
+        results.append(
+            pltpu.make_async_copy(
+                ggate.at[3 + piece, low_rows],
+                queries_out.at[:, pl.ds(piece * span, span)],
+                result_sem.at[3 + piece],
+            )
+        )
+    for copy in results:
+        copy.start()
+    group = heads_width // key_weight.shape[1]
     blocks = 2
     block_rows = tokens // blocks
 
     def head_pair(pair, carry):
-        here = pl.ds(pl.multiple_of(pair * 128, 128), 128)
+        tile = 3 + lax.div(pair, 2)
+        here = pl.ds(pl.multiple_of(lax.rem(pair, 2) * 128, 128), 128)
         for block in range(blocks):
-            rows = slice(block * block_rows, (block + 1) * block_rows)
-            reach = (block + 1) * block_rows
+            start = block * block_rows
+            reach = start + block_rows
             total = jnp.zeros((block_rows, 128), jnp.float32)
+            query_block = ggate[tile, pl.ds(start, block_rows), here]
             for parity in range(2):
                 slot = 2 * lax.div(2 * pair + parity, group) + parity
-                scores = causal_scores(
-                    queries[rows, here], key_slots[slot, :reach, :], block * block_rows
-                )
+                scores = causal_scores(query_block, gup[slot, pl.ds(0, reach), :128], start)
                 weight = jnp.exp(scores - jnp.max(scores, axis=-1, keepdims=True))
                 weight = weight / jnp.sum(weight, axis=-1, keepdims=True)
                 total = total + matmul(
-                    weight.astype(jnp.bfloat16), value_slots[slot, :reach, :]
+                    weight.astype(jnp.bfloat16), gup[slot, pl.ds(tokens, reach), :128]
                 )
-            mixed[rows, here] = total.astype(jnp.bfloat16)
+            ggate[tile, pl.ds(tokens + start, block_rows), here] = total.astype(jnp.bfloat16)
         return carry
 
-    lax.fori_loop(0, query_v.shape[1] // 128, head_pair, 0)
+    lax.fori_loop(0, heads_width // 128, head_pair, 0)
     receive_relay(0, 0)
     start_relay(0, 1)
-    loads[4].wait()
-    part_send[...] = matmul(mixed[other_rows, :], out_v[...]).astype(jnp.bfloat16)
+    for piece in range(pieces):
+        results.append(
+            pltpu.make_async_copy(
+                ggate.at[3 + piece, high_rows],
+                mixed_out.at[:, pl.ds(piece * span, span)],
+                result_sem.at[3 + pieces + piece],
+            )
+        )
+    for copy in results[3 + pieces :]:
+        copy.start()
+    for copy in out_loads:
+        copy.wait()
+
+    def out_product(first_row):
+        rows = pl.ds(pl.multiple_of(tokens + first_row * half, half), half)
+        found = []
+        for column in range(column_tiles):
+            found.append(
+                sum(
+                    matmul(
+                        ggate[3 + piece, rows, :],
+                        grow[column, pl.ds(piece * span, span), :],
+                    )
+                    for piece in range(pieces)
+                )
+            )
+        return jnp.concatenate(found, axis=1)
+
+    part_send[...] = out_product(1 - core).astype(jnp.bfloat16)
     part_copy = pltpu.make_async_remote_copy(
         src_ref=part_send,
         dst_ref=part_recv,
@@ -627,36 +727,46 @@
         device_id_type=MESH,
     )
     part_copy.start()
-    own_part = matmul(mixed[own_rows, :], out_v[...])
+    own_part = out_product(core)
     part_copy.wait()
     attended_half = own_part + part_recv[...].astype(jnp.float32)
     attended[...] = attended_half.astype(jnp.bfloat16)
     middle = stream_v[own_rows, :].astype(jnp.float32) + residual_scale * attended_half
     inverse = lax.rsqrt(jnp.mean(middle * middle, axis=-1, keepdims=True) + epsilon)
-    mixer[...] = (middle * inverse * gain_second[...]).astype(jnp.bfloat16)
+    mixer[line_rows, :] = (middle * inverse * gain_second[...]).astype(jnp.bfloat16)
     start_relay(1, 0)
-    logits = matmul(mixer[...], router[...])
+    logits = matmul(mixer[line_rows, :], router[...])
     lane = lax.broadcasted_iota(jnp.int32, logits.shape, 1)
     routed = lane < 0
     for entry in range(TOP):
         routed = jnp.logical_or(routed, lane == routes[own_rows, entry : entry + 1])
     largest = jnp.max(jnp.where(routed, logits, masked_score), axis=-1, keepdims=True)
     gate_exp = jnp.where(routed, jnp.exp(jnp.minimum(logits - largest, 0.0)), 0.0)
-    probs[...] = gate_exp / jnp.sum(gate_exp, axis=-1, keepdims=True)
+    probs[line_rows, :] = gate_exp / jnp.sum(gate_exp, axis=-1, keepdims=True)
 
     def probs_copy(step):
         return send(
-            probs,
-            probs_all.at[line],
+            probs.at[line_rows],
+            probs.at[line_rows],
             (probs_send, probs_recv),
-            (step - 1,),
-            (partners[step], core),
+            (step,),
+            partners[step],
+        )
+
+    def probs_arriving(step):
+        theirs = block_rows_of(lax.div(partners[step][0], PLANE))
+        return send(
+            probs.at[theirs],
+            probs.at[theirs],
+            (probs_send, probs_recv),
+            (step,),
+            partners[step],
         )
 
     for step in range(1, LINES):
         probs_copy(step).start()
-    own_copies.append(pltpu.make_async_copy(probs, probs_all.at[line], own_sem.at[4]))
-    own_copies.append(pltpu.make_async_copy(mixer, mixer_all.at[line], own_sem.at[5]))
+    own_copies.append(pltpu.make_async_copy(probs.at[line_rows], probs_own, own_sem.at[4]))
+    own_copies.append(pltpu.make_async_copy(mixer.at[line_rows], mixer_own, own_sem.at[5]))
     for copy in own_copies[4:]:
         copy.start()
 
@@ -668,6 +778,111 @@
         for slot in (1, 2):
             to_sibling(kind, slot).start()
 
+    def hidden_tile(block, tile):
+        rows = block_rows_of(block)
+        step = lax.rem(tile, PLANE)
+        owner = lax.rem(place, PLANE)
+        owner = jnp.where(lax.rem(step, 2) == 1, flip(owner, 1), owner)
+        owner = jnp.where(lax.div(step, 2) == 1, flip(owner, 2), owner)
+        chosen = lax.broadcasted_iota(jnp.int32, (half, 128), 1) == line * PLANE + owner
+        prob = jnp.sum(jnp.where(chosen, probs[rows, :], 0.0), axis=1, keepdims=True)
+        gate_pre = matmul(mixer[rows, :], gates[tile])
+        up_pre = matmul(mixer[rows, :], ups[tile])
+        grad_raw = residual_scale * matmul_nt(cots[rows, :], downs[tile])
+        sigmoid_gate = 1.0 / (1.0 + jnp.exp(-gate_pre))
+        silu_gate = gate_pre * sigmoid_gate
+        active = silu_gate * up_pre
+        share = jnp.sum(active * grad_raw, axis=1, keepdims=True)
+        weighting[rows, :] += jnp.where(chosen, share, 0.0)
+        grad_active = prob * grad_raw
+        scaled[tile, rows, :] = (prob * active).astype(jnp.bfloat16)
+        ggate[tile, rows, :] = (
+            grad_active * up_pre * sigmoid_gate * (1.0 + gate_pre * (1.0 - sigmoid_gate))
+        ).astype(jnp.bfloat16)
+        gup[tile, rows, :] = (grad_active * silu_gate).astype(jnp.bfloat16)
+
+    def early_tiles(block):
+        def body(index, carry):
+            hidden_tile(block, index + lax.div(index, 3))
+            return carry
+
+        lax.fori_loop(0, 6, body, 0)
+
+    def late_tiles(block):
+        def body(index, carry):
+            hidden_tile(block, 3 + PLANE * index)
+            return carry
+
+        lax.fori_loop(0, 2, body, 0)
+
+    def grow_tiles(block):
+        rows = block_rows_of(block)
+
+        def body(column, carry):
+            here = pl.ds(pl.multiple_of(column * span, span), span)
+            total = matmul_nt(ggate[0, rows, :], gates[0, here, :])
+            for tile in range(1, tiles):
+                total = total + matmul_nt(ggate[tile, rows, :], gates[tile, here, :])
+            for tile in range(tiles):
+                total = total + matmul_nt(gup[tile, rows, :], ups[tile, here, :])
+            grow[column, rows, :] = total.astype(jnp.bfloat16)
+            return carry
+
+        lax.fori_loop(0, column_tiles, body, 0)
+
+    def remote_block(index):
+        near = (jnp.where(line == 0, 1, jnp.where(line == 1, 0, jnp.where(line == 2, 3, 2))))
+        middle_block = jnp.where(line < 2, 2, 1)
+        distant = jnp.where(line < 2, 3, 0)
+        return (near, middle_block, distant)[index]
+
+    def home_of(block):
+        return (place + (block - line) * PLANE, core)
+
+    def grow_copy(index):
+        block = remote_block(index)
+        return pltpu.make_async_remote_copy(
+            src_ref=grow.at[:, block_rows_of(block)],
+            dst_ref=grow_in.at[line],
+            send_sem=grow_send.at[index],
+            recv_sem=grow_recv.at[line],
+            device_id=home_of(block),
+            device_id_type=MESH,
+        )
+
+    def weighting_copy(index):
+        block = remote_block(index)
+        return pltpu.make_async_remote_copy(
+            src_ref=weighting.at[block_rows_of(block)],
+            dst_ref=weighting_in.at[line],
+            send_sem=weighting_send.at[index],
+            recv_sem=weighting_recv.at[line],
+            device_id=home_of(block),
+            device_id_type=MESH,
+        )
+
+    def returned(index):
+        block = remote_block(index)
+        return [
+            pltpu.make_async_remote_copy(
+                src_ref=target.at[block],
+                dst_ref=target.at[block],
+                send_sem=sems[0].at[index],
+                recv_sem=sems[1].at[block],
+                device_id=home_of(block),
+                device_id_type=MESH,
+            )
+            for target, sems in (
+                (grow_in, (grow_send, grow_recv)),
+                (weighting_in, (weighting_send, weighting_recv)),
+            )
+        ]
+
+    def send_back(index):
+        grow_tiles(remote_block(index))
+        weighting_copy(index).start()
+        grow_copy(index).start()
+
     pass_on(0)
     receive_relay(1, 0)
     start_relay(1, 1)
@@ -675,21 +890,61 @@
     start_relay(0, 2)
     pass_on(1)
     pass_on(2)
+    for copy in results:
+        copy.wait()
+    for copy in own_copies:
+        copy.wait()
+    for step in range(1, LINES):
+        probs_copy(step).wait_send()
+        probs_arriving(step).wait_recv()
+    for kind in range(3):
+        for slot in range(3):
+            to_sibling(kind, slot).wait_recv()
+    early_tiles(remote_block(0))
     receive_relay(1, 1)
     start_relay(1, 2)
     for kind in range(3):
         for axis in onwards[kind]:
             onward(kind, axis).wait_recv()
         to_sibling(kind, 3).start()
+    early_tiles(line)
+    for kind in range(3):
+        to_sibling(kind, 3).wait_recv()
+    late_tiles(remote_block(0))
+    send_back(0)
+    early_tiles(remote_block(1))
+    late_tiles(remote_block(1))
+    send_back(1)
     receive_relay(0, 2)
     receive_relay(1, 2)
-    for step in range(1, LINES):
-        probs_copy(step).wait()
-    for copy in own_copies:
-        copy.wait()
+    early_tiles(remote_block(2))
+    late_tiles(remote_block(2))
+    send_back(2)
+    late_tiles(line)
+    grow_tiles(line)
+
+    def out_tile(column, carry):
+        here = pl.ds(pl.multiple_of(column * span, span), span)
+        total = matmul(scaled[0], downs[0, :, here])
+        for tile in range(1, tiles):
+            total = total + matmul(scaled[tile], downs[tile, :, here])
+        outs[:, here] = total.astype(jnp.bfloat16)
+        return carry
+
+    lax.fori_loop(0, column_tiles, out_tile, 0)
+    stores = [
+        pltpu.make_async_copy(
+            outs.at[block_rows_of(lax.div(partners[step][0], PLANE))],
+            out_parts[step],
+            store_sem.at[step],
+        )
+        for step in range(LINES)
+    ]
+    for copy in stores:
+        copy.start()
     for kind in range(3):
         for slot in range(PLANE):
-            to_sibling(kind, slot).wait()
+            to_sibling(kind, slot).wait_send()
         for axis in (0, 1):
             direct(kind, axis).wait_send()
         for axis in onwards[kind]:
@@ -698,217 +953,8 @@
         for hop in range(LINES - 1):
             finish_relay(array, hop)
 
-
-def run_front(operands, weights):
-    low, wide = jnp.bfloat16, jnp.float32
-    shape = jax.ShapeDtypeStruct
-    far = pl.BlockSpec(memory_space=pl.ANY)
-    near = pl.BlockSpec(memory_space=pltpu.VMEM)
-    tokens, width = operands[0].shape
-    half = tokens // 2
-    query_width, key_width = operands[4].shape[1], operands[5].shape[1]
-    span = weights[0].shape[1]
-    tiles = 2 * PLANE
-    dma = pltpu.SemaphoreType.DMA
-    slots = 2 * key_width // HEAD_FEATURES
-    return pl.pallas_call(
-        front_kernel,
-        name="front",
-        out_shape=(
-            shape((tiles, width, span), low),
-            shape((tiles, width, span), low),
-            shape((tiles, span, width), low),
-            shape((LINES, half, width), low),
-            shape((LINES, half, width), low),
-            shape((LINES, half, 128), wide),
-            shape((tokens, width), low),
-            shape((tokens, query_width), low),
-            shape((tokens, key_width), low),
-            shape((tokens, key_width), low),
-            shape((tokens, query_width), low),
-            shape((half, width), low),
-        ),
-        in_specs=[far, far, near, near, far, far, far, far, near, near, near, near] + [far] * 3,
-        out_specs=(far,) * 6 + (near,) * 6,
-        scratch_shapes=[
-            pltpu.VMEM((tokens, width), low),
-            pltpu.VMEM((width, query_width), low),
-            pltpu.VMEM((width, key_width), low),
-            pltpu.VMEM((width, key_width), low),
-            pltpu.VMEM((query_width, width), low),
-            pltpu.VMEM((slots, tokens, 128), low),
-            pltpu.VMEM((slots, tokens, 128), low),
-            pltpu.VMEM((half, width), low),
-            pltpu.VMEM((half, width), low),
-            pltpu.VMEM((half, width), low),
-            pltpu.VMEM((half, 128), wide),
-            dma((5,)),
-            dma((6,)),
-            dma((3, 8)),
-            dma((3, 8)),
-            dma((2, 2, LINES - 1)),
-            dma((2, 2, LINES - 1)),
-            dma((LINES - 1,)),
-            dma((LINES - 1,)),
-            dma((2,)),
-        ],
-        compiler_params=pltpu.CompilerParams(
-            collective_id=2, has_side_effects=True, vmem_limit_bytes=60 << 20
-        ),
-    )(*operands, *weights)
-
-
-def expert_kernel(*refs):
-    tiles = 2 * PLANE
-    refs = list(refs)
-
-    def take(count):
-        taken = refs[:count]
-        del refs[:count]
-        return taken
-
-    mixer_all, cot_all, probs_all, gate_all, up_all, down_all = take(6)
-    out_parts = take(LINES)
-    grow_sum, weighting_sum = take(2)
-    kept = take(3)
-    landed = take(3)
-    mixer, cots, probs, gates, ups, downs = take(6)
-    scaled, ggate, gup, grow, grow_in, outs, weighting, weighting_in = take(8)
-    load_sem, tile_sem, store_sem, kept_sem = take(4)
-    grow_send, grow_recv, weighting_send, weighting_recv = take(4)
-    core_send, core_recv, plane_send, plane_recv, ready_sem = take(5)
-    half, width = mixer_all.shape[1:]
-    rows = LINES * half
-    span = gates.shape[2]
-    column_tiles = width // span
-
-    place = lax.axis_index("ep")
-    core = lax.axis_index("tp")
-    partners = [flip_line(place, step) for step in range(LINES)]
-    barrier = pltpu.get_barrier_semaphore()
-    for step in range(1, LINES):
-        pl.semaphore_signal(
-            barrier, inc=1, device_id=(partners[step], core), device_id_type=MESH
-        )
-    sibling = (place, 1 - core)
-    across = [(flip(place, 1), core), (flip(place, 2), core)]
-    for other in across + [sibling]:
-        pl.semaphore_signal(barrier, inc=1, device_id=other, device_id_type=MESH)
-
-    loads = []
-    for step in range(LINES):
-        part = pl.ds(step * half, half)
-        for kind, (source, target) in enumerate(
-            ((mixer_all, mixer), (cot_all, cots), (probs_all, probs))
-        ):
-            loads.append(
-                pltpu.make_async_copy(source.at[step], target.at[part], load_sem.at[kind, step])
-            )
-    for copy in loads:
-        copy.start()
-    for tile in range(tiles):
-        for kind, (source, target) in enumerate(
-            ((gate_all, gates), (up_all, ups), (down_all, downs))
-        ):
-            pltpu.make_async_copy(source.at[tile], target.at[tile], tile_sem.at[kind, tile]).start()
-    pl.semaphore_wait(barrier, LINES + 2)
-    for copy in loads:
-        copy.wait()
-    weighting[...] = jnp.zeros_like(weighting)
-    line_place = lax.div(place, PLANE)
-    lanes = lax.broadcasted_iota(jnp.int32, (rows, 128), 1)
-
-    def hidden_tile(tile, carry):
-        for kind, (source, target) in enumerate(
-            ((gate_all, gates), (up_all, ups), (down_all, downs))
-        ):
-            pltpu.make_async_copy(source.at[tile], target.at[tile], tile_sem.at[kind, tile]).wait()
-        step = lax.rem(tile, PLANE)
-        owner = lax.rem(place, PLANE)
-        owner = jnp.where(lax.rem(step, 2) == 1, flip(owner, 1), owner)
-        owner = jnp.where(lax.div(step, 2) == 1, flip(owner, 2), owner)
-        chosen = lanes == line_place * PLANE + owner
-        prob = jnp.sum(jnp.where(chosen, probs[...], 0.0), axis=1, keepdims=True)
-        gate_pre = matmul(mixer[...], gates[tile])
-        up_pre = matmul(mixer[...], ups[tile])
-        grad_raw = residual_scale * matmul_nt(cots[...], downs[tile])
-        sigmoid_gate = 1.0 / (1.0 + jnp.exp(-gate_pre))
-        silu_gate = gate_pre * sigmoid_gate
-        active = silu_gate * up_pre
-        share = jnp.sum(active * grad_raw, axis=1, keepdims=True)
-        weighting[...] += jnp.where(chosen, share, 0.0)
-        grad_active = prob * grad_raw
-        scaled[tile] = (prob * active).astype(jnp.bfloat16)
-        ggate[tile] = (
-            grad_active * up_pre * sigmoid_gate * (1.0 + gate_pre * (1.0 - sigmoid_gate))
-        ).astype(jnp.bfloat16)
-        gup[tile] = (grad_active * silu_gate).astype(jnp.bfloat16)
-        return carry
-
-    lax.fori_loop(0, tiles, hidden_tile, 0)
-
-    def rows_for(step):
-        return pl.ds(pl.multiple_of(lax.div(partners[step], PLANE) * half, half), half)
-
-    def weighting_copy(step):
-        return pltpu.make_async_remote_copy(
-            src_ref=weighting.at[rows_for(step)],
-            dst_ref=weighting_in.at[step - 1],
-            send_sem=weighting_send.at[step - 1],
-            recv_sem=weighting_recv.at[step - 1],
-            device_id=(partners[step], core),
-            device_id_type=MESH,
-        )
-
-    def grow_copy(step, column):
-        return pltpu.make_async_remote_copy(
-            src_ref=grow.at[column, rows_for(step)],
-            dst_ref=grow_in.at[step - 1, column],
-            send_sem=grow_send.at[step - 1, column],
-            recv_sem=grow_recv.at[step - 1, column],
-            device_id=(partners[step], core),
-            device_id_type=MESH,
-        )
-
-    for step in range(1, LINES):
-        weighting_copy(step).start()
-
-    def grow_tile(column, carry):
-        here = pl.ds(pl.multiple_of(column * span, span), span)
-        total = matmul_nt(ggate[0], gates[0, here, :])
-        for tile in range(1, tiles):
-            total = total + matmul_nt(ggate[tile], gates[tile, here, :])
-        for tile in range(tiles):
-            total = total + matmul_nt(gup[tile], ups[tile, here, :])
-        grow[column] = total.astype(jnp.bfloat16)
-        for step in range(1, LINES):
-            grow_copy(step, column).start()
-        return carry
-
-    lax.fori_loop(0, column_tiles, grow_tile, 0)
-
-    def out_tile(column, carry):
-        here = pl.ds(pl.multiple_of(column * span, span), span)
-        total = matmul(scaled[0], downs[0, :, here])
-        for tile in range(1, tiles):
-            total = total + matmul(scaled[tile], downs[tile, :, here])
-        outs[:, here] = total.astype(jnp.bfloat16)
-        return carry
-
-    lax.fori_loop(0, column_tiles, out_tile, 0)
-    stores = [
-        pltpu.make_async_copy(
-            outs.at[rows_for(step)], out_parts[step], store_sem.at[step]
-        )
-        for step in range(LINES)
-    ]
-    for copy in stores:
-        copy.start()
-
     pl.semaphore_signal(ready_sem, inc=1, device_id=sibling, device_id_type=MESH)
     pl.semaphore_wait(ready_sem, 1)
-    held = (gates, ups, downs)
-
     def tile_order(index):
         return jnp.where(index == 0, 3, jnp.where(index == 3, 0, index))
 
@@ -977,23 +1023,23 @@
         return carry
 
     lax.fori_loop(0, PLANE, own_tile, 0)
-    for step in range(1, LINES):
-        weighting_copy(step).wait()
-    total = weighting[rows_for(0), :]
-    for step in range(1, LINES):
-        total = total + weighting_in[step - 1]
+    for index in range(LINES - 1):
+        weighting_copy(index).wait_send()
+        grow_copy(index).wait_send()
+        for copy in returned(index):
+            copy.wait_recv()
+    total = weighting[line_rows, :]
+    for index in range(LINES - 1):
+        total = total + weighting_in[remote_block(index)]
     weighting_sum[...] = total
     for column in range(column_tiles):
         here = pl.ds(column * span, span)
-        for step in range(1, LINES):
-            grow_copy(step, column).wait()
-        total = grow[column, rows_for(0), :].astype(jnp.float32)
-        for step in range(1, LINES):
-            total = total + grow_in[step - 1, column].astype(jnp.float32)
+        total = grow[column, line_rows, :].astype(jnp.float32)
+        for index in range(LINES - 1):
+            total = total + grow_in[remote_block(index), column].astype(jnp.float32)
         grow_sum[:, here] = total
     for copy in stores:
         copy.wait()
-
     for kind in range(3):
         for step in range(PLANE):
             core_copy(kind, step).wait_send()
@@ -1004,21 +1050,24 @@
                 plane_copy(kind, axis, passing).wait()
 
 
-def run_experts(mixer_all, cot_all, probs_all, gate_all, up_all, down_all):
-    tiles = 2 * PLANE
-    half, width = mixer_all.shape[1:]
-    span = gate_all.shape[2]
-    rows = LINES * half
+def run_front(operands, weights):
     low, wide = jnp.bfloat16, jnp.float32
     shape = jax.ShapeDtypeStruct
+    vmem = pltpu.VMEM
     far = pl.BlockSpec(memory_space=pl.ANY)
     near = pl.BlockSpec(memory_space=pltpu.VMEM)
-    operands = [mixer_all, cot_all, probs_all, gate_all, up_all, down_all]
+    tokens, width = operands[0].shape
+    half = tokens // 2
+    rows = LINES * half
+    query_width, key_width = operands[4].shape[1], operands[5].shape[1]
+    span = weights[0].shape[1]
+    tiles = 2 * PLANE
     dma = pltpu.SemaphoreType.DMA
-    flops = 18 * rows * width * span * tiles
-    results = pl.pallas_call(
-        expert_kernel,
-        name="experts",
+    pieces = query_width // span
+    columns = width // span
+    return pl.pallas_call(
+        front_kernel,
+        name="front",
         out_shape=(
             *[shape((half, width), low)] * LINES,
             shape((half, width), wide),
@@ -1029,32 +1078,50 @@
             shape((2, 2, width // 2, span), low),
             shape((2, 2, width // 2, span), low),
             shape((2, 2, span // 2, width), low),
+            shape((half, width), low),
+            shape((half, 128), wide),
+            shape((tokens, width), low),
+            shape((tokens, query_width), low),
+            shape((tokens, key_width), low),
+            shape((tokens, key_width), low),
+            shape((tokens, query_width), low),
+            shape((half, width), low),
         ),
-        in_specs=[far] * len(operands),
-        out_specs=(*[far] * LINES, near, near, *[far] * 6),
+        in_specs=[far, far, near, near, far, far, far, far, near, near, near, near] + [far] * 3,
+        out_specs=(*[far] * LINES, near, near, *[far] * 13, near),
         scratch_shapes=[
-            pltpu.VMEM((rows, width), low),
-            pltpu.VMEM((rows, width), low),
-            pltpu.VMEM((rows, 128), wide),
-            pltpu.VMEM((tiles, width, span), low),
-            pltpu.VMEM((tiles, width, span), low),
-            pltpu.VMEM((tiles, span, width), low),
-            pltpu.VMEM((tiles, rows, span), low),
-            pltpu.VMEM((tiles, rows, span), low),
-            pltpu.VMEM((tiles, rows, span), low),
-            pltpu.VMEM((width // span, rows, span), low),
-            pltpu.VMEM((LINES - 1, width // span, half, span), low),
-            pltpu.VMEM((rows, width), low),
-            pltpu.VMEM((rows, 128), wide),
-            pltpu.VMEM((LINES - 1, half, 128), wide),
-            dma((3, LINES)),
-            dma((3, tiles)),
+            vmem((rows, width), low),
+            vmem((rows, width), low),
+            vmem((rows, 128), wide),
+            vmem((tiles, width, span), low),
+            vmem((tiles, width, span), low),
+            vmem((tiles, span, width), low),
+            vmem((tiles, rows, span), low),
+            vmem((tiles, rows, span), low),
+            vmem((tiles, rows, span), low),
+            vmem((columns, rows, span), low),
+            vmem((LINES, columns, half, span), low),
+            vmem((rows, width), low),
+            vmem((rows, 128), wide),
+            vmem((LINES, half, 128), wide),
+            vmem((half, width), low),
+            vmem((half, width), low),
+            dma((5 + 2 * pieces + columns,)),
+            dma((6,)),
+            dma((3, 8)),
+            dma((3, 8)),
+            dma((2, 2, LINES - 1)),
+            dma((2, 2, LINES - 1)),
+            dma((LINES,)),
+            dma((LINES,)),
+            dma((2,)),
+            dma((3 + 2 * pieces,)),
             dma((LINES,)),
             dma((3, 3)),
-            dma((LINES - 1, width // span)),
-            dma((LINES - 1, width // span)),
             dma((LINES - 1,)),
+            dma((LINES,)),
             dma((LINES - 1,)),
+            dma((LINES,)),
             dma((3, PLANE)),
             dma((3, PLANE)),
             dma((3, 2, 2)),
@@ -1065,10 +1132,11 @@
             collective_id=0, has_side_effects=True, vmem_limit_bytes=63 << 20
         ),
         cost_estimate=pl.CostEstimate(
-            flops=flops, bytes_accessed=12 * width * span * tiles, transcendentals=0
+            flops=18 * rows * width * span * tiles,
+            bytes_accessed=12 * width * span * tiles,
+            transcendentals=0,
         ),
-    )(*operands)
-    return results
+    )(*operands, *weights)
 
 
 def back_kernel(*refs):
@@ -1084,7 +1152,7 @@
     kept, landed = take(3), take(3)
     stream, cotangent, gain_first, gain_second, query_weight, key_weight = take(6)
     value_weight, out_weight, router, cosine, sine = take(5)
-    mixer_all, probs_all, normed, queries, keys, values, mixed, attended = take(8)
+    mixer_own, probs_own, normed, queries, keys, values, mixed, attended = take(8)
     layer_out, grad_stream, out_result_a, out_result_b, query_result, rest_result = take(6)
     expert_grads = take(3)
     small_out = take(1)[0]
@@ -1107,7 +1175,6 @@
 
     place = lax.axis_index("ep")
     core = lax.axis_index("tp")
-    line = lax.div(place, PLANE)
     sibling = (place, 1 - core)
     across = [flip(place, 1), flip(place, 2)]
     partners = [flip_line(place, step) for step in range(LINES)]
@@ -1123,7 +1190,7 @@
         (grow_sum, grow_v),
         (weighting_sum, weighting_v),
         (attended, attended_v),
-        (probs_all.at[line], probs_v),
+        (probs_own, probs_v),
         (stream, stream_v),
         (cotangent.at[own_rows], cot_v),
         (out_weight, out_v),
@@ -1135,7 +1202,7 @@
         (query_weight, query_v),
         (key_weight, key_v),
         (value_weight, value_v),
-        (mixer_all.at[line], mixer_v),
+        (mixer_own, mixer_v),
         (out_parts[0], mixer_v),
     ]
     loads = [
@@ -1375,7 +1442,7 @@
                     weight.astype(jnp.bfloat16), grad_block
                 )
             query_grads[rows, here] = turned_back(
-                score_scale * total, cosine[rows, :128], sine[rows, :128]
+                score_scale * total, cosine[rows, :], sine[rows, :]
             )
         return carry
 
@@ -1392,12 +1459,14 @@
                 lane_halves(totals[second])[0], HEAD_FEATURES, 1
             )
             found.append(low + high)
-        return jnp.concatenate(found, axis=1)
-
-    key_grads[...] = turned_back(
-        score_scale * gathered_pairs(key_totals), cosine[...], sine[...]
-    )
-    value_grads[...] = gathered_pairs(value_totals).astype(jnp.bfloat16)
+        return found
+
+    for pair, value in enumerate(gathered_pairs(key_totals)):
+        key_grads[:, pair * 128 : pair * 128 + 128] = turned_back(
+            score_scale * value, cosine[...], sine[...]
+        )
+    for pair, value in enumerate(gathered_pairs(value_totals)):
+        value_grads[:, pair * 128 : pair * 128 + 128] = value.astype(jnp.bfloat16)
     for copy in loads[11:-1]:
         copy.wait()
     query_source[...] = matmul_tn(normed_v[...], query_grads[...]).astype(jnp.bfloat16)
@@ -1616,7 +1685,10 @@
     experts = router_weight.shape[1]
     query_width = query_weight.shape[1]
     key_width = key_matrix.shape[1]
-    cosine_rows, sine_rows = rope_tables(SEQ_LEN)
+    steps_up = np.arange(HEAD_FEATURES // 2, dtype=np.float32) * np.float32(2.0 / HEAD_FEATURES)
+    turns = np.exp(-steps_up * np.log(np.float32(rope_base)))
+    angles = np.arange(SEQ_LEN, dtype=np.float32)[:, None] * turns[None, :]
+    cosines, sines = np.cos(angles), np.sin(angles)
     operands = [
         stream,
         cotangent,
@@ -1628,12 +1700,10 @@
         out_weight,
         jnp.pad(router_weight, ((0, 0), (0, 128 - experts))),
         routes,
-        jnp.tile(cosine_rows, (1, 8)),
-        jnp.tile(jnp.concatenate([-sine_rows, sine_rows], axis=1), (1, 4)),
+        jnp.asarray(np.tile(cosines, (1, 4))),
+        jnp.asarray(np.tile(np.concatenate([-sines, sines], axis=1), (1, 2))),
     ]
     front = run_front(operands, [gate_weight[0], up_weight[0], down_weight[0]])
-    gate_all, up_all, down_all, mixer_all, cot_all, probs_all = front[:6]
-    expert_results = run_experts(mixer_all, cot_all, probs_all, gate_all, up_all, down_all)
     (
         layer_out,
         grad_stream,
@@ -1645,7 +1715,7 @@
         up_grad,
         down_grad,
         small,
-    ) = run_back(expert_results, operands[:9] + operands[10:], [mixer_all, *front[5:]])
+    ) = run_back(front[: LINES + 8], operands[:9] + operands[10:], front[LINES + 8 :])
     slab = query_grad.shape[0]
     rms_stats = jnp.sqrt(small[slab : slab + 1, :3] / (tok_rows * model_width))
     return (

time: 391 us -> 360 us (0.921)
  Pallas kernels: 364 us -> 335 us
    pallas_call x2 -> x1, Pallas kernels: 251 us -> 223 us  [run_front(): pl.pallas_call(front_kernel, name='front', out_shape=(*[shape((half, widt...]
where the time goes in v4:
time: 360 us; the launch traced here: 357 us
  Pallas kernels  335 us (93%)
  local copies, waits for them, and re-layouts  12.6 us (4%)
  other arithmetic  8.39 us (2%)
    pallas_call x1, Pallas kernels, run_front(): pl.pallas_call(front_kernel, name='front', out_shape=(*[shape((half, widt...  223 us
    pallas_call x1, Pallas kernels, run_back(): pl.pallas_call(back_kernel, name='back', out_shape=(shape((tokens, width)...  112 us

profile of v4, /device:TPU:0, one launch (start us, length us, event | category | flops | bytes accessed | tf_op | source)
XLA Modules:
  0.0 356.7 jit_solution(16372441647827245924)
XLA Ops:
  0.6 1.3 reshape.50.refs_2_.refs_14_
  1.9 1.3 reshape.51.refs_3_.refs_15_
  3.2 1.6 copy.32.refs_9_
  4.8 1.0 copy.31
  5.8 0.8 pad.4.refs_8_.refs_20_
  6.6 222.6 %front.1 = (bf16[256,1536]{1,0:T(8,128)(2,1)}, bf16[256,1536]{1,0:T(8,128)(2,1)}, bf16[256,1536]{1,0:T(8,128)(2,1)}, bf16[256,1536]{1,0:T(8,128)(2,1)}, f32[256,...) custom-call(bf16[512,1536]{1,0:T(8,128)(2,1)} %refs_12_.1, ...), custom_call_target="tpu_custom_call" | custom-call | flops 57982058496 | bytes 37748736 | tf_op jit(solution)/shard_map/front/pallas_call | solution.py:1068
  229.3 112.2 %back.1 = (bf16[512,1536]{1,0:T(8,128)(2,1)}, bf16[512,1536]{1,0:T(8,128)(2,1)}, f32[96,384]{1,0:T(8,128)}, f32[96,384]{1,0:T(8,128)}, f32[96,768]{1,0:T(8,128)}...) custom-call(bf16[256,1536]{1,0:T(8,128)(2,1)} %get-tuple-element.43., ...), custom_call_target="tpu_custom_call" | custom-call | tf_op jit(solution)/shard_map/back/pallas_call | solution.py:1604
  341.5 0.0 copy-start.4
  341.5 1.3 multiply_sqrt_fusion
  342.8 1.6 slice_reduce_fusion
  344.4 0.8 slice.22
  345.2 0.7 copy.33
  345.8 1.6 fusion
  347.5 1.8 maximum_bitcast_fusion
  349.3 0.0 copy-done.4
  349.3 1.3 bitcast_convert_fusion
  350.6 0.0 copy-done.1
  350.6 2.1 convert_element_type.4
  352.7 0.0 copy-done.2
  352.7 0.0 copy-done.3
  352.7 1.9 bitcast_convert_fusion.1
  354.6 0.0 copy-done
  354.6 1.1 copy.36
  355.8 0.7 copy.37
  (6 shorter events, 0.0 us)
Async XLA Ops:
  341.5 7.8 %copy-start.4 = (bf16[2,128,1536]{2,1,0:T(8,128)(2,1)S(1)}, bf16[2,128,1536]{2,1,0:T(8,128)(2,1)}, u32[]{:S(2)}) copy-start(bf16[2,128,1536]{2,1,0:T(8,128)(2,1)} %get-tuple-element.72) | copy-start | bytes 2359300
  347.5 3.2 copy-start.1
  350.6 2.1 copy-start.2
  350.6 2.1 copy-start.3
  352.7 1.9 copy-start
  354.6 1.1 copy-start.5

commit v5 on v4

--- a/solution.py
+++ b/solution.py
@@ -357,6 +357,7 @@
 MESH = pl.DeviceIdType.MESH
 PLANE = 4
 LINES = 4
+DEFERRED = (2,)
 
 
 def flip(place, unit):
@@ -611,7 +612,7 @@
     loads[0].wait()
     stream_f = stream_v[...].astype(jnp.float32)
     inverse = lax.rsqrt(jnp.mean(stream_f * stream_f, axis=-1, keepdims=True) + epsilon)
-    normed[...] = (stream_f * inverse * gain_first[...]).astype(jnp.bfloat16)
+    normed[...] = (stream_f * inverse * gain_first[...].astype(jnp.float32)[None, :]).astype(jnp.bfloat16)
     for copy in loads[1:]:
         copy.wait()
 
@@ -733,13 +734,17 @@
     attended[...] = attended_half.astype(jnp.bfloat16)
     middle = stream_v[own_rows, :].astype(jnp.float32) + residual_scale * attended_half
     inverse = lax.rsqrt(jnp.mean(middle * middle, axis=-1, keepdims=True) + epsilon)
-    mixer[line_rows, :] = (middle * inverse * gain_second[...]).astype(jnp.bfloat16)
+    mixer[line_rows, :] = (middle * inverse * gain_second[...].astype(jnp.float32)[None, :]).astype(jnp.bfloat16)
     start_relay(1, 0)
-    logits = matmul(mixer[line_rows, :], router[...])
+    padding = jnp.zeros((128 - router.shape[0], width), jnp.bfloat16)
+    logits = matmul_nt(
+        mixer[line_rows, :], jnp.concatenate([router[...], padding], axis=0)
+    )
+    own_routes = routes[:, own_rows].T
     lane = lax.broadcasted_iota(jnp.int32, logits.shape, 1)
     routed = lane < 0
     for entry in range(TOP):
-        routed = jnp.logical_or(routed, lane == routes[own_rows, entry : entry + 1])
+        routed = jnp.logical_or(routed, lane == own_routes[:, entry : entry + 1])
     largest = jnp.max(jnp.where(routed, logits, masked_score), axis=-1, keepdims=True)
     gate_exp = jnp.where(routed, jnp.exp(jnp.minimum(logits - largest, 0.0)), 0.0)
     probs[line_rows, :] = gate_exp / jnp.sum(gate_exp, axis=-1, keepdims=True)
@@ -815,7 +820,7 @@
 
         lax.fori_loop(0, 2, body, 0)
 
-    def grow_tiles(block):
+    def grow_tiles(block, first, last):
         rows = block_rows_of(block)
 
         def body(column, carry):
@@ -828,27 +833,60 @@
             grow[column, rows, :] = total.astype(jnp.bfloat16)
             return carry
 
-        lax.fori_loop(0, column_tiles, body, 0)
+        lax.fori_loop(first, last, body, 0)
+
+    outer = jnp.logical_or(line == 0, line == LINES - 1)
+    near_line = flip(line, 1)
+    far_inner = jnp.where(line < 2, 2, 1)
+    far_outer = jnp.where(line < 2, 3, 0)
 
     def remote_block(index):
-        near = (jnp.where(line == 0, 1, jnp.where(line == 1, 0, jnp.where(line == 2, 3, 2))))
-        middle_block = jnp.where(line < 2, 2, 1)
-        distant = jnp.where(line < 2, 3, 0)
-        return (near, middle_block, distant)[index]
+        outside = (near_line, far_inner, far_outer)[index]
+        inside = (far_inner, far_outer, near_line)[index]
+        return jnp.where(outer, outside, inside)
 
     def home_of(block):
         return (place + (block - line) * PLANE, core)
 
-    def grow_copy(index):
+    chunks = 2
+    chunk_columns = column_tiles // chunks
+
+    def grow_copy(index, chunk):
         block = remote_block(index)
+        home = jnp.where(outer, near_line, block)
+        slot = jnp.where(outer, (0, 2, 3)[index], (1, 1, 0)[index])
+        columns = pl.ds(chunk * chunk_columns, chunk_columns)
         return pltpu.make_async_remote_copy(
-            src_ref=grow.at[:, block_rows_of(block)],
-            dst_ref=grow_in.at[line],
-            send_sem=grow_send.at[index],
-            recv_sem=grow_recv.at[line],
-            device_id=home_of(block),
+            src_ref=grow.at[columns, block_rows_of(block)],
+            dst_ref=grow_in.at[slot, columns],
+            send_sem=grow_send.at[index, chunk],
+            recv_sem=grow_recv.at[slot, chunk],
+            device_id=home_of(home),
             device_id_type=MESH,
         )
+
+    def grow_arriving(slot, chunk):
+        columns = pl.ds(chunk * chunk_columns, chunk_columns)
+        return pltpu.make_async_remote_copy(
+            src_ref=grow_in.at[slot, columns],
+            dst_ref=grow_in.at[slot, columns],
+            send_sem=grow_send.at[0, chunk],
+            recv_sem=grow_recv.at[slot, chunk],
+            device_id=home_of(near_line),
+            device_id_type=MESH,
+        )
+
+    def combine(index, chunk):
+        @pl.when(jnp.logical_not(outer))
+        def _():
+            grow_arriving(2 + index, chunk).wait_recv()
+            rows = block_rows_of(remote_block(index))
+            for column in range(chunk * chunk_columns, (chunk + 1) * chunk_columns):
+                grow[column, rows, :] = (
+                    grow[column, rows, :].astype(jnp.float32)
+                    + grow_in[2 + index, column].astype(jnp.float32)
+                ).astype(jnp.bfloat16)
+            grow_copy(index, chunk).start()
 
     def weighting_copy(index):
         block = remote_block(index)
@@ -861,27 +899,30 @@
             device_id_type=MESH,
         )
 
-    def returned(index):
+    def weighting_arriving(index):
         block = remote_block(index)
-        return [
-            pltpu.make_async_remote_copy(
-                src_ref=target.at[block],
-                dst_ref=target.at[block],
-                send_sem=sems[0].at[index],
-                recv_sem=sems[1].at[block],
-                device_id=home_of(block),
-                device_id_type=MESH,
+        return pltpu.make_async_remote_copy(
+            src_ref=weighting_in.at[block],
+            dst_ref=weighting_in.at[block],
+            send_sem=weighting_send.at[index],
+            recv_sem=weighting_recv.at[block],
+            device_id=home_of(block),
+            device_id_type=MESH,
+        )
+
+    def send_back(index):
+        weighting_copy(index).start()
+        for chunk in range(chunks):
+            grow_tiles(
+                remote_block(index), chunk * chunk_columns, (chunk + 1) * chunk_columns
             )
-            for target, sems in (
-                (grow_in, (grow_send, grow_recv)),
-                (weighting_in, (weighting_send, weighting_recv)),
-            )
-        ]
-
-    def send_back(index):
-        grow_tiles(remote_block(index))
-        weighting_copy(index).start()
-        grow_copy(index).start()
+            if index == 2:
+                grow_copy(index, chunk).start()
+            else:
+
+                @pl.when(outer)
+                def _():
+                    grow_copy(index, chunk).start()
 
     pass_on(0)
     receive_relay(1, 0)
@@ -908,40 +949,22 @@
             onward(kind, axis).wait_recv()
         to_sibling(kind, 3).start()
     early_tiles(line)
+    early_tiles(remote_block(1))
     for kind in range(3):
         to_sibling(kind, 3).wait_recv()
     late_tiles(remote_block(0))
     send_back(0)
-    early_tiles(remote_block(1))
     late_tiles(remote_block(1))
     send_back(1)
+    late_tiles(line)
+    grow_tiles(line, 0, column_tiles)
     receive_relay(0, 2)
     receive_relay(1, 2)
     early_tiles(remote_block(2))
     late_tiles(remote_block(2))
     send_back(2)
-    late_tiles(line)
-    grow_tiles(line)
-
-    def out_tile(column, carry):
-        here = pl.ds(pl.multiple_of(column * span, span), span)
-        total = matmul(scaled[0], downs[0, :, here])
-        for tile in range(1, tiles):
-            total = total + matmul(scaled[tile], downs[tile, :, here])
-        outs[:, here] = total.astype(jnp.bfloat16)
-        return carry
-
-    lax.fori_loop(0, column_tiles, out_tile, 0)
-    stores = [
-        pltpu.make_async_copy(
-            outs.at[block_rows_of(lax.div(partners[step][0], PLANE))],
-            out_parts[step],
-            store_sem.at[step],
-        )
-        for step in range(LINES)
-    ]
-    for copy in stores:
-        copy.start()
+    combine(0, 0)
+    combine(0, 1)
     for kind in range(3):
         for slot in range(PLANE):
             to_sibling(kind, slot).wait_send()
@@ -953,15 +976,33 @@
         for hop in range(LINES - 1):
             finish_relay(array, hop)
 
+    def out_tile(column, carry):
+        here = pl.ds(pl.multiple_of(column * span, span), span)
+        total = matmul(scaled[0], downs[0, :, here])
+        for tile in range(1, tiles):
+            total = total + matmul(scaled[tile], downs[tile, :, here])
+        outs[:, here] = total.astype(jnp.bfloat16)
+        return carry
+
+    stores = [
+        pltpu.make_async_copy(
+            outs.at[block_rows_of(lax.div(partners[step][0], PLANE))],
+            out_parts[step],
+            store_sem.at[step],
+        )
+        for step in range(LINES)
+    ]
     pl.semaphore_signal(ready_sem, inc=1, device_id=sibling, device_id_type=MESH)
     pl.semaphore_wait(ready_sem, 1)
     def tile_order(index):
         return jnp.where(index == 0, 3, jnp.where(index == 3, 0, index))
 
-    def tile_grads(tile):
-        yield matmul_tn(mixer[...], ggate[tile])
-        yield matmul_tn(mixer[...], gup[tile])
-        yield residual_scale * matmul_tn(scaled[tile], cots[...])
+    def tile_grads(tile, kinds):
+        for kind in kinds:
+            if kind == 2:
+                yield kind, residual_scale * matmul_tn(scaled[tile], cots[...])
+            else:
+                yield kind, matmul_tn(mixer[...], (ggate, gup)[kind][tile])
 
     def core_copy(kind, step):
         return pltpu.make_async_remote_copy(
@@ -973,14 +1014,11 @@
             device_id_type=MESH,
         )
 
-    def sibling_tile(index, carry):
+    def sibling_tile(index, kinds):
         step = tile_order(index)
-        for kind, grad in enumerate(tile_grads(PLANE + step)):
+        for kind, grad in tile_grads(PLANE + step, kinds):
             held[kind][PLANE + step] = grad.astype(jnp.bfloat16)
             core_copy(kind, step).start()
-        return carry
-
-    lax.fori_loop(0, PLANE, sibling_tile, 0)
 
     def plane_copy(kind, axis, passing):
         span_rows = held[kind].shape[1] // 2
@@ -999,9 +1037,13 @@
             held[kind].at[step], kept[kind].at[step], kept_sem.at[kind, step]
         )
 
-    def own_tile(index, carry):
+    def own_tile(index, kinds):
+        @pl.when(index < PLANE - 1)
+        def _():
+            sibling_tile(index + 1, kinds)
+
         step = tile_order(index)
-        for kind, grad in enumerate(tile_grads(step)):
+        for kind, grad in tile_grads(step, kinds):
             core_copy(kind, step).wait_recv()
             held[kind][step] = (grad + held[kind][step].astype(jnp.float32)).astype(jnp.bfloat16)
 
@@ -1012,6 +1054,9 @@
 
             for axis in (0, 1):
 
+                if kind in DEFERRED:
+                    continue
+
                 @pl.when(step == axis + 1)
                 def _():
                     plane_copy(kind, axis, 0).start()
@@ -1020,14 +1065,37 @@
             def _():
                 kept_copy(kind, step).start()
 
+        return kinds
+
+    def gate_and_up(index, carry):
+        own_tile(index, (0, 1))
         return carry
 
-    lax.fori_loop(0, PLANE, own_tile, 0)
+    def down_only(index, carry):
+        own_tile(index, (2,))
+        return carry
+
+    sibling_tile(0, (0, 1))
+    lax.fori_loop(0, 2, gate_and_up, 0)
+    combine(1, 0)
+    lax.fori_loop(2, 3, gate_and_up, 0)
+    combine(1, 1)
+    lax.fori_loop(3, PLANE, gate_and_up, 0)
+    lax.fori_loop(0, column_tiles, out_tile, 0)
+    for copy in stores:
+        copy.start()
+    pl.semaphore_signal(ready_sem, inc=1, device_id=sibling, device_id_type=MESH)
+    pl.semaphore_wait(ready_sem, 1)
+    sibling_tile(0, (2,))
+    lax.fori_loop(0, PLANE, down_only, 0)
     for index in range(LINES - 1):
         weighting_copy(index).wait_send()
-        grow_copy(index).wait_send()
-        for copy in returned(index):
-            copy.wait_recv()
+        for chunk in range(chunks):
+            grow_copy(index, chunk).wait_send()
+        weighting_arriving(index).wait_recv()
+    for slot in (0, 1):
+        for chunk in range(chunks):
+            grow_arriving(slot, chunk).wait_recv()
     total = weighting[line_rows, :]
     for index in range(LINES - 1):
         total = total + weighting_in[remote_block(index)]
@@ -1035,8 +1103,8 @@
     for column in range(column_tiles):
         here = pl.ds(column * span, span)
         total = grow[column, line_rows, :].astype(jnp.float32)
-        for index in range(LINES - 1):
-            total = total + grow_in[remote_block(index), column].astype(jnp.float32)
+        for slot in (0, 1):
+            total = total + grow_in[slot, column].astype(jnp.float32)
         grow_sum[:, here] = total
     for copy in stores:
         copy.wait()
@@ -1046,7 +1114,7 @@
         for step in range(3):
             kept_copy(kind, step).wait()
         for axis in (0, 1):
-            for passing in (0, 1):
+            for passing in (1,) if kind in DEFERRED else (0, 1):
                 plane_copy(kind, axis, passing).wait()
 
 
@@ -1118,8 +1186,8 @@
             dma((3 + 2 * pieces,)),
             dma((LINES,)),
             dma((3, 3)),
-            dma((LINES - 1,)),
-            dma((LINES,)),
+            dma((LINES - 1, 2)),
+            dma((LINES, 2)),
             dma((LINES - 1,)),
             dma((LINES,)),
             dma((3, PLANE)),
@@ -1169,7 +1237,7 @@
     scatter_scratch = [take(5) for _ in range(4)]
     last_send, last_recv = take(2)
     load_sem, part_sem, out_send, out_recv, pair_sem, plane_send, plane_recv = take(7)
-    store_sem = take(1)[0]
+    store_sem, deferred_send, deferred_recv = take(3)
     tokens, width = stream_v.shape
     half = tokens // 2
 
@@ -1224,13 +1292,34 @@
             )
         ]
 
-    def landed_copy(kind):
-        return pltpu.make_async_copy(landed[kind], landed_v[kind], part_sem.at[kind, 2])
+    def landed_copies(kind):
+        if kind in DEFERRED:
+            return [
+                pltpu.make_async_copy(
+                    landed[kind].at[axis, 1],
+                    landed_v[kind].at[axis, 1],
+                    part_sem.at[kind, 2 + axis],
+                )
+                for axis in (0, 1)
+            ]
+        return [pltpu.make_async_copy(landed[kind], landed_v[kind], part_sem.at[kind, 2])]
+
+    def deferred_copy(kind, axis):
+        rows = own_parts[kind].shape[1]
+        return pltpu.make_async_remote_copy(
+            src_ref=kept[kind].at[axis + 1, pl.ds(axis * rows, rows)],
+            dst_ref=landed_v[kind].at[axis, 0],
+            send_sem=deferred_send.at[kind, axis],
+            recv_sem=deferred_recv.at[kind, axis],
+            device_id=(across[axis], core),
+            device_id_type=MESH,
+        )
 
     for copy in loads[:6]:
         copy.start()
     for kind in range(3):
-        landed_copy(kind).start()
+        for copy in landed_copies(kind):
+            copy.start()
         for copy in part_copies(kind, False):
             copy.start()
     for copy in loads[6:-1]:
@@ -1256,6 +1345,9 @@
             (partners[step], core),
         )
 
+    for kind in DEFERRED:
+        for axis in (0, 1):
+            deferred_copy(kind, axis).start()
     for step in (3, 2, 1):
         out_copy(step).start()
 
@@ -1267,8 +1359,11 @@
     weighting = weighting_v[...]
     grad_chosen = probs * (weighting - jnp.sum(probs * weighting, axis=-1, keepdims=True))
     grad_logits = grad_chosen.astype(jnp.bfloat16)
-    grad_mixer = matmul_nt(grad_logits, router[...]) + grow_v[...]
-    weighted = grad_mixer * gain_second[...]
+    padding = jnp.zeros((128 - router.shape[0], width), jnp.bfloat16)
+    grad_mixer = (
+        matmul(grad_logits, jnp.concatenate([router[...], padding], axis=0)) + grow_v[...]
+    )
+    weighted = grad_mixer * gain_second[...].astype(jnp.float32)[None, :]
     grad_middle = (
         cot_v[...].astype(jnp.float32)
         + inverse * weighted
@@ -1301,7 +1396,8 @@
         )
 
     for kind in range(3):
-        landed_copy(kind).wait()
+        for copy in landed_copies(kind):
+            copy.wait()
         for copy in part_copies(kind, False):
             copy.wait()
         for axis in (0, 1):
@@ -1494,7 +1590,7 @@
         )
         stream_f = stream_v[rows, :].astype(jnp.float32)
         inverse = lax.rsqrt(jnp.mean(stream_f * stream_f, axis=-1, keepdims=True) + epsilon)
-        weighted = grad_normed * gain_first[...]
+        weighted = grad_normed * gain_first[...].astype(jnp.float32)[None, :]
         total = (
             middle_grads[rows, :].astype(jnp.float32)
             + inverse * weighted
@@ -1553,6 +1649,8 @@
             copy.wait()
         for axis in (0, 1):
             plane_copy(kind, axis).wait()
+            if kind in DEFERRED:
+                deferred_copy(kind, axis).wait()
             own_parts[kind][axis] = (
                 own_parts[kind][axis].astype(jnp.float32)
                 + landed_v[kind][axis, 0].astype(jnp.float32)
@@ -1652,18 +1750,92 @@
             vmem((slab + 8, 128), wide),
             vmem((slab + 8, 128), wide),
             dma((17,)),
-            dma((3, 3)),
+            dma((3, 4)),
             dma((LINES - 1,)),
             dma((LINES - 1,)),
             dma((2, 4)),
             dma((3, 2)),
             dma((3, 2)),
             dma((5,)),
+            dma((3, 2)),
+            dma((3, 2)),
         ],
         compiler_params=pltpu.CompilerParams(
             collective_id=1, has_side_effects=True, vmem_limit_bytes=63 << 20
         ),
     )(*expert_results, *operands, *front_results)
+
+
+def finish_kernel(*refs):
+    layer_in, sources, refs = refs[0], refs[1:10], refs[10:]
+    layer_out, refs = refs[0], refs[1:]
+    grad_stream, out_grad, query_grad, key_grad, value_grad = refs[:5]
+    gate_grad, up_grad, down_grad, router_grad, second_gain, first_gain, rms = refs[5:12]
+    loaded, load_sem = refs[12:21], refs[21]
+    layer_copy = pltpu.make_async_copy(layer_in, layer_out, load_sem.at[9])
+    layer_copy.start()
+    stream_low, out_first, out_second, query_low, rest, gate_low, up_low, down_low, small = loaded
+    copies = [
+        pltpu.make_async_copy(source, target, load_sem.at[index])
+        for index, (source, target) in enumerate(zip(sources, loaded))
+    ]
+    for copy in copies:
+        copy.start()
+    copies[0].wait()
+    grad_stream[...] = stream_low[...].astype(jnp.float32)
+    for copy in copies[1:]:
+        copy.wait()
+    half = out_first.shape[1]
+    out_grad[:, :half] = out_first[...]
+    out_grad[:, half:] = out_second[...]
+    query_grad[...] = query_low[...]
+    width = key_grad.shape[1]
+    key_grad[...] = rest[:, :width]
+    value_grad[...] = rest[:, width : 2 * width]
+    for low, grad in ((gate_low, gate_grad), (up_low, up_grad), (down_low, down_grad)):
+        rows = low.shape[1]
+        grad[0, :rows, :] = low[0].astype(jnp.float32)
+        grad[0, rows:, :] = low[1].astype(jnp.float32)
+    experts, slab = router_grad.shape
+    turned = small[:slab, :].T
+    router_grad[...] = turned[:experts, :]
+    second_gain[...] = turned[experts, :]
+    first_gain[...] = turned[experts + 1, :]
+    total = grad_stream.shape[0] * grad_stream.shape[1]
+    rms[...] = jnp.sqrt(small[slab : slab + 1, :3] / total)
+    layer_copy.wait()
+
+
+def run_finish(layer, values, tokens, width, experts):
+    shape = jax.ShapeDtypeStruct
+    wide = jnp.float32
+    far = pl.BlockSpec(memory_space=pl.ANY)
+    near = pl.BlockSpec(memory_space=pltpu.VMEM)
+    slab, query_width = values[3].shape
+    key_width = (values[4].shape[1] - 128) // 2
+    tiles = [(1, 2 * value.shape[1], value.shape[2]) for value in values[5:8]]
+    return pl.pallas_call(
+        finish_kernel,
+        name="finish",
+        out_shape=(
+            shape(layer.shape, layer.dtype),
+            shape((tokens, width), wide),
+            shape((slab, query_width), wide),
+            shape((slab, query_width), wide),
+            shape((slab, key_width), wide),
+            shape((slab, key_width), wide),
+            *[shape(tile, wide) for tile in tiles],
+            shape((experts, slab), wide),
+            shape((slab,), wide),
+            shape((slab,), wide),
+            shape((1, 3), wide),
+        ),
+        in_specs=[far] * 10,
+        out_specs=(near,) * 13,
+        scratch_shapes=[pltpu.VMEM(value.shape, value.dtype) for value in values]
+        + [pltpu.SemaphoreType.DMA((10,))],
+        compiler_params=pltpu.CompilerParams(vmem_limit_bytes=63 << 20),
+    )(layer, *values)
 
 
 def dense_shards(
@@ -1683,8 +1855,6 @@
 ):
     tok_rows, model_width = stream.shape
     experts = router_weight.shape[1]
-    query_width = query_weight.shape[1]
-    key_width = key_matrix.shape[1]
     steps_up = np.arange(HEAD_FEATURES // 2, dtype=np.float32) * np.float32(2.0 / HEAD_FEATURES)
     turns = np.exp(-steps_up * np.log(np.float32(rope_base)))
     angles = np.arange(SEQ_LEN, dtype=np.float32)[:, None] * turns[None, :]
@@ -1692,45 +1862,49 @@
     operands = [
         stream,
         cotangent,
-        attention_gain.astype(jnp.float32)[None, :],
-        mixture_gain.astype(jnp.float32)[None, :],
+        attention_gain,
+        mixture_gain,
         query_weight,
         key_matrix,
         value_matrix,
         out_weight,
-        jnp.pad(router_weight, ((0, 0), (0, 128 - experts))),
-        routes,
+        router_weight.T,
+        routes.T,
         jnp.asarray(np.tile(cosines, (1, 4))),
         jnp.asarray(np.tile(np.concatenate([-sines, sines], axis=1), (1, 2))),
     ]
     front = run_front(operands, [gate_weight[0], up_weight[0], down_weight[0]])
+    layer_part, *partial = run_back(
+        front[: LINES + 8], operands[:9] + operands[10:], front[LINES + 8 :]
+    )
     (
         layer_out,
         grad_stream,
-        out_first,
-        out_second,
+        out_grad,
         query_grad,
-        rest_grad,
+        key_grad,
+        value_grad,
         gate_grad,
         up_grad,
         down_grad,
-        small,
-    ) = run_back(front[: LINES + 8], operands[:9] + operands[10:], front[LINES + 8 :])
-    slab = query_grad.shape[0]
-    rms_stats = jnp.sqrt(small[slab : slab + 1, :3] / (tok_rows * model_width))
+        router_grad,
+        second_gain,
+        first_gain,
+        rms_stats,
+    ) = run_finish(layer_part, partial, tok_rows, model_width, experts)
     return (
         layer_out,
-        grad_stream.astype(jnp.float32),
-        small[:slab, experts + 1],
+        grad_stream,
+        first_gain,
         query_grad,
-        rest_grad[:, :key_width],
-        rest_grad[:, key_width : 2 * key_width],
-        jnp.concatenate([out_first, out_second], axis=1).T,
-        small[:slab, experts],
-        small[:slab, :experts],
-        gate_grad.astype(jnp.float32).reshape(gate_weight.shape),
-        up_grad.astype(jnp.float32).reshape(up_weight.shape),
-        down_grad.astype(jnp.float32).reshape(down_weight.shape),
+        key_grad,
+        value_grad,
+        out_grad.T,
+        second_gain,
+        router_grad.T,
+        gate_grad,
+        up_grad,
+        down_grad,
         rms_stats,
     )
 

time: 360 us -> 326 us (0.906)
  Pallas kernels: 335 us -> 322 us
  local copies, waits for them, and re-layouts: 12.6 us -> 0 us
  other arithmetic: 8.39 us -> 0 us
    pallas_call x1, Pallas kernels: 223 us -> 190 us  [run_front(): pl.pallas_call(front_kernel, name='front', out_shape=(*[shape((half, widt...]
    pallas_call x1, Pallas kernels: 112 us -> 125 us  [run_back(): pl.pallas_call(back_kernel, name='back', out_shape=(shape((tokens, width)...]
    pallas_call x0 -> x1, Pallas kernels: none -> 7.16 us  [run_finish(): pl.pallas_call(finish_kernel, name='finish', out_shape=(shape(layer.shape...]
    unnamed x17 -> x0, local copies, waits for them, and re-layouts: 5.14 us -> none
    slice x3 -> x0, local copies, waits for them, and re-layouts: 4.02 us -> none  [the longest x1 1.63 us: dense_shards(): rest_grad[:, key_width:2 * key_width]]
where the time goes in v5:
time: 326 us; the launch traced here: 323 us
  Pallas kernels  322 us (99%)
    pallas_call x1, Pallas kernels, run_front(): pl.pallas_call(front_kernel, name='front', out_shape=(*[shape((half, widt...  190 us
    pallas_call x1, Pallas kernels, run_back(): pl.pallas_call(back_kernel, name='back', out_shape=(shape((tokens, width)...  125 us
    pallas_call x1, Pallas kernels, run_finish(): pl.pallas_call(finish_kernel, name='finish', out_shape=(shape(layer.shape...  7.16 us

profile of v5, /device:TPU:0, one launch (start us, length us, event | category | flops | bytes accessed | tf_op | source)
XLA Modules:
  0.0 323.2 jit_solution(15309801184045540389)
XLA Ops:
  0.6 190.5 %front.1 = (bf16[256,1536]{1,0:T(8,128)(2,1)}, bf16[256,1536]{1,0:T(8,128)(2,1)}, bf16[256,1536]{1,0:T(8,128)(2,1)}, bf16[256,1536]{1,0:T(8,128)(2,1)}, f32[256,...) custom-call(bf16[512,1536]{1,0:T(8,128)(2,1)} %refs_12_.1, ...), custom_call_target="tpu_custom_call" | custom-call | flops 57982058496 | bytes 37748736 | tf_op jit(solution)/shard_map/front/pallas_call | solution.py:1136
  191.1 124.7 %back.1 = (bf16[512,1536]{1,0:T(8,128)(2,1)}, bf16[512,1536]{1,0:T(8,128)(2,1)}, f32[96,384]{1,0:T(8,128)}, f32[96,384]{1,0:T(8,128)}, f32[96,768]{1,0:T(8,128)}...) custom-call(bf16[256,1536]{1,0:T(8,128)(2,1)} %get-tuple-element.56., ...), custom_call_target="tpu_custom_call" | custom-call | tf_op jit(solution)/shard_map/back/pallas_call | solution.py:1702
  315.8 7.2 %finish.1 = (bf16[512,1536]{1,0:T(8,128)(2,1)}, f32[512,1536]{1,0:T(8,128)}, f32[96,768]{1,0:T(8,128)}, f32[96,768]{1,0:T(8,128)}, f32[96,256]{1,0:T(8,128)}, /*...) custom-call(bf16[512,1536]{1,0:T(8,128)(2,1)} %get-tuple-element.76., ...), custom_call_target="tpu_custom_call" | custom-call | tf_op jit(solution)/shard_map/finish/pallas_call | solution.py:1817
